TPU v7x, 32 devices: a whole 2x2x4 slice. The times are simulated.
32 devices in a mesh: dp: 8 (over z, x), mp: 4 (over y, core).
Axes of the slice: x: 2, y: 2, z: 4, core: 2. Of those that a mesh axis runs over, the one named last changes fastest.
Arguments:
- latents: float32 [128, 4, 1024], P(('dp', 'mp')), may hold values from -6 to 6
- noises: float32 [128, 4, 1024], P(('dp', 'mp')), may hold values from -6 to 6
- timesteps: int32 [128], P('dp'), may hold values from 0 to 999, as said below
- labels: int32 [128], P('dp'), may hold values from 0 to 999
- dropped: int32 [128], P('dp'), may hold values 0 or 1
- buckets: int32 [8], P('dp'), may hold values from 0 to 19
- counts: int32 [8], P('dp'), may hold values from 1 to 16, as said below
- joined_weight: float32 [1152, 3456], P('dp', 'mp'), may hold values from -0.1875 to 0.1875
- joined_moment: float32 [1152, 3456], P('dp', 'mp'), may hold values from -1.1920929e-07 to 1.1920929e-07
- joined_second: float32 [1152, 3456], P('dp', 'mp'), may hold values from 1.5599667e-17 to 2.4959467e-16
- mixback_weight: float32 [1152, 1152], P('dp', 'mp'), may hold values from -0.375 to 0.375
- mixback_moment: float32 [1152, 1152], P('dp', 'mp'), may hold values from -1.1920929e-07 to 1.1920929e-07
- mixback_second: float32 [1152, 1152], P('dp', 'mp'), may hold values from 1.5599667e-17 to 2.4959467e-16
- expand_weight: float32 [1152, 4608], P('dp', 'mp'), may hold values from -0.1875 to 0.1875
- expand_moment: float32 [1152, 4608], P('dp', 'mp'), may hold values from -1.1920929e-07 to 1.1920929e-07
- expand_second: float32 [1152, 4608], P('dp', 'mp'), may hold values from 1.5599667e-17 to 2.4959467e-16
- narrow_weight: float32 [1152, 4608], P('dp', 'mp'), may hold values from -0.09375 to 0.09375
- narrow_moment: float32 [1152, 4608], P('dp', 'mp'), may hold values from -1.1920929e-07 to 1.1920929e-07
- narrow_second: float32 [1152, 4608], P('dp', 'mp'), may hold values from 1.5599667e-17 to 2.4959467e-16
- timeone_weight: float32 [256, 1152], P('dp', 'mp'), may hold values from -0.375 to 0.375
- timeone_moment: float32 [256, 1152], P('dp', 'mp'), may hold values from -1.1920929e-07 to 1.1920929e-07
- timeone_second: float32 [256, 1152], P('dp', 'mp'), may hold values from 1.5599667e-17 to 2.4959467e-16
- timetwo_weight: float32 [1152, 1152], P('dp', 'mp'), may hold values from -0.1875 to 0.1875
- timetwo_moment: float32 [1152, 1152], P('dp', 'mp'), may hold values from -1.1920929e-07 to 1.1920929e-07
- timetwo_second: float32 [1152, 1152], P('dp', 'mp'), may hold values from 1.5599667e-17 to 2.4959467e-16
- modulator_weight: float32 [1152, 11520], P('dp', 'mp'), may hold values from -0.1875 to 0.1875
- modulator_moment: float32 [1152, 11520], P('dp', 'mp'), may hold values from -1.1920929e-07 to 1.1920929e-07
- modulator_second: float32 [1152, 11520], P('dp', 'mp'), may hold values from 1.5599667e-17 to 2.4959467e-16
- classes_weight: float32 [1001, 1152], P(None, 'mp'), may hold values from -0.625 to 0.625
- classes_moment: float32 [1001, 1152], P(None, 'mp'), may hold values from -1.4901161e-08 to 1.4901161e-08
- classes_second: float32 [1001, 1152], P(None, 'mp'), may hold values from 2.437448e-19 to 3.8999167e-18
- smalls_weight: float32 [80512], replicated, may hold values from -0.3125 to 0.3125
- smalls_moment: float32 [80512], replicated, may hold values from -4.7683716e-07 to 4.7683716e-07
- smalls_second: float32 [80512], replicated, may hold values from 2.4959467e-16 to 3.9935147e-15
Outputs:
- loss_sum: float32 [], replicated
- token_count: float32 [], replicated
- grad_norm: float32 [], replicated
- joined_first: float32 [1152, 3456], P('dp', 'mp')
- joined_square: float32 [1152, 3456], P('dp', 'mp')
- joined_master: float32 [1152, 3456], P('dp', 'mp')
- mixback_first: float32 [1152, 1152], P('dp', 'mp')
- mixback_square: float32 [1152, 1152], P('dp', 'mp')
- mixback_master: float32 [1152, 1152], P('dp', 'mp')
- expand_first: float32 [1152, 4608], P('dp', 'mp')
- expand_square: float32 [1152, 4608], P('dp', 'mp')
- expand_master: float32 [1152, 4608], P('dp', 'mp')
- narrow_first: float32 [1152, 4608], P('dp', 'mp')
- narrow_square: float32 [1152, 4608], P('dp', 'mp')
- narrow_master: float32 [1152, 4608], P('dp', 'mp')
- timeone_first: float32 [256, 1152], P('dp', 'mp')
- timeone_square: float32 [256, 1152], P('dp', 'mp')
- timeone_master: float32 [256, 1152], P('dp', 'mp')
- timetwo_first: float32 [1152, 1152], P('dp', 'mp')
- timetwo_square: float32 [1152, 1152], P('dp', 'mp')
- timetwo_master: float32 [1152, 1152], P('dp', 'mp')
- modulator_first: float32 [1152, 11520], P('dp', 'mp')
- modulator_square: float32 [1152, 11520], P('dp', 'mp')
- modulator_master: float32 [1152, 11520], P('dp', 'mp')
- classes_first: float32 [1001, 1152], P(None, 'mp')
- classes_square: float32 [1001, 1152], P(None, 'mp')
- classes_master: float32 [1001, 1152], P(None, 'mp')
- smalls_first: float32 [80512], replicated
- smalls_square: float32 [80512], replicated
- smalls_master: float32 [80512], replicated
Inputs may be any that keep to these rules, and one draw needn't show every extreme that they name: `timesteps`: each image's timestep lies in its group's bucket: from (50) times the bucket to that plus 1000 // 20 - 1. `counts`: the true images of a group are its last slots; some group is full.
All inputs are finite; a program needn't handle non-finite values. No bound on the sum of `dropped` on one device may be relied on, other than what follows from the above.
Results may differ from a plain program's by a relative error of at most 0.007.
Values may be sent and summed in bfloat16 or wider, within the bound.
No kernel may reach another device: no remote copies, remote signals or barrier semaphores. Data moves between devices by JAX's collectives and lax.ppermute only.
A program may use at most 320 MiB of HBM per device.

v0:
```python
from functools import partial
import math

import jax
import jax.numpy as jnp
from jax import lax
from jax.experimental import pallas as pl
from jax.experimental.pallas import tpu as pltpu
from jax.sharding import Mesh
from jax.sharding import PartitionSpec as P

D = 1152
H = 16
HD = 72
FF = 4608
FREQ = 256
NCLS = 1000
GRID = 16
NB = 20
STEP = 10
TOKS = 256
REL = 62


norm_eps = 1e-06
beta_one = 0.9
beta_two = 0.999
learn_rate = 0.04
weight_decay = 0.01
adam_eps = 1e-12
clip_level = 0.001
highest = lax.Precision.HIGHEST


def layout():
    entries = [
        ("embed_bias", D),
        ("time_bias_one", D),
        ("time_bias_two", D),
        ("cond_bias", 10 * D),
        ("query_bias", D),
        ("value_bias", D),
        ("out_bias", D),
        ("fc1_bias", FF),
        ("fc2_bias", D),
        ("final_bias", 32),
        ("embed_weight", 16 * D),
        ("final_weight", 32 * D),
        ("rel_bias", H * REL),
    ]
    places = {}
    offset = 0
    for entry_name, length in entries:
        places[entry_name] = (offset, length)
        offset = offset + length
    return places


def patchify(field):
    images, channels = (field.shape[0], field.shape[1])
    shaped = field.reshape(images, channels, GRID, 2, GRID, 2)
    return shaped.transpose(0, 2, 4, 1, 3, 5).reshape(images, GRID * GRID, channels * 4)


def frequencies(moments_in):
    half_freq = FREQ // 2
    omegas = jnp.exp(-math.log(10000.0) * jnp.arange(half_freq, dtype=jnp.float32) / half_freq)
    angles = moments_in[:, None] * omegas[None, :]
    return jnp.concatenate([jnp.cos(angles), jnp.sin(angles)], 1)


def position_table():
    quarter = D // 4
    omegas = 1.0 / 10000.0 ** (jnp.arange(quarter, dtype=jnp.float32) / quarter)
    coords = jnp.arange(GRID, dtype=jnp.float32)
    row_angle = jnp.repeat(coords, GRID)[:, None] * omegas[None, :]
    col_angle = jnp.tile(coords, GRID)[:, None] * omegas[None, :]
    return jnp.concatenate(
        [jnp.sin(row_angle), jnp.cos(row_angle), jnp.sin(col_angle), jnp.cos(col_angle)], 1
    )


def offset_table():
    coords = jnp.arange(GRID)
    shifts = coords[:, None] - coords[None, :] + GRID - 1
    return (
        (shifts[None, :, :] == jnp.arange(2 * GRID - 1)[:, None, None])
        .astype(jnp.float32)
        .reshape(2 * GRID - 1, GRID * GRID)
    )


def layernorm_parts(values):
    center = values - jnp.mean(values, -1, keepdims=True)
    inverse = lax.rsqrt(jnp.mean(center * center, -1, keepdims=True) + norm_eps)
    return (center * inverse, inverse)


def layernorm_back(normed, inverse, gradient):
    return (
        gradient
        - jnp.mean(gradient, -1, keepdims=True)
        - normed * jnp.mean(gradient * normed, -1, keepdims=True)
    ) * inverse


def column_of(modulation, index_col):
    return modulation[:, None, index_col * D : (index_col + 1) * D]


SCALE = 1.0 / math.sqrt(HD)
JOIN = 3 * HD


def dot_nn(left, right):
    return jnp.dot(left, right, preferred_element_type=jnp.float32)


def dot_nt(left, right):
    return lax.dot_general(
        left, right, (((1,), (1,)), ((), ())), preferred_element_type=jnp.float32
    )


def dot_tn(left, right):
    return lax.dot_general(
        left, right, (((0,), (0,)), ((), ())), preferred_element_type=jnp.float32
    )


def attention_forward_kernel(joined_ref, table_ref, spots_ref, mixed_ref, total_ref):
    for head in range(H):
        base = head * JOIN
        query = joined_ref[0, :, base : base + HD]
        keys = joined_ref[0, :, base + HD : base + 2 * HD]
        values = joined_ref[0, :, base + 2 * HD : base + 3 * HD]
        scores = (dot_nt(keys, query) + dot_nt(spots_ref[...], table_ref[head])) * SCALE
        largest = jnp.max(scores, 0, keepdims=True)
        grown = jnp.exp(scores - largest)
        total = jnp.sum(grown, 0, keepdims=True)
        prob = (grown * (1.0 / total)).astype(jnp.bfloat16)
        mixed_ref[0, :, head * HD : (head + 1) * HD] = dot_tn(prob, values).astype(jnp.bfloat16)
        total_ref[0, head : head + 1, :] = largest + jnp.log(total)


def attention_forward(joined_rows, table, spots):
    images = joined_rows.shape[0]
    return pl.pallas_call(
        attention_forward_kernel,
        grid=(images,),
        in_specs=[
            pl.BlockSpec((1, TOKS, H * JOIN), lambda i: (i, 0, 0)),
            pl.BlockSpec(table.shape, lambda i: (0, 0, 0)),
            pl.BlockSpec(spots.shape, lambda i: (0, 0)),
        ],
        out_specs=[
            pl.BlockSpec((1, TOKS, D), lambda i: (i, 0, 0)),
            pl.BlockSpec((1, H, TOKS), lambda i: (i, 0, 0)),
        ],
        out_shape=[
            jax.ShapeDtypeStruct((images, TOKS, D), jnp.bfloat16),
            jax.ShapeDtypeStruct((images, H, TOKS), jnp.float32),
        ],
        cost_estimate=pl.CostEstimate(
            flops=images * H * 4 * TOKS * TOKS * 128,
            transcendentals=images * H * TOKS * TOKS,
            bytes_accessed=images * TOKS * D * 8,
        ),
        compiler_params=pltpu.CompilerParams(vmem_limit_bytes=48 * 1024 * 1024),
        name="attention_forward",
    )(joined_rows, table, spots)


def attention_backward_kernel(
    joined_ref, total_ref, mixed_grad_ref, table_ref, spots_ref, grad_ref, column_ref, shift_ref
):
    @pl.when(pl.program_id(0) == 0)
    def start():
        shift_ref[...] = jnp.zeros_like(shift_ref)

    for head in range(H):
        base = head * JOIN
        query = joined_ref[0, :, base : base + HD]
        keys = joined_ref[0, :, base + HD : base + 2 * HD]
        values = joined_ref[0, :, base + 2 * HD : base + 3 * HD]
        mixed_grad = mixed_grad_ref[0, :, head * HD : (head + 1) * HD]
        scores = (dot_nt(keys, query) + dot_nt(spots_ref[...], table_ref[head])) * SCALE
        exact = jnp.exp(scores - total_ref[0, head : head + 1, :])
        value_grad = dot_nn(exact.astype(jnp.bfloat16), mixed_grad)
        prob_grad = dot_nt(values, mixed_grad)
        shared = jnp.sum(exact * prob_grad, 0, keepdims=True)
        score_grad = (exact * (prob_grad - shared)).astype(jnp.bfloat16)
        key_grad = dot_nn(score_grad, query) * SCALE
        wide = jnp.concatenate([keys, spots_ref[:, : 2 * GRID]], 1)
        query_wide = dot_tn(score_grad, wide)
        shift_ref[head] += query_wide
        grad_ref[0, :, base : base + HD] = (query_wide[:, :HD] * SCALE).astype(jnp.bfloat16)
        grad_ref[0, :, base + HD : base + 2 * HD] = key_grad.astype(jnp.bfloat16)
        grad_ref[0, :, base + 2 * HD : base + 3 * HD] = value_grad.astype(jnp.bfloat16)
    column_ref[0] = dot_nn(jnp.ones((8, TOKS), jnp.bfloat16), grad_ref[0])


def attention_backward(joined_rows, total, mixed_grad, table, spots):
    images = joined_rows.shape[0]
    wide = HD + 2 * GRID
    return pl.pallas_call(
        attention_backward_kernel,
        grid=(images,),
        in_specs=[
            pl.BlockSpec((1, TOKS, H * JOIN), lambda i: (i, 0, 0)),
            pl.BlockSpec((1, H, TOKS), lambda i: (i, 0, 0)),
            pl.BlockSpec((1, TOKS, D), lambda i: (i, 0, 0)),
            pl.BlockSpec(table.shape, lambda i: (0, 0, 0)),
            pl.BlockSpec(spots.shape, lambda i: (0, 0)),
        ],
        out_specs=[
            pl.BlockSpec((1, TOKS, H * JOIN), lambda i: (i, 0, 0)),
            pl.BlockSpec((1, 8, H * JOIN), lambda i: (i, 0, 0)),
            pl.BlockSpec((H, TOKS, wide), lambda i: (0, 0, 0)),
        ],
        out_shape=[
            jax.ShapeDtypeStruct((images, TOKS, H * JOIN), jnp.bfloat16),
            jax.ShapeDtypeStruct((images, 8, H * JOIN), jnp.float32),
            jax.ShapeDtypeStruct((H, TOKS, wide), jnp.float32),
        ],
        cost_estimate=pl.CostEstimate(
            flops=images * H * 10 * TOKS * TOKS * 128,
            transcendentals=images * H * TOKS * TOKS,
            bytes_accessed=images * TOKS * D * 16,
        ),
        compiler_params=pltpu.CompilerParams(vmem_limit_bytes=48 * 1024 * 1024),
        name="attention_backward",
    )(joined_rows, total, mixed_grad, table, spots)


def relative_tables(rel_table):
    rows = offset_table()
    span = 2 * GRID - 1
    along_rows = jnp.dot(rel_table[:, :span], rows, precision=highest).reshape(H, GRID, 1, GRID)
    along_cols = jnp.dot(rel_table[:, span:], rows, precision=highest).reshape(H, 1, GRID, GRID)
    full = (H, GRID, GRID, GRID)
    table = jnp.concatenate(
        [jnp.broadcast_to(along_rows, full), jnp.broadcast_to(along_cols, full)], 3
    ).reshape(H, TOKS, 2 * GRID) * math.sqrt(HD)
    upper = table.astype(jnp.bfloat16)
    lower = (table - upper.astype(jnp.float32)).astype(jnp.bfloat16)
    return jnp.concatenate([upper, lower], 2)


def spot_table():
    places = jnp.arange(TOKS)
    rows = (places[:, None] // GRID == jnp.arange(GRID)[None, :]).astype(jnp.bfloat16)
    cols = (places[:, None] % GRID == jnp.arange(GRID)[None, :]).astype(jnp.bfloat16)
    return jnp.concatenate([rows, cols, rows, cols], 1)


def relative_gradient(shifts):
    rows = offset_table()
    row_part = jnp.sum(shifts[:, :, :GRID].reshape(H, GRID, GRID, GRID), 2)
    col_part = jnp.sum(shifts[:, :, GRID:].reshape(H, GRID, GRID, GRID), 1)
    return jnp.concatenate(
        [
            jnp.dot(row_part.reshape(H, TOKS), rows.T, precision=highest),
            jnp.dot(col_part.reshape(H, TOKS), rows.T, precision=highest),
        ],
        1,
    ).reshape(H * REL)


def small_gather(values, axes, count):
    spread = jnp.broadcast_to(values[None], (count,) + values.shape)
    return lax.all_to_all(spread, axes, 0, 0, tiled=True)


def pick(values, index, dim):
    return lax.dynamic_index_in_dim(values, index, dim, keepdims=False)


def reduce_step(values, dim, axis, size, index):
    if size == 2:
        received = lax.ppermute(pick(values, 1 - index, dim), axis, [(0, 1), (1, 0)])
        return pick(values, index, dim).astype(jnp.float32) + received.astype(jnp.float32)
    moved = jnp.moveaxis(values, dim, 0)
    received = lax.all_to_all(moved, axis, 0, 0, tiled=True)
    return jnp.sum(received.astype(jnp.float32), 0)


def reduce_weight(gradient, sizes, places):
    da, db, ny = (sizes[key] for key in ("da", "db", "y"))
    rows = gradient.shape[0] // (da * db)
    width = gradient.shape[1] // (ny * 2)
    blocks = gradient.reshape(da, db, rows, ny, 2, width)
    kept = reduce_step(blocks, 4, "c", 2, places["c"]).astype(jnp.bfloat16)
    half = da // 2
    first = reduce_step(kept[:half], 3, "y", ny, places["y"]).astype(jnp.bfloat16)
    second = reduce_step(kept[half:], 1, "db", db, places["db"]).astype(jnp.bfloat16)
    first = reduce_step(first, 1, "db", db, places["db"]).astype(jnp.bfloat16)
    second = reduce_step(second, 2, "y", ny, places["y"]).astype(jnp.bfloat16)
    received = lax.all_to_all(jnp.concatenate([first, second], 0), "da", 0, 0, tiled=True)
    return jnp.sum(received.astype(jnp.float32), 0)


def whole_weight(gathered, groups, parts, begin, width):
    block = gathered.reshape(groups, parts, gathered.shape[1], gathered.shape[2])
    block = block[:, :, :, begin : begin + width].transpose(0, 2, 1, 3)
    return block.reshape(groups * gathered.shape[1], parts * width)


def adamw_update(master, moment, second, gradient):
    first_new = beta_one * moment + (1.0 - beta_one) * gradient
    square_new = beta_two * second + (1.0 - beta_two) * gradient * gradient
    first_hat = first_new / (1.0 - beta_one**STEP)
    square_hat = square_new / (1.0 - beta_two**STEP)
    master_new = master - learn_rate * (
        first_hat / (jnp.sqrt(square_hat) + adam_eps) + weight_decay * master
    )
    return (first_new, square_new, master_new)


TOKEN_SMALLS = (
    "embed_bias",
    "query_bias",
    "value_bias",
    "out_bias",
    "fc1_bias",
    "fc2_bias",
    "final_bias",
    "embed_weight",
    "final_weight",
    "rel_bias",
)


def per_device(
    sizes,
    latents,
    noises,
    timesteps,
    labels,
    dropped,
    buckets,
    counts,
    *state,
):
    masters, moments, seconds = (state[0::3], state[1::3], state[2::3])
    (
        joined_weight,
        mixback_weight,
        expand_weight,
        narrow_weight,
        timeone_weight,
        timetwo_weight,
        modulator_weight,
        classes_weight,
        smalls_weight,
    ) = masters
    da, db, ny, nc = (sizes[key] for key in ("da", "db", "y", "c"))
    dp, mp = (da * db, ny * nc)
    dp_axes, mp_axes = (("da", "db"), ("y", "c"))
    all_axes = dp_axes + mp_axes
    places_now = {key: lax.axis_index(key) for key in ("da", "db", "y", "c")}
    dp_index = places_now["da"] * db + places_now["db"]
    mp_index = places_now["y"] * nc + places_now["c"]
    places = layout()
    zero_index = jnp.zeros((), jnp.int32)

    def small_piece(key_name):
        begin_at, length = places[key_name]
        return smalls_weight[begin_at : begin_at + length]

    own_images = latents.shape[0]
    group_size = timesteps.shape[0]
    images_all = dp * group_size
    row_width = timetwo_weight.shape[0]
    width_mp = timetwo_weight.shape[1]
    mod_width = modulator_weight.shape[1]

    gathered_one = lax.all_gather(
        jnp.concatenate([joined_weight, mixback_weight], 1).astype(jnp.bfloat16), all_axes
    )
    gathered_two = lax.all_gather(
        jnp.concatenate([expand_weight, narrow_weight], 1).astype(jnp.bfloat16), all_axes
    )
    joined = whole_weight(gathered_one, dp, mp, 0, joined_weight.shape[1])
    mixback = whole_weight(gathered_one, dp, mp, joined_weight.shape[1], mixback_weight.shape[1])
    expand = whole_weight(gathered_two, dp, mp, 0, expand_weight.shape[1])
    narrow = whole_weight(gathered_two, dp, mp, expand_weight.shape[1], narrow_weight.shape[1])

    facts = small_gather(
        jnp.concatenate([timesteps, labels, dropped, buckets, counts]).astype(jnp.float32),
        dp_axes,
        dp,
    )
    times_all = facts[:, :group_size].reshape(images_all)
    labels_all = facts[:, group_size : 2 * group_size].reshape(images_all)
    dropped_all = facts[:, 2 * group_size : 3 * group_size].reshape(images_all)
    buckets_all = facts[:, 3 * group_size]
    token_count = jnp.sum(facts[:, 3 * group_size + 1]) * TOKS
    time_first = small_gather(timeone_weight.astype(jnp.bfloat16), dp_axes, dp).reshape(
        FREQ, width_mp
    )
    time_second_all = small_gather(timetwo_weight.astype(jnp.bfloat16), dp_axes, dp).reshape(
        D, width_mp
    )
    bucket_width = float(1000 // NB)
    rows_in = frequencies(
        jnp.concatenate([times_all, buckets_all * bucket_width + 0.5 * bucket_width])
    ).astype(jnp.bfloat16)
    hidden_time = jnp.dot(
        rows_in, time_first, preferred_element_type=jnp.float32
    ) + lax.dynamic_slice_in_dim(small_piece("time_bias_one"), mp_index * width_mp, width_mp)
    hidden_act = jax.nn.silu(hidden_time).astype(jnp.bfloat16)
    embed_part = dot_nt(hidden_act, timetwo_weight.astype(jnp.bfloat16))
    class_index = jnp.where(dropped_all > 0, float(NCLS), labels_all)
    onehot = (class_index[:, None] == jnp.arange(NCLS + 1, dtype=jnp.float32)[None, :]).astype(
        jnp.bfloat16
    )
    label_cols = jnp.dot(
        onehot, classes_weight.astype(jnp.bfloat16), preferred_element_type=jnp.float32
    )
    column_at = dp_index * row_width
    owner = column_at // width_mp
    label_part = lax.dynamic_slice_in_dim(label_cols, column_at - owner * width_mp, row_width, 1)
    label_part = jnp.where(mp_index == owner, label_part, 0.0)
    condition = jnp.sum(
        small_gather(
            jnp.concatenate([embed_part[:images_all] + label_part, embed_part[images_all:]], 0),
            mp_axes,
            mp,
        ),
        0,
    ) + lax.dynamic_slice_in_dim(small_piece("time_bias_two"), column_at, row_width)
    cond_act = jax.nn.silu(condition).astype(jnp.bfloat16)
    modulator = modulator_weight.astype(jnp.bfloat16)
    global_cols = mp_index * mod_width + jnp.arange(mod_width)
    mods_part = jnp.dot(cond_act, modulator, preferred_element_type=jnp.float32)
    outgoing = jnp.where(
        global_cols < 8 * D,
        mods_part[:images_all].reshape(dp, group_size, mod_width),
        mods_part[images_all:].reshape(dp, 1, mod_width),
    ).astype(jnp.bfloat16)
    incoming = lax.all_to_all(
        outgoing.reshape(dp * mp, own_images, mod_width), all_axes, 0, 0, tiled=True
    ).reshape(dp, mp, own_images, mod_width)
    modulation = jnp.sum(incoming.astype(jnp.float32), 0).transpose(1, 0, 2).reshape(
        own_images, 10 * D
    ) + small_piece("cond_bias")

    own_times = lax.dynamic_slice_in_dim(timesteps, mp_index * own_images, own_images)
    slot_index = mp_index * own_images + jnp.arange(own_images)
    valid_flags = (slot_index >= group_size - counts[0]).astype(jnp.float32)
    time_frac = (own_times.astype(jnp.float32) + 1.0) / 1000.0
    alpha_scale = jnp.cos(0.5 * math.pi * time_frac)[:, None, None]
    sigma_scale = jnp.sin(0.5 * math.pi * time_frac)[:, None, None]
    noisy_all = patchify(alpha_scale * latents + sigma_scale * noises)
    target = patchify(jnp.concatenate([alpha_scale * noises - sigma_scale * latents, noises], 1))
    embed_weight = small_piece("embed_weight").reshape(16, D)
    final_weight = small_piece("final_weight").reshape(D, 32)
    table = relative_tables(small_piece("rel_bias").reshape(H, REL))
    spots = spot_table()
    images = own_images
    rows_all = images * TOKS

    embed_in = noisy_all.astype(jnp.bfloat16)
    stream_zero = (
        jnp.einsum(
            "ntc,cd->ntd",
            embed_in,
            embed_weight.astype(jnp.bfloat16),
            preferred_element_type=jnp.float32,
        )
        + small_piece("embed_bias")
        + position_table()
    )
    normed_a, inverse_a = layernorm_parts(stream_zero)
    first_in = (
        (normed_a * (1.0 + column_of(modulation, 1)) + column_of(modulation, 0))
        .astype(jnp.bfloat16)
        .reshape(rows_all, D)
    )
    added = jnp.stack(
        [
            (small_piece("query_bias") + modulation[:, 8 * D : 9 * D]).reshape(images, H, HD),
            jnp.zeros((images, H, HD), jnp.float32),
            (small_piece("value_bias") + modulation[:, 9 * D :]).reshape(images, H, HD),
        ],
        2,
    ).reshape(images, 1, 3 * D)
    joined_rows = (
        dot_nn(first_in, joined).reshape(images, TOKS, 3 * D) + added
    ).astype(jnp.bfloat16)
    mixed_heads, log_total = attention_forward(joined_rows, table, spots)
    mixed_heads = mixed_heads.reshape(rows_all, D)
    branch = (dot_nt(mixed_heads, mixback) + small_piece("out_bias")).reshape(images, TOKS, D)
    stream_one = stream_zero + column_of(modulation, 2) * branch
    normed_b, inverse_b = layernorm_parts(stream_one)
    second_in = (
        (normed_b * (1.0 + column_of(modulation, 4)) + column_of(modulation, 3))
        .astype(jnp.bfloat16)
        .reshape(rows_all, D)
    )
    hidden = dot_nn(second_in, expand) + small_piece("fc1_bias")
    active = jax.nn.gelu(hidden, approximate=True).astype(jnp.bfloat16)
    branch_two = (dot_nt(active, narrow) + small_piece("fc2_bias")).reshape(images, TOKS, D)
    stream_two = stream_one + column_of(modulation, 5) * branch_two
    normed_c, inverse_c = layernorm_parts(stream_two)
    final_in = (
        (normed_c * (1.0 + column_of(modulation, 7)) + column_of(modulation, 6))
        .astype(jnp.bfloat16)
        .reshape(rows_all, D)
    )
    output = dot_nn(final_in, final_weight.astype(jnp.bfloat16)) + small_piece("final_bias")

    residual_error = output - target.reshape(rows_all, 32)
    valid_rows = jnp.repeat(valid_flags, TOKS)[:, None]
    loss_part = jnp.sum(valid_rows * jnp.mean(residual_error * residual_error, -1, keepdims=True))
    grad_out = (valid_rows * 2.0 * residual_error / 32.0).astype(jnp.bfloat16)
    grad_small = {}
    grad_small["final_bias"] = jnp.sum(grad_out.astype(jnp.float32), 0)
    grad_small["final_weight"] = dot_tn(final_in, grad_out).reshape(32 * D)
    grad_final = dot_nt(grad_out, final_weight.astype(jnp.bfloat16)).reshape(images, TOKS, D)

    def modulate_back(gradient, normed, inverse, scale_col):
        scaled = gradient * (1.0 + column_of(modulation, scale_col))
        return (
            layernorm_back(normed, inverse, scaled),
            jnp.sum(gradient, 1),
            jnp.sum(gradient * normed, 1),
        )

    grad_two, shift_c, scale_c = modulate_back(grad_final, normed_c, inverse_c, 7)
    grad_branch_two = (
        (column_of(modulation, 5) * grad_two).astype(jnp.bfloat16).reshape(rows_all, D)
    )
    gate_two = jnp.sum(grad_two * branch_two, 1)
    grad_small["fc2_bias"] = jnp.sum(grad_branch_two.astype(jnp.float32), 0)
    narrow_grad = reduce_weight(
        dot_tn(grad_branch_two, active).astype(jnp.bfloat16), sizes, places_now
    )
    grad_active = dot_nn(grad_branch_two, narrow)
    _, pullback = jax.vjp(partial(jax.nn.gelu, approximate=True), hidden)
    grad_hidden = pullback(grad_active)[0].astype(jnp.bfloat16)
    grad_small["fc1_bias"] = jnp.sum(grad_hidden.astype(jnp.float32), 0)
    expand_grad = reduce_weight(
        dot_tn(second_in, grad_hidden).astype(jnp.bfloat16), sizes, places_now
    )
    grad_second = dot_nt(grad_hidden, expand).reshape(images, TOKS, D)
    grad_one_part, shift_b, scale_b = modulate_back(grad_second, normed_b, inverse_b, 4)
    grad_one = grad_two + grad_one_part
    grad_branch = (column_of(modulation, 2) * grad_one).astype(jnp.bfloat16).reshape(rows_all, D)
    gate_one = jnp.sum(grad_one * branch, 1)
    grad_small["out_bias"] = jnp.sum(grad_branch.astype(jnp.float32), 0)
    mixback_grad = reduce_weight(
        dot_tn(grad_branch, mixed_heads).astype(jnp.bfloat16), sizes, places_now
    )
    grad_mixed = dot_nn(grad_branch, mixback).astype(jnp.bfloat16).reshape(images, TOKS, D)
    grad_joined, column_sums, shifts = attention_backward(
        joined_rows, log_total, grad_mixed, table, spots
    )
    grad_joined = grad_joined.reshape(rows_all, 3 * D)
    grad_small["rel_bias"] = relative_gradient(shifts[:, :, HD:])
    sums = column_sums[:, 0].reshape(images, H, 3, HD)
    time_query = sums[:, :, 0].reshape(images, D)
    time_value = sums[:, :, 2].reshape(images, D)
    grad_small["query_bias"] = jnp.sum(time_query, 0)
    grad_small["value_bias"] = jnp.sum(time_value, 0)
    grad_first = dot_nt(grad_joined, joined).reshape(images, TOKS, D)
    joined_grad = reduce_weight(
        dot_tn(first_in, grad_joined).astype(jnp.bfloat16), sizes, places_now
    )
    grad_zero_part, shift_a, scale_a = modulate_back(grad_first, normed_a, inverse_a, 1)
    grad_zero = grad_one + grad_zero_part
    grad_small["embed_bias"] = jnp.sum(grad_zero, (0, 1))
    grad_small["embed_weight"] = jnp.einsum(
        "ntc,ntd->cd", embed_in.astype(jnp.float32), grad_zero, precision=highest
    ).reshape(16 * D)

    mods_grads = jnp.concatenate(
        [
            shift_a,
            scale_a,
            gate_one,
            shift_b,
            scale_b,
            gate_two,
            shift_c,
            scale_c,
            time_query,
            time_value,
        ],
        1,
    ).astype(jnp.bfloat16)
    to_owners = mods_grads.reshape(own_images, mp, mod_width).transpose(1, 0, 2)
    returned = lax.all_to_all(
        jnp.broadcast_to(to_owners[None], (dp,) + to_owners.shape).reshape(
            dp * mp, own_images, mod_width
        ),
        all_axes,
        0,
        0,
        tiled=True,
    ).reshape(images_all, mod_width)
    is_image = (global_cols < 8 * D)[None, :]
    returned_wide = returned.astype(jnp.float32)
    cond_bias_grad = jnp.sum(returned_wide, 0)
    bucket_sums = jnp.where(
        is_image, 0.0, jnp.sum(returned_wide.reshape(dp, group_size, mod_width), 1)
    )

    def split_rows(image_rows, bucket_rows):
        upper = bucket_rows.astype(jnp.bfloat16)
        lower = (bucket_rows - upper.astype(jnp.float32)).astype(jnp.bfloat16)
        return jnp.concatenate([image_rows.astype(jnp.bfloat16), upper, lower], 0)

    def double_rows(rows):
        return jnp.concatenate([rows, rows[images_all:]], 0)

    grad_mod = split_rows(jnp.where(is_image, returned, jnp.zeros_like(returned)), bucket_sums)
    modulator_grad = dot_tn(double_rows(cond_act), grad_mod)
    cond_part = dot_nt(grad_mod, modulator)
    cond_part = jnp.concatenate(
        [cond_part[:images_all], cond_part[images_all : images_all + dp] + cond_part[images_all + dp :]],
        0,
    )
    grad_act = jnp.sum(small_gather(cond_part, mp_axes, mp), 0)
    _, pullback = jax.vjp(jax.nn.silu, condition)
    grad_cond_own = pullback(grad_act)[0]
    grad_embed_own = split_rows(grad_cond_own[:images_all], grad_cond_own[images_all:])
    timetwo_grad = dot_tn(grad_embed_own, double_rows(hidden_act))
    grad_cond = (
        small_gather(grad_cond_own, dp_axes, dp)
        .transpose(1, 0, 2)
        .reshape(images_all + dp, D)
    )
    grad_embed = split_rows(grad_cond[:images_all], grad_cond[images_all:])
    bias_two_grad = jnp.sum(grad_embed.astype(jnp.float32), 0)
    grad_hidden_act = dot_nn(grad_embed, time_second_all)
    grad_hidden_act = jnp.concatenate(
        [
            grad_hidden_act[:images_all],
            grad_hidden_act[images_all : images_all + dp] + grad_hidden_act[images_all + dp :],
        ],
        0,
    )
    _, pullback = jax.vjp(jax.nn.silu, hidden_time)
    grad_hidden_time = pullback(grad_hidden_act)[0]
    grad_hidden_time = split_rows(grad_hidden_time[:images_all], grad_hidden_time[images_all:])
    bias_one_grad = jnp.sum(grad_hidden_time.astype(jnp.float32), 0)
    rows_own = lax.dynamic_slice_in_dim(
        rows_in, dp_index * timeone_weight.shape[0], timeone_weight.shape[0], 1
    )
    timeone_grad = dot_tn(double_rows(rows_own), grad_hidden_time)
    label_rows = lax.dynamic_slice_in_dim(grad_cond[:images_all], mp_index * width_mp, width_mp, 1)
    label_upper = label_rows.astype(jnp.bfloat16)
    label_lower = (label_rows - label_upper.astype(jnp.float32)).astype(jnp.bfloat16)
    class_raw = dot_tn(
        jnp.concatenate([onehot, onehot], 0), jnp.concatenate([label_upper, label_lower], 0)
    )

    vector = jnp.concatenate([grad_small[key_name] for key_name in TOKEN_SMALLS])
    slice_length = -(-vector.shape[0] // (dp * mp))
    padded = jnp.pad(vector, (0, slice_length * dp * mp - vector.shape[0]))
    slice_sum = jnp.sum(
        lax.all_to_all(padded.reshape(dp * mp, slice_length), all_axes, 0, 0, tiled=True), 0
    )
    mod_slice = -(-mod_width // dp)
    one_slice = -(-width_mp // dp)
    own_cond = lax.dynamic_slice_in_dim(
        jnp.pad(cond_bias_grad, (0, mod_slice * dp - mod_width)), dp_index * mod_slice, mod_slice
    )
    own_one = lax.dynamic_slice_in_dim(
        jnp.pad(bias_one_grad, (0, one_slice * dp - width_mp)), dp_index * one_slice, one_slice
    )
    own_two = lax.dynamic_slice_in_dim(bias_two_grad, column_at, row_width)

    owned = [
        member / token_count
        for member in (
            joined_grad,
            mixback_grad,
            expand_grad,
            narrow_grad,
            timeone_grad,
            timetwo_grad,
            modulator_grad,
        )
    ]
    class_grad = class_raw / token_count
    own_slices = jnp.concatenate([slice_sum, own_cond, own_one]) / token_count
    squares = sum((jnp.sum(member * member) for member in owned)) + jnp.sum(own_slices * own_slices)
    squares = squares + jnp.where(dp_index == 0, jnp.sum(class_grad * class_grad), 0.0)
    own_two = own_two / token_count
    squares = squares + jnp.where(mp_index == 0, jnp.sum(own_two * own_two), 0.0)
    final = small_gather(
        jnp.concatenate([own_slices, squares[None], loss_part[None]]), all_axes, dp * mp
    )
    ends = slice_length + mod_slice + one_slice
    grad_norm = jnp.sqrt(jnp.sum(final[:, ends]))
    loss_sum = jnp.sum(final[:, ends + 1])
    factor = jnp.minimum(1.0, clip_level / grad_norm)
    token_smalls = final[:, :slice_length].reshape(dp * mp * slice_length)
    pieces = {"time_bias_two": bias_two_grad / token_count}
    pieces["cond_bias"] = (
        final[:, slice_length : slice_length + mod_slice]
        .reshape(dp, mp, mod_slice)
        .transpose(1, 0, 2)
        .reshape(mp, dp * mod_slice)[:, :mod_width]
        .reshape(10 * D)
    )
    pieces["time_bias_one"] = (
        final[:, slice_length + mod_slice : ends]
        .reshape(dp, mp, one_slice)
        .transpose(1, 0, 2)
        .reshape(mp, dp * one_slice)[:, :width_mp]
        .reshape(D)
    )
    offset = 0
    for key_name in TOKEN_SMALLS:
        length = places[key_name][1]
        pieces[key_name] = token_smalls[offset : offset + length]
        offset = offset + length
    small_grad = jnp.concatenate([pieces[key_name] for key_name in places])
    gradients = owned + [class_grad, small_grad]
    results = [loss_sum, token_count, grad_norm]
    for master, moment, second, gradient in zip(masters, moments, seconds, gradients):
        results.extend(adamw_update(master, moment, second, gradient * factor))
    return tuple(results)


def solution(mesh):
    dp, mp = (mesh.shape["dp"], mesh.shape["mp"])
    sizes = {"da": dp // 2, "db": 2, "y": mp // 2, "c": 2}
    inner = Mesh(
        mesh.devices.reshape(sizes["da"], sizes["db"], sizes["y"], sizes["c"]),
        ("da", "db", "y", "c"),
    )
    groups, parts = (("da", "db"), ("y", "c"))
    weight_specs = (P(groups, parts),) * 21 + (P(None, parts),) * 3 + (P(),) * 3
    in_specs = (P(groups + parts, None, None),) * 2 + (P(groups),) * 5 + weight_specs
    out_specs = (P(),) * 3 + weight_specs
    return jax.shard_map(
        partial(per_device, sizes),
        mesh=inner,
        in_specs=in_specs,
        out_specs=out_specs,
        check_vma=False,
    )
```

profile of v0, /device:TPU:0, one launch (start us, length us, event | category | flops | bytes accessed | tf_op | source)
XLA Modules:
  0.0 1051.4 jit_solution(15694357364449010491)
XLA Ops:
  14.6 7.3 all-to-all-start
  55.0 9.1 all-to-all-done.1
  71.9 13.3 %all-to-all-done.2 = f32[4,136,144]{2,1,0:T(8,128)S(1)} async-done(((f32[4,136,144]{2,1,0:T(8,128)}), f32[4,136,144]{2,1,0:T(8,128)S(1)}, u32[]{:S(2)}, u32[]{:S(2)}) %all-to-all-start.2) | async-done | bytes 313376 | tf_op jit(solution)/shard_map/all_to_all | solution.py:272
  103.2 20.6 %all-to-all-done.3 = bf16[32,4,2880]{2,1,0:T(4,128)(2,1)S(1)} async-done(((bf16[32,4,2880]{2,1,0:T(4,128)(2,1)}), bf16[32,4,2880]{2,1,0:T(4,128)(2,1)S(1)}, u32[]{:S(2)}, u32[]{:S(2)}) %all-to-all-start.3) | async-done | bytes 737312 | tf_op jit(solution)/shard_map/all_to_all | solution.py:442
  131.3 7.7 slice.338
  139.0 8.3 copy.458
  147.3 14.6 %reshape.702 = bf16[1152,3456,1]{1,0,2:T(8,128)(2,1)} reshape(bf16[8,144,4,864]{3,2,1,0:T(4,128)(2,1)} %bitcast.287) | data formatting | bytes 15925248 | tf_op jit(solution)/shard_map/reshape | solution.py:306
  167.2 6.4 reshape.653
  173.6 16.2 %add_convert_fusion.joined_ref = bf16[4,256,3456]{2,1,0:T(8,128)(2,1)} fusion(bf16[1152,3456,1]{1,0,2:T(8,128)(2,1)} %reshape.702, f32[4,3456]{1,0:T(4,128)S(1)} %add.615, f32[4,256,1152]{2,1,0:T(8,128)} %copy-done.9, f32[4,1152]{1,0:T(4,128)S(1)} %get-tuple-element.161, f32[4,1152]{1,0:T(4,128)S(1)} %get-tuple-element.162, ...), kind=kOutput, calls=%fused_computation.15 | convolution fusion | flops 8166703104 | bytes 19859456 | tf_op jit(solution)/shard_map/dot_general | solution.py:116
  189.8 29.8 %attention_forward.1 = (bf16[4,256,1152]{2,1,0:T(8,128)(2,1)S(1)}, f32[4,16,256]{2,1,0:T(8,128)S(1)}) custom-call(bf16[4,256,3456]{2,1,0:T(8,128)(2,1)} %add_convert_fusion.joined_ref, bf16[16,256,64]{2,1,0:T(8,128)(2,1)S(1)} %pad_maximum_fusion.2.table_ref, bf16[256,64]{1,0:T(8,128)(2,1)S(1)} %add_convert_fusion.4.spots_ref), custom_call_target="tpu_custom_call" | custom-call | flops 2147483648 | bytes 9437184 | tf_op jit(solution)/shard_map/attention_forward/pallas_call | solution.py:148
  229.6 31.1 %all-gather.5.cloned.1.call-done = bf16[32,144,2304]{2,1,0:T(8,128)(2,1)} async-done(((bf16[1,144,2304]{2,1,0:T(8,128)(2,1)}), bf16[32,144,2304]{2,1,0:T(8,128)(2,1)}) %all-gather.5.cloned.1.call-update) | async-done | bytes 21233680 | tf_op jit(solution)/shard_map/all_gather | solution.py:381
  260.8 8.6 fusion.113
  269.3 8.0 copy.469
  281.1 7.9 copy.385
  294.0 15.4 %fusion.121 = f32[1024,4608]{1,0:T(8,128)} fusion(bf16[1024,1152]{1,0:T(8,128)(2,1)S(1)} %bitcast.315, bf16[1152,4608]{1,0:T(8,128)(2,1)S(1)} %bitcast.300), kind=kOutput, calls=%fused_computation.410 | convolution fusion | flops 10871635968 | bytes 31850496 | tf_op jit(solution)/shard_map/dot_general | solution.py:116
  309.4 22.0 %convolution_add_fusion = f32[1024,1152]{1,0:T(8,128)} fusion(bf16[1152,4608]{1,0:T(8,128)(2,1)} %bitcast.296, f32[1152]{0:T(1024)S(1)} %copy-done.132, f32[1024,4608]{1,0:T(8,128)} %fusion.121, f32[4608]{0:T(1024)S(1)} %copy-done.119), kind=kOutput, calls=%fused_computation.29 | convolution fusion | flops 10920001536 | bytes 34232832 | tf_op jit(solution)/shard_map/dot_general | solution.py:120
  351.3 26.3 %convert_reduce_fusion = (f32[4608]{0:T(1024)S(1)}, bf16[1024,4608]{1,0:T(8,128)(2,1)}) fusion(f32[1024,4608]{1,0:T(8,128)} %fusion.121, f32[4608]{0:T(1024)S(1)} %copy-done.119, bf16[1024,1152]{1,0:T(8,128)(2,1)S(1)} %bitcast.312, bf16[1152,4608]{1,0:T(8,128)(2,1)S(1)} %bitcast.299), kind=kOutput, calls=%fused_computation.11 | convolution fusion | flops 10980159488 | bytes 41324544 | tf_op jit(solution)/shard_map/dot_general | solution.py:116
  377.5 18.1 %convolution_convert_fusion = bf16[1152,4608]{1,0:T(8,128)(2,1)} fusion(bf16[1024,1152]{1,0:T(8,128)(2,1)S(1)} %bitcast.313, f32[1024,4608]{1,0:T(8,128)} %fusion.121, f32[4608]{0:T(1024)S(1)} %copy-done.119), kind=kOutput, calls=%fused_computation.2 | convolution fusion | flops 10924130304 | bytes 31868928 | tf_op jit(solution)/shard_map/dot_general | solution.py:126
  395.6 15.5 %reshape.704 = bf16[1152,4608,1]{1,0,2:T(8,128)(2,1)} reshape(bf16[8,144,4,1152]{3,2,1,0:T(4,128)(2,1)} %bitcast.279) | data formatting | bytes 21233664 | tf_op jit(solution)/shard_map/reshape | solution.py:306
  411.1 21.1 %multiply_reduce_fusion.2 = (bf16[4,1152]{1,0:T(4,128)(2,1)S(1)}, f32[4,256]{1,0:T(4,128)S(1)}, f32[4,256]{1,0:T(4,128)S(1)}, bf16[4,1152]{1,0:T(4,128)(2,1)S(1)}, f32[4,256,1152]{2,1,0:T(8,128)}) fusion(f32[4,256,1152]{2,1,0:T(8,128)} %copy-done.6, f32[4,256]{1,0:T(4,128)S(1)} %copy-done.116, f32[4,256]{1,0:T(4,128)S(1)} %copy-done.107, ...), kind=kOutput, calls=%fused_computation.34 | convolution fusion | flops 10882242560 | bytes 29544448 | tf_op jit(solution)/shard_map/dot_general | solution.py:120
  432.2 7.5 multiply_reduce_fusion.3
  447.2 39.3 %attention_backward.1 = (bf16[4,256,3456]{2,1,0:T(8,128)(2,1)}, f32[4,8,3456]{2,1,0:T(8,128)S(1)}, f32[16,256,104]{2,1,0:T(8,128)S(1)}) custom-call(bf16[4,256,3456]{2,1,0:T(8,128)(2,1)} %add_convert_fusion.joined_ref, f32[4,16,256]{2,1,0:T(8,128)S(1)} %get-tuple-element.36.total_ref, bf16[4,256,1152]{2,1,0:T(8,128)(2,1)S(1)} %bitcast.277, ...), custom_call_target="tpu_custom_call" | custom-call | flops 5368709120 | bytes 18874368 | tf_op jit(solution)/shard_map/attention_backward/pallas_call | solution.py:206
  486.6 16.1 %multiply_reduce_fusion.4 = (bf16[4,1152]{1,0:T(4,128)(2,1)S(1)}, f32[4,256]{1,0:T(4,128)S(1)}, f32[4,256]{1,0:T(4,128)S(1)}, bf16[4,1152]{1,0:T(4,128)(2,1)S(1)}, f32[4,256,1152]{2,1,0:T(8,128)}) fusion(f32[4,256,1152]{2,1,0:T(8,128)S(1)} %bitcast.283, f32[4,256]{1,0:T(4,128)S(1)} %copy-done.125, f32[4,256]{1,0:T(4,128)S(1)} %copy-done.114, ...), kind=kOutput, calls=%fused_computation.36 | convolution fusion | flops 8164332544 | bytes 24530944 | tf_op jit(solution)/shard_map/dot_general | solution.py:120
  502.7 14.6 %fusion.7 = bf16[1152,3456]{1,0:T(8,128)(2,1)} fusion(bf16[4,256,3456]{2,1,0:T(8,128)(2,1)} %get-tuple-element.37, f32[4,256,1152]{2,1,0:T(8,128)S(1)} %bitcast.283, f32[4,1152]{1,0:T(4,128)S(1)} %copy-done.121, f32[4,1152]{1,0:T(4,128)S(1)} %copy-done.104, f32[4,256]{1,0:T(4,128)S(1)} %copy-done.125, f32[4,256]{1,0:T(4,128)S(1)} %copy-done.114), kind=kOutput, calls=%fused_computation.14 | convolution fusion | flops 8163606528 | bytes 19804160 | tf_op jit(solution)/shard_map/dot_general | solution.py:126
  525.4 13.7 %convolution_convert_fusion.1 = bf16[1152,4608]{1,0:T(8,128)(2,1)} fusion(bf16[1024,1152]{1,0:T(8,128)(2,1)S(1)} %bitcast.316, bf16[1024,4608]{1,0:T(8,128)(2,1)S(1)} %bitcast.335), kind=kOutput, calls=%fused_computation.3 | convolution fusion | flops 10876944384 | bytes 22413312 | tf_op jit(solution)/shard_map/dot_general | solution.py:126
  539.3 14.5 %reshape.676 = bf16[4,2,144,2,2,1152]{5,4,3,2,1,0:T(2,128)(2,1)} reshape(bf16[1152,4608]{1,0:T(8,128)(2,1)} %convolution_convert_fusion) | data formatting | bytes 21233664 | tf_op jit(solution)/shard_map/reshape | solution.py:292
  570.4 20.5 %reshape.673 = bf16[4,2,144,2,2,864]{5,4,3,2,1,0:T(2,128)(2,1)} reshape(bf16[1152,3456]{1,0:T(8,128)(2,1)} %fusion.7) | data formatting | bytes 15925248 | tf_op jit(solution)/shard_map/reshape | solution.py:292
  590.9 8.2 reshape.674
  599.1 11.2 %constant_dynamic-slice_fusion.11 = (bf16[4,2,144,2,1,288]{5,4,3,2,1,0:T(2,128)(2,1)}, bf16[4,2,144,2,1,288]{5,4,3,2,1,0:T(2,128)(2,1)}) fusion(bf16[4,2,144,2,2,288]{5,4,3,2,1,0:T(2,128)(2,1)S(1)} %reshape.674, s32[]{:T(128)S(6)} %select_n.175, s32[]{:T(128)S(6)} %select_n.176), kind=kLoop, calls=%fused_computation.337 | loop fusion | bytes 5308424 | tf_op jit(solution)/shard_map/jit(dynamic_index_in_dim)/dynamic_slice | solution.py:276
  614.1 14.7 %reshape.675 = bf16[4,2,144,2,2,1152]{5,4,3,2,1,0:T(2,128)(2,1)} reshape(bf16[1152,4608]{1,0:T(8,128)(2,1)} %convolution_convert_fusion.1) | data formatting | bytes 21233664 | tf_op jit(solution)/shard_map/reshape | solution.py:292
  628.7 19.9 %constant_dynamic-slice_fusion.15 = (bf16[4,2,144,2,1,864]{5,4,3,2,1,0:T(2,128)(2,1)}, bf16[4,2,144,2,1,864]{5,4,3,2,1,0:T(2,128)(2,1)S(1)}) fusion(bf16[4,2,144,2,2,864]{5,4,3,2,1,0:T(2,128)(2,1)} %reshape.673, s32[]{:T(128)S(6)} %select_n.175, s32[]{:T(128)S(6)} %select_n.176), kind=kLoop, calls=%fused_computation.341 | loop fusion | bytes 15925256 | tf_op jit(solution)/shard_map/jit(dynamic_index_in_dim)/dynamic_slice | solution.py:276
  654.1 23.7 %constant_dynamic-slice_fusion.7 = (bf16[4,2,144,2,1,1152]{5,4,3,2,1,0:T(2,128)(2,1)}, bf16[4,2,144,2,1,1152]{5,4,3,2,1,0:T(2,128)(2,1)}) fusion(bf16[4,2,144,2,2,1152]{5,4,3,2,1,0:T(2,128)(2,1)S(1)} %copy-done.8, s32[]{:T(128)S(6)} %select_n.175, s32[]{:T(128)S(6)} %select_n.176), kind=kLoop, calls=%fused_computation.333 | loop fusion | bytes 21233672 | tf_op jit(solution)/shard_map/jit(dynamic_index_in_dim)/dynamic_slice | solution.py:276
  677.9 7.2 copy.460
  686.4 6.1 all-to-all-start.5
  692.5 25.1 %constant_dynamic-slice_fusion.3 = (bf16[4,2,144,2,1,1152]{5,4,3,2,1,0:T(2,128)(2,1)}, bf16[4,2,144,2,1,1152]{5,4,3,2,1,0:T(2,128)(2,1)S(1)}) fusion(bf16[4,2,144,2,2,1152]{5,4,3,2,1,0:T(2,128)(2,1)} %reshape.676, s32[]{:T(128)S(6)} %select_n.175, s32[]{:T(128)S(6)} %select_n.176), kind=kLoop, calls=%fused_computation.329 | loop fusion | bytes 21233672 | tf_op jit(solution)/shard_map/jit(dynamic_index_in_dim)/dynamic_slice | solution.py:276
  745.8 8.8 collective-permute-done.9
  763.8 9.3 all-to-all-done.10
  791.9 12.7 %all-to-all-done.7 = f32[8,136,144]{2,1,0:T(8,128)S(1)} async-done(((f32[8,136,144]{2,1,0:T(8,128)}), f32[8,136,144]{2,1,0:T(8,128)S(1)}, u32[]{:S(2)}, u32[]{:S(2)}) %all-to-all-start.7) | async-done | bytes 626720 | tf_op jit(solution)/shard_map/all_to_all | solution.py:272
  826.0 9.3 fusion.9
  843.6 9.1 fusion.8
  864.3 9.9 collective-permute-done.13
  880.4 22.1 %collective-permute-done.18 = bf16[2,144,2,1152]{3,1,2,0:T(8,128)(2,1)S(1)} collective-permute-done((bf16[2,144,2,1152]{3,1,2,0:T(8,128)(2,1)S(1)}, bf16[2,144,2,1152]{3,1,2,0:T(8,128)(2,1)S(1)}, u32[]{:S(2)}, u32[]{:S(2)}) %collective-permute-start.18) | collective-permute-done | bytes 1327136 | tf_op jit(solution)/shard_map/ppermute | solution.py:281
  910.0 7.2 collective-permute-done.14
  921.4 6.5 all-to-all-done.9
  937.8 8.3 collective-permute-done.17
  947.5 12.0 %all-to-all-done.11 = bf16[4,144,1152]{2,1,0:T(8,128)(2,1)S(1)} async-done(((bf16[4,144,1152]{2,1,0:T(8,128)(2,1)}), bf16[4,144,1152]{2,1,0:T(8,128)(2,1)S(1)}, u32[]{:S(2)}, u32[]{:S(2)}) %all-to-all-start.11) | async-done | bytes 1327136 | tf_op jit(solution)/shard_map/all_to_all | solution.py:299
  982.7 11.0 %all-to-all-done.12 = bf16[4,144,1152]{2,1,0:T(8,128)(2,1)S(1)} async-done(((bf16[4,144,1152]{2,1,0:T(8,128)(2,1)}), bf16[4,144,1152]{2,1,0:T(8,128)(2,1)S(1)}, u32[]{:S(2)}, u32[]{:S(2)}) %all-to-all-start.12) | async-done | bytes 1327136 | tf_op jit(solution)/shard_map/all_to_all | solution.py:299
  1003.0 12.0 %all-to-all-done.13 = f32[32,1,2482]{2,1,0:T(1,128)S(1)} async-done(((f32[32,1,2482]{2,1,0:T(1,128)}), f32[32,1,2482]{2,1,0:T(1,128)S(1)}, u32[]{:S(2)}, u32[]{:S(2)}) %all-to-all-start.13) | async-done | bytes 317728 | tf_op jit(solution)/shard_map/all_to_all | solution.py:272
  (672 shorter events, 335.3 us)
Async XLA Ops:
  7.3 118.3 %all-gather.3.cloned.1.call-start = ((), (), s32[]{:S(2)}) async-start(), calls=%async_computation.14 | async-start | bytes 10948608 | tf_op jit(solution)/shard_map/all_gather | solution.py:378
  10.3 250.5 %all-gather.5.cloned.1.call-start = ((), (), s32[]{:S(2)}) async-start(), calls=%async_computation.15 | async-start | bytes 21897216 | tf_op jit(solution)/shard_map/all_gather | solution.py:381
  14.6 30.5 %all-to-all-start = ((f32[8,1,50]{2,1,0:T(1,128)}), f32[8,1,50]{2,1,0:T(1,128)S(1)}, u32[]{:S(2)}, u32[]{:S(2)}) async-start(f32[8,1,50]{2,1,0:T(1,128)} %broadcast_in_dim.76), calls=%async_computation | async-start | bytes 8192 | tf_op jit(solution)/shard_map/all_to_all | solution.py:272
  23.5 166.4 %copy-start.2 = (bf16[256,64]{1,0:T(8,128)(2,1)}, bf16[256,64]{1,0:T(8,128)(2,1)S(1)}, u32[]{:S(2)}) copy-start(bf16[256,64]{1,0:T(8,128)(2,1)S(1)} %add_convert_fusion.4.spots_ref) | copy-start | bytes 98308
  38.8 55.7 %copy-start.77 = (bf16[4,256,16]{1,2,0:T(8,128)(2,1)}, bf16[4,256,16]{1,2,0:T(8,128)(2,1)S(1)}, u32[]{:S(2)}) copy-start(bf16[4,256,16]{1,2,0:T(8,128)(2,1)S(1)} %convert_element_type.487) | copy-start | bytes 98308
  45.8 18.2 %all-to-all-start.1 = ((bf16[8,32,288]{2,1,0:T(8,128)(2,1)}), bf16[8,32,288]{2,1,0:T(8,128)(2,1)S(1)}, u32[]{:S(2)}, u32[]{:S(2)}) async-start(bf16[8,32,288]{2,1,0:T(8,128)(2,1)} %broadcast_in_dim.77), calls=%async_computation.1 | async-start | bytes 393216 | tf_op jit(solution)/shard_map/all_to_all | solution.py:272
  66.2 19.0 %all-to-all-start.2 = ((f32[4,136,144]{2,1,0:T(8,128)}), f32[4,136,144]{2,1,0:T(8,128)S(1)}, u32[]{:S(2)}, u32[]{:S(2)}) async-start(f32[4,136,144]{2,1,0:T(8,128)} %broadcast_in_dim.80), calls=%async_computation.2 | async-start | bytes 1114112 | tf_op jit(solution)/shard_map/all_to_all | solution.py:272
  71.9 118.0 %copy-start = (bf16[16,256,64]{2,1,0:T(8,128)(2,1)}, bf16[16,256,64]{2,1,0:T(8,128)(2,1)S(1)}, u32[]{:S(2)}) copy-start(bf16[16,256,64]{2,1,0:T(8,128)(2,1)S(1)} %pad_maximum_fusion.2.table_ref) | copy-start | bytes 1572868
  91.6 32.2 %all-to-all-start.3 = ((bf16[32,4,2880]{2,1,0:T(4,128)(2,1)}), bf16[32,4,2880]{2,1,0:T(4,128)(2,1)S(1)}, u32[]{:S(2)}, u32[]{:S(2)}) async-start(bf16[32,4,2880]{2,1,0:T(4,128)(2,1)} %select_convert_fusion), calls=%async_computation.3 | async-start | bytes 1507328 | tf_op jit(solution)/shard_map/all_to_all | solution.py:442
  96.3 77.3 %copy-start.113 = (f32[4,256]{1,0:T(4,128)}, f32[4,256]{1,0:T(4,128)S(1)}, u32[]{:S(2)}) copy-start(f32[4,256]{1,0:T(4,128)S(1)} %broadcast_multiply_fusion.8) | copy-start | bytes 12292
  99.0 74.6 %copy-start.124 = (f32[4,256]{1,0:T(4,128)}, f32[4,256]{1,0:T(4,128)S(1)}, u32[]{:S(2)}) copy-start(f32[4,256]{1,0:T(4,128)S(1)} %add_rsqrt_fusion.2) | copy-start | bytes 12292
  125.1 48.5 %copy-start.103 = (f32[4,1152]{1,0:T(4,128)}, f32[4,1152]{1,0:T(4,128)S(1)}, u32[]{:S(2)}) copy-start(f32[4,1152]{1,0:T(4,128)S(1)} %get-tuple-element.162) | copy-start | bytes 55300
  125.1 48.5 %copy-start.120 = (f32[4,1152]{1,0:T(4,128)}, f32[4,1152]{1,0:T(4,128)S(1)}, u32[]{:S(2)}) copy-start(f32[4,1152]{1,0:T(4,128)S(1)} %get-tuple-element.161) | copy-start | bytes 55300
  125.1 98.2 %copy-start.87 = (f32[4,1152]{1,0:T(4,128)}, f32[4,1152]{1,0:T(4,128)S(1)}, u32[]{:S(2)}) copy-start(f32[4,1152]{1,0:T(4,128)S(1)} %get-tuple-element.163) | copy-start | bytes 55300
  125.1 100.9 %copy-start.90 = (f32[4,1152]{1,0:T(4,128)}, f32[4,1152]{1,0:T(4,128)S(1)}, u32[]{:S(2)}) copy-start(f32[4,1152]{1,0:T(4,128)S(1)} %get-tuple-element.157) | copy-start | bytes 55300
  229.6 64.3 %copy-start.41 = (bf16[4,256,1152]{2,1,0:T(8,128)(2,1)}, bf16[4,256,1152]{2,1,0:T(8,128)(2,1)S(1)}, u32[]{:S(2)}) copy-start(bf16[4,256,1152]{2,1,0:T(8,128)(2,1)S(1)} %add_convert_fusion.2) | copy-start | bytes 7077892
  439.7 46.8 %slice-start.2 = ((s8[4718592]{0:T(1024)(128)(4,1)}), s8[4194304]{0:T(1024)(128)(4,1)S(1)}, s32[]{:S(2)}) async-start(s8[4718592]{0:T(1024)(128)(4,1)} %bitcast.282), calls=%async_computation.18 | async-start | bytes 8388608
  566.9 118.5 %all-to-all-start.4 = ((f32[32,1,2084]{2,1,0:T(1,128)}), f32[32,1,2084]{2,1,0:T(1,128)}, u32[]{:S(2)}, u32[]{:S(2)}) async-start(f32[32,1,2084]{2,1,0:T(1,128)} %all_to_all.56), calls=%async_computation.4 | async-start | bytes 557056 | tf_op jit(solution)/shard_map/all_to_all | solution.py:664
  613.8 108.9 %collective-permute-start.5 = (bf16[4,2,144,2,288]{4,2,3,1,0:T(8,128)(2,1)}, bf16[4,2,144,2,288]{4,2,3,1,0:T(8,128)(2,1)}, u32[]{:S(2)}, u32[]{:S(2)}) collective-permute-start(bf16[4,2,144,2,288]{4,2,3,1,0:T(8,128)(2,1)} %bitcast.269), channel_id=1, source_target_pairs={{0,1},{1,0},{2,3},{3,2},{4,5},{5,4},{6,7},{7,6},{8,9},{9,8},{10,11... | collective-permute-start | bytes 3981320 | tf_op jit(solution)/shard_map/ppermute | solution.py:281
  651.4 126.4 %collective-permute-start = (bf16[4,2,144,2,864]{4,2,3,1,0:T(8,128)(2,1)}, bf16[4,2,144,2,864]{4,2,3,1,0:T(8,128)(2,1)}, u32[]{:S(2)}, u32[]{:S(2)}) collective-permute-start(bf16[4,2,144,2,864]{4,2,3,1,0:T(8,128)(2,1)} %bitcast.307), channel_id=1, source_target_pairs={{0,1},{1,0},{2,3},{3,2},{4,5},{5,4},{6,7},{7,6},{8,9},{9,8},{10,11... | collective-permute-start | bytes 11943944 | tf_op jit(solution)/shard_map/ppermute | solution.py:281
  685.1 140.9 %collective-permute-start.10 = (bf16[4,2,144,2,1152]{4,2,3,1,0:T(8,128)(2,1)}, bf16[4,2,144,2,1152]{4,2,3,1,0:T(8,128)(2,1)}, u32[]{:S(2)}, u32[]{:S(2)}) collective-permute-start(bf16[4,2,144,2,1152]{4,2,3,1,0:T(8,128)(2,1)} %bitcast.266), channel_id=1, source_target_pairs={{0,1},{1,0},{2,3},{3,2},{4,5},{5,4},{6,7},{7,6},{8,9},{9,8},{10,11... | collective-permute-start | bytes 15925256 | tf_op jit(solution)/shard_map/ppermute | solution.py:281
  686.4 44.1 %all-to-all-start.5 = ((bf16[32,4,2880]{2,1,0:T(4,128)(2,1)}), bf16[32,4,2880]{2,1,0:T(4,128)(2,1)}, u32[]{:S(2)}, u32[]{:S(2)}) async-start(bf16[32,4,2880]{2,1,0:T(4,128)(2,1)} %bitcast.40), calls=%async_computation.5 | async-start | bytes 1507328 | tf_op jit(solution)/shard_map/all_to_all | solution.py:594
  720.8 122.8 %collective-permute-start.15 = (bf16[4,2,144,2,1152]{4,2,3,1,0:T(8,128)(2,1)}, bf16[4,2,144,2,1152]{4,2,3,1,0:T(8,128)(2,1)}, u32[]{:S(2)}, u32[]{:S(2)}) collective-permute-start(bf16[4,2,144,2,1152]{4,2,3,1,0:T(8,128)(2,1)} %bitcast.303), channel_id=1, source_target_pairs={{0,1},{1,0},{2,3},{3,2},{4,5},{5,4},{6,7},{7,6},{8,9},{9,8},{10,11... | collective-permute-start | bytes 15925256 | tf_op jit(solution)/shard_map/ppermute | solution.py:281
  727.4 13.3 %collective-permute-start.8 = (bf16[2,144,2,288]{3,1,2,0:T(8,128)(2,1)}, bf16[2,144,2,288]{3,1,2,0:T(8,128)(2,1)}, u32[]{:S(2)}, u32[]{:S(2)}) collective-permute-start(bf16[2,144,2,288]{3,1,2,0:T(8,128)(2,1)} %dynamic-slice_bitcast_fusion.9), channel_id=1, source_target_pairs={{0,4},{4,0},{1,5},{5,1},{2,6},{6,2},{3,7},{7,3},{8,12},{12,8},{9,1... | collective-permute-start | bytes 995336 | tf_op jit(solution)/shard_map/ppermute | solution.py:281
  729.1 14.8 %collective-permute-start.6 = (bf16[2,2,144,288]{3,2,0,1:T(8,128)(2,1)}, bf16[2,2,144,288]{3,2,0,1:T(8,128)(2,1)}, u32[]{:S(2)}, u32[]{:S(2)}) collective-permute-start(bf16[2,2,144,288]{3,2,0,1:T(8,128)(2,1)} %bitcast.273), channel_id=1, source_target_pairs={{0,2},{2,0},{1,3},{3,1},{4,6},{6,4},{5,7},{7,5},{8,10},{10,8},{9,1... | collective-permute-start | bytes 995336 | tf_op jit(solution)/shard_map/ppermute | solution.py:281
  737.2 18.4 %all-to-all-start.6 = ((f32[4,136,144]{2,1,0:T(8,128)}), f32[4,136,144]{2,1,0:T(8,128)S(1)}, u32[]{:S(2)}, u32[]{:S(2)}) async-start(f32[4,136,144]{2,1,0:T(8,128)} %broadcast_in_dim.93), calls=%async_computation.6 | async-start | bytes 1114112 | tf_op jit(solution)/shard_map/all_to_all | solution.py:272
  741.9 12.7 %collective-permute-start.9 = (bf16[2,144,288]{2,1,0:T(8,128)(2,1)S(1)}, bf16[2,144,288]{2,1,0:T(8,128)(2,1)S(1)}, u32[]{:S(2)}, u32[]{:S(2)}) collective-permute-start(bf16[2,144,288]{2,1,0:T(8,128)(2,1)S(1)} %dynamic-slice_bitcast_fusion.10), channel_id=1, source_target_pairs={{0,2},{2,0},{1,3},{3,1},{4,6},{6,4},{5,7},{7,5},{8,10},{10,8},{9,1... | collective-permute-start | bytes 497672 | tf_op jit(solution)/shard_map/ppermute | solution.py:281
  745.1 9.6 collective-permute-start.7
  755.6 17.6 %all-to-all-start.10 = ((bf16[4,144,288]{2,1,0:T(8,128)(2,1)}), bf16[4,144,288]{2,1,0:T(8,128)(2,1)S(1)}, u32[]{:S(2)}, u32[]{:S(2)}) async-start(bf16[4,144,288]{2,1,0:T(8,128)(2,1)} %pad_maximum_fusion.7), calls=%async_computation.10 | async-start | bytes 884736 | tf_op jit(solution)/shard_map/all_to_all | solution.py:299
  774.3 30.4 %all-to-all-start.7 = ((f32[8,136,144]{2,1,0:T(8,128)}), f32[8,136,144]{2,1,0:T(8,128)S(1)}, u32[]{:S(2)}, u32[]{:S(2)}) async-start(f32[8,136,144]{2,1,0:T(8,128)} %broadcast_in_dim.94), calls=%async_computation.7 | async-start | bytes 2228224 | tf_op jit(solution)/shard_map/all_to_all | solution.py:272
  784.9 33.9 %collective-permute-start.3 = (bf16[2,144,2,864]{3,1,2,0:T(8,128)(2,1)}, bf16[2,144,2,864]{3,1,2,0:T(8,128)(2,1)}, u32[]{:S(2)}, u32[]{:S(2)}) collective-permute-start(bf16[2,144,2,864]{3,1,2,0:T(8,128)(2,1)} %dynamic-slice_bitcast_fusion.2), channel_id=1, source_target_pairs={{0,4},{4,0},{1,5},{5,1},{2,6},{6,2},{3,7},{7,3},{8,12},{12,8},{9,1... | collective-permute-start | bytes 2985992 | tf_op jit(solution)/shard_map/ppermute | solution.py:281
  790.5 31.3 %collective-permute-start.1 = (bf16[2,2,144,864]{3,2,0,1:T(8,128)(2,1)}, bf16[2,2,144,864]{3,2,0,1:T(8,128)(2,1)}, u32[]{:S(2)}, u32[]{:S(2)}) collective-permute-start(bf16[2,2,144,864]{3,2,0,1:T(8,128)(2,1)} %bitcast.272), channel_id=1, source_target_pairs={{0,2},{2,0},{1,3},{3,1},{4,6},{6,4},{5,7},{7,5},{8,10},{10,8},{9,1... | collective-permute-start | bytes 2985992 | tf_op jit(solution)/shard_map/ppermute | solution.py:281
  805.9 97.0 %all-to-all-start.8 = ((bf16[8,144,288]{2,1,0:T(8,128)(2,1)}), bf16[8,144,288]{2,1,0:T(8,128)(2,1)}, u32[]{:S(2)}, u32[]{:S(2)}) async-start(bf16[8,144,288]{2,1,0:T(8,128)(2,1)} %broadcast_in_dim.95), calls=%async_computation.8 | async-start | bytes 1769472 | tf_op jit(solution)/shard_map/all_to_all | solution.py:272
  821.2 38.8 %collective-permute-start.4 = (bf16[2,144,864]{2,1,0:T(8,128)(2,1)}, bf16[2,144,864]{2,1,0:T(8,128)(2,1)}, u32[]{:S(2)}, u32[]{:S(2)}) collective-permute-start(bf16[2,144,864]{2,1,0:T(8,128)(2,1)} %dynamic-slice_bitcast_fusion.7), channel_id=1, source_target_pairs={{0,2},{2,0},{1,3},{3,1},{4,6},{6,4},{5,7},{7,5},{8,10},{10,8},{9,1... | collective-permute-start | bytes 1493000 | tf_op jit(solution)/shard_map/ppermute | solution.py:281
  824.3 37.6 %collective-permute-start.2 = (bf16[2,144,864]{2,1,0:T(8,128)(2,1)S(1)}, bf16[2,144,864]{2,1,0:T(8,128)(2,1)}, u32[]{:S(2)}, u32[]{:S(2)}) collective-permute-start(bf16[2,144,864]{2,1,0:T(8,128)(2,1)S(1)} %dynamic-slice_bitcast_fusion.8), channel_id=1, source_target_pairs={{0,4},{4,0},{1,5},{5,1},{2,6},{6,2},{3,7},{7,3},{8,12},{12,8},{9,1... | collective-permute-start | bytes 1493000 | tf_op jit(solution)/shard_map/ppermute | solution.py:281
  841.9 32.4 %collective-permute-start.13 = (bf16[2,144,2,1152]{3,1,2,0:T(8,128)(2,1)}, bf16[2,144,2,1152]{3,1,2,0:T(8,128)(2,1)}, u32[]{:S(2)}, u32[]{:S(2)}) collective-permute-start(bf16[2,144,2,1152]{3,1,2,0:T(8,128)(2,1)} %dynamic-slice_bitcast_fusion.1), channel_id=1, source_target_pairs={{0,4},{4,0},{1,5},{5,1},{2,6},{6,2},{3,7},{7,3},{8,12},{12,8},{9,1... | collective-permute-start | bytes 3981320 | tf_op jit(solution)/shard_map/ppermute | solution.py:281
  842.2 35.3 %collective-permute-start.11 = (bf16[2,2,144,1152]{3,2,0,1:T(8,128)(2,1)}, bf16[2,2,144,1152]{3,2,0,1:T(8,128)(2,1)}, u32[]{:S(2)}, u32[]{:S(2)}) collective-permute-start(bf16[2,2,144,1152]{3,2,0,1:T(8,128)(2,1)} %bitcast.271), channel_id=1, source_target_pairs={{0,2},{2,0},{1,3},{3,1},{4,6},{6,4},{5,7},{7,5},{8,10},{10,8},{9,1... | collective-permute-start | bytes 3981320 | tf_op jit(solution)/shard_map/ppermute | solution.py:281
  858.3 44.3 %collective-permute-start.18 = (bf16[2,144,2,1152]{3,1,2,0:T(8,128)(2,1)S(1)}, bf16[2,144,2,1152]{3,1,2,0:T(8,128)(2,1)S(1)}, u32[]{:S(2)}, u32[]{:S(2)}) collective-permute-start(bf16[2,144,2,1152]{3,1,2,0:T(8,128)(2,1)S(1)} %dynamic-slice_bitcast_fusion), channel_id=1, source_target_pairs={{0,4},{4,0},{1,5},{5,1},{2,6},{6,2},{3,7},{7,3},{8,12},{12,8},{9,1... | collective-permute-start | bytes 3981320 | tf_op jit(solution)/shard_map/ppermute | solution.py:281
  860.1 71.4 %collective-permute-start.16 = (bf16[2,2,144,1152]{3,2,0,1:T(8,128)(2,1)}, bf16[2,2,144,1152]{3,2,0,1:T(8,128)(2,1)}, u32[]{:S(2)}, u32[]{:S(2)}) collective-permute-start(bf16[2,2,144,1152]{3,2,0,1:T(8,128)(2,1)} %bitcast.270), channel_id=1, source_target_pairs={{0,2},{2,0},{1,3},{3,1},{4,6},{6,4},{5,7},{7,5},{8,10},{10,8},{9,1... | collective-permute-start | bytes 3981320 | tf_op jit(solution)/shard_map/ppermute | solution.py:281
  876.0 41.3 %collective-permute-start.14 = (bf16[2,144,1152]{2,1,0:T(8,128)(2,1)S(1)}, bf16[2,144,1152]{2,1,0:T(8,128)(2,1)}, u32[]{:S(2)}, u32[]{:S(2)}) collective-permute-start(bf16[2,144,1152]{2,1,0:T(8,128)(2,1)S(1)} %dynamic-slice_bitcast_fusion.5), channel_id=1, source_target_pairs={{0,2},{2,0},{1,3},{3,1},{4,6},{6,4},{5,7},{7,5},{8,10},{10,8},{9,1... | collective-permute-start | bytes 1990664 | tf_op jit(solution)/shard_map/ppermute | solution.py:281
  880.1 38.6 %collective-permute-start.12 = (bf16[2,144,1152]{2,1,0:T(8,128)(2,1)}, bf16[2,144,1152]{2,1,0:T(8,128)(2,1)}, u32[]{:S(2)}, u32[]{:S(2)}) collective-permute-start(bf16[2,144,1152]{2,1,0:T(8,128)(2,1)} %dynamic-slice_bitcast_fusion.6), channel_id=1, source_target_pairs={{0,4},{4,0},{1,5},{5,1},{2,6},{6,2},{3,7},{7,3},{8,12},{12,8},{9,1... | collective-permute-start | bytes 1990664 | tf_op jit(solution)/shard_map/ppermute | solution.py:281
  902.9 24.9 %all-to-all-start.9 = ((bf16[4,144,864]{2,1,0:T(8,128)(2,1)}), bf16[4,144,864]{2,1,0:T(8,128)(2,1)}, u32[]{:S(2)}, u32[]{:S(2)}) async-start(bf16[4,144,864]{2,1,0:T(8,128)(2,1)} %pad_maximum_fusion.3), calls=%async_computation.9 | async-start | bytes 2064384 | tf_op jit(solution)/shard_map/all_to_all | solution.py:299
  908.6 27.9 %collective-permute-start.19 = (bf16[2,144,1152]{2,1,0:T(8,128)(2,1)}, bf16[2,144,1152]{2,1,0:T(8,128)(2,1)}, u32[]{:S(2)}, u32[]{:S(2)}) collective-permute-start(bf16[2,144,1152]{2,1,0:T(8,128)(2,1)} %dynamic-slice_bitcast_fusion.3), channel_id=1, source_target_pairs={{0,2},{2,0},{1,3},{3,1},{4,6},{6,4},{5,7},{7,5},{8,10},{10,8},{9,1... | collective-permute-start | bytes 1990664 | tf_op jit(solution)/shard_map/ppermute | solution.py:281
  927.9 31.6 %all-to-all-start.11 = ((bf16[4,144,1152]{2,1,0:T(8,128)(2,1)}), bf16[4,144,1152]{2,1,0:T(8,128)(2,1)S(1)}, u32[]{:S(2)}, u32[]{:S(2)}) async-start(bf16[4,144,1152]{2,1,0:T(8,128)(2,1)} %pad_maximum_fusion), calls=%async_computation.11 | async-start | bytes 2654208 | tf_op jit(solution)/shard_map/all_to_all | solution.py:299
  933.3 12.8 %collective-permute-start.17 = (bf16[2,144,1152]{2,1,0:T(8,128)(2,1)S(1)}, bf16[2,144,1152]{2,1,0:T(8,128)(2,1)S(1)}, u32[]{:S(2)}, u32[]{:S(2)}) collective-permute-start(bf16[2,144,1152]{2,1,0:T(8,128)(2,1)S(1)} %dynamic-slice_bitcast_fusion.4), channel_id=1, source_target_pairs={{0,4},{4,0},{1,5},{5,1},{2,6},{6,2},{3,7},{7,3},{8,12},{12,8},{9,1... | collective-permute-start | bytes 1990664 | tf_op jit(solution)/shard_map/ppermute | solution.py:281
  959.5 34.2 %all-to-all-start.12 = ((bf16[4,144,1152]{2,1,0:T(8,128)(2,1)}), bf16[4,144,1152]{2,1,0:T(8,128)(2,1)S(1)}, u32[]{:S(2)}, u32[]{:S(2)}) async-start(bf16[4,144,1152]{2,1,0:T(8,128)(2,1)} %pad_maximum_fusion.1), calls=%async_computation.12 | async-start | bytes 2654208 | tf_op jit(solution)/shard_map/all_to_all | solution.py:299
  981.9 44.5 %copy-start.27 = (f32[144,864]{1,0:T(8,128)S(1)}, f32[144,864]{1,0:T(8,128)}, u32[]{:S(2)}) copy-start(f32[144,864]{1,0:T(8,128)} %copy-done.26) | copy-start | bytes 1492996
  1000.3 14.7 %all-to-all-start.13 = ((f32[32,1,2482]{2,1,0:T(1,128)}), f32[32,1,2482]{2,1,0:T(1,128)S(1)}, u32[]{:S(2)}, u32[]{:S(2)}) async-start(f32[32,1,2482]{2,1,0:T(1,128)} %broadcast_in_dim.98), calls=%async_computation.13 | async-start | bytes 655360 | tf_op jit(solution)/shard_map/all_to_all | solution.py:272
  (144 other events, 1438.9 us)
Sparse Core Ops, SparseCore 0:
  11.6 111.8 all-gather.2
  127.0 133.7 all-gather.4
where the time goes:
time: 1060 us; the launch traced here: 1050 us
  local copies, waits for them, and re-layouts  344 us (32%)
  matrix products  200 us (19%)
  waiting for transfers between devices  194 us (18%)
  other arithmetic  136 us (13%)
  starting transfers between devices  79.5 us (8%)
  Pallas kernels  69.2 us (7%)
  between operations  28.4 us (3%)
    dynamic_slice x8, local copies, waits for them, and re-layouts, pick(): return lax.dynamic_index_in_dim(values, index, dim, keepdims=False)  84.5 us
    unnamed x340, local copies, waits for them, and re-layouts  74.1 us
    dot_general x7, matrix products, dot_nt(): lax.dot_general(left, right, (((1,), (1,)), ((), ())), preferred_element_...  66.7 us
    dot_general x6, matrix products, dot_nn(): return jnp.dot(left, right, preferred_element_type=jnp.float32)  65.3 us
    dot_general x9, matrix products, dot_tn(): lax.dot_general(left, right, (((0,), (0,)), ((), ())), preferred_element_...  60.9 us
    reshape x4, local copies, waits for them, and re-layouts, reduce_weight(): blocks = gradient.reshape(da, db, rows, ny, 2, width)  58 us
    ppermute x20, waiting for transfers between devices, reduce_step(): lax.ppermute(pick(values, 1 - index, dim), axis, [(0, 1), (1, 0)])  56.6 us
    all_to_all x7, waiting for transfers between devices, small_gather(): return lax.all_to_all(spread, axes, 0, 0, tiled=True)  47.1 us
  transfers between devices with their start and end apart: 36, of which 16 were waited for; matrix products, arithmetic and copies ran while one was open for 35% of the time, Pallas kernels for 3%

commit v1 on v0

--- a/solution.py
+++ b/solution.py
@@ -96,7 +96,59 @@
     return (center * inverse, inverse)
 
 
-def layernorm_back(normed, inverse, gradient):
+def column_of(modulation, index_col):
+    return modulation[:, None, index_col * D : (index_col + 1) * D]
+
+
+BIG = 58 * 1024 * 1024
+SCALE = 1.0 / math.sqrt(HD)
+JOIN = 3 * HD
+ROOT = math.sqrt(2.0 / math.pi)
+
+
+def dot_nn(left, right):
+    return jnp.dot(left, right, preferred_element_type=jnp.float32)
+
+
+def dot_nt(left, right):
+    return lax.dot_general(
+        left, right, (((1,), (1,)), ((), ())), preferred_element_type=jnp.float32
+    )
+
+
+def dot_tn(left, right):
+    return lax.dot_general(
+        left, right, (((0,), (0,)), ((), ())), preferred_element_type=jnp.float32
+    )
+
+
+def params(*order):
+    return pltpu.CompilerParams(
+        dimension_semantics=order, vmem_limit_bytes=BIG
+    )
+
+
+def cost(flops, moved, exps=0):
+    return pl.CostEstimate(flops=int(flops), bytes_accessed=int(moved), transcendentals=int(exps))
+
+
+def block_of(weight_ref, width):
+    block = weight_ref[:, 0, :, :width]
+    return block.reshape(block.shape[0] * block.shape[1], width)
+
+
+def weight_spec(weights, width, place):
+    groups, _, rows, _ = weights.shape
+    return pl.BlockSpec((groups, 1, rows, width), lambda m, i: (0, m, 0, place))
+
+
+def norm_of(values):
+    center = values - jnp.mean(values, -1, keepdims=True)
+    inverse = lax.rsqrt(jnp.mean(center * center, -1, keepdims=True) + norm_eps)
+    return center * inverse, inverse
+
+
+def norm_back(normed, inverse, gradient):
     return (
         gradient
         - jnp.mean(gradient, -1, keepdims=True)
@@ -104,88 +156,104 @@
     ) * inverse
 
 
-def column_of(modulation, index_col):
-    return modulation[:, None, index_col * D : (index_col + 1) * D]
-
-
-SCALE = 1.0 / math.sqrt(HD)
-JOIN = 3 * HD
-
-
-def dot_nn(left, right):
-    return jnp.dot(left, right, preferred_element_type=jnp.float32)
-
-
-def dot_nt(left, right):
-    return lax.dot_general(
-        left, right, (((1,), (1,)), ((), ())), preferred_element_type=jnp.float32
-    )
-
-
-def dot_tn(left, right):
-    return lax.dot_general(
-        left, right, (((0,), (0,)), ((), ())), preferred_element_type=jnp.float32
-    )
-
-
-def attention_forward_kernel(joined_ref, table_ref, spots_ref, mixed_ref, total_ref):
-    for head in range(H):
+def total_rows(values):
+    return jnp.sum(values, 0, keepdims=True)
+
+
+def ordered(kernel, count, extra):
+    def run(*refs):
+        return kernel(*refs[:count], *refs[count + extra :])
+
+    return run
+
+
+def unread(others):
+    return [pl.BlockSpec(memory_space=pl.ANY) for _ in others]
+
+
+def hold(m, last, i):
+    return jnp.where(m == last, i, 0)
+
+
+def attention_forward_kernel(
+    width, first_ref, weight_ref, added_ref, table_ref, spots_ref, joined_ref, mixed_ref, total_ref
+):
+    heads = width // JOIN
+    rows = dot_nn(first_ref[0], block_of(weight_ref, width)) + added_ref[0, 0]
+    joined_ref[0, 0] = rows.astype(jnp.bfloat16)
+    for head in range(heads):
         base = head * JOIN
-        query = joined_ref[0, :, base : base + HD]
-        keys = joined_ref[0, :, base + HD : base + 2 * HD]
-        values = joined_ref[0, :, base + 2 * HD : base + 3 * HD]
+        query = joined_ref[0, 0, :, base : base + HD]
+        keys = joined_ref[0, 0, :, base + HD : base + 2 * HD]
+        values = joined_ref[0, 0, :, base + 2 * HD : base + 3 * HD]
         scores = (dot_nt(keys, query) + dot_nt(spots_ref[...], table_ref[head])) * SCALE
         largest = jnp.max(scores, 0, keepdims=True)
         grown = jnp.exp(scores - largest)
         total = jnp.sum(grown, 0, keepdims=True)
         prob = (grown * (1.0 / total)).astype(jnp.bfloat16)
-        mixed_ref[0, :, head * HD : (head + 1) * HD] = dot_tn(prob, values).astype(jnp.bfloat16)
-        total_ref[0, head : head + 1, :] = largest + jnp.log(total)
-
-
-def attention_forward(joined_rows, table, spots):
-    images = joined_rows.shape[0]
+        mixed_ref[0, 0, :, head * HD : (head + 1) * HD] = dot_tn(prob, values).astype(jnp.bfloat16)
+        total_ref[0, 0, head : head + 1, :] = largest + jnp.log(total)
+
+
+def attention_forward(first_in, weights, lanes, width, added, table, spots):
+    images = first_in.shape[0]
+    parts = weights.shape[1]
+    heads = width // JOIN
     return pl.pallas_call(
-        attention_forward_kernel,
-        grid=(images,),
+        partial(attention_forward_kernel, width),
+        grid=(parts, images),
         in_specs=[
-            pl.BlockSpec((1, TOKS, H * JOIN), lambda i: (i, 0, 0)),
-            pl.BlockSpec(table.shape, lambda i: (0, 0, 0)),
-            pl.BlockSpec(spots.shape, lambda i: (0, 0)),
+            pl.BlockSpec((1, TOKS, D), lambda m, i: (i, 0, 0)),
+            weight_spec(weights, lanes, 0),
+            pl.BlockSpec((1, 1, 1, width), lambda m, i: (m, i, 0, 0)),
+            pl.BlockSpec((heads, TOKS, 4 * GRID), lambda m, i: (m, 0, 0)),
+            pl.BlockSpec((TOKS, 4 * GRID), lambda m, i: (0, 0)),
         ],
         out_specs=[
-            pl.BlockSpec((1, TOKS, D), lambda i: (i, 0, 0)),
-            pl.BlockSpec((1, H, TOKS), lambda i: (i, 0, 0)),
+            pl.BlockSpec((1, 1, TOKS, width), lambda m, i: (m, i, 0, 0)),
+            pl.BlockSpec((1, 1, TOKS, heads * HD), lambda m, i: (m, i, 0, 0)),
+            pl.BlockSpec((1, 1, heads, TOKS), lambda m, i: (m, i, 0, 0)),
         ],
         out_shape=[
-            jax.ShapeDtypeStruct((images, TOKS, D), jnp.bfloat16),
-            jax.ShapeDtypeStruct((images, H, TOKS), jnp.float32),
-        ],
-        cost_estimate=pl.CostEstimate(
-            flops=images * H * 4 * TOKS * TOKS * 128,
-            transcendentals=images * H * TOKS * TOKS,
-            bytes_accessed=images * TOKS * D * 8,
-        ),
-        compiler_params=pltpu.CompilerParams(vmem_limit_bytes=48 * 1024 * 1024),
+            jax.ShapeDtypeStruct((parts, images, TOKS, width), jnp.bfloat16),
+            jax.ShapeDtypeStruct((parts, images, TOKS, heads * HD), jnp.bfloat16),
+            jax.ShapeDtypeStruct((parts, images, heads, TOKS), jnp.float32),
+        ],
+        cost_estimate=cost(images * (2 * TOKS * D * 3 * D + H * 4 * TOKS * TOKS * 128), 3e7),
+        compiler_params=params("arbitrary", "arbitrary"),
         name="attention_forward",
-    )(joined_rows, table, spots)
+    )(first_in, weights, added, table, spots)
 
 
 def attention_backward_kernel(
-    joined_ref, total_ref, mixed_grad_ref, table_ref, spots_ref, grad_ref, column_ref, shift_ref
+    branch_grad_ref,
+    weight_ref,
+    joined_ref,
+    total_ref,
+    table_ref,
+    spots_ref,
+    grad_ref,
+    column_ref,
+    shift_ref,
+    mixed_grad_ref,
 ):
-    @pl.when(pl.program_id(0) == 0)
+    heads = shift_ref.shape[0]
+
+    @pl.when(pl.program_id(1) == 0)
     def start():
         shift_ref[...] = jnp.zeros_like(shift_ref)
 
-    for head in range(H):
+    mixed_grad_ref[...] = dot_nn(
+        branch_grad_ref[0], block_of(weight_ref, heads * HD)
+    ).astype(jnp.bfloat16)
+    for head in range(heads):
         base = head * JOIN
-        query = joined_ref[0, :, base : base + HD]
-        keys = joined_ref[0, :, base + HD : base + 2 * HD]
-        values = joined_ref[0, :, base + 2 * HD : base + 3 * HD]
-        mixed_grad = mixed_grad_ref[0, :, head * HD : (head + 1) * HD]
+        query = joined_ref[0, 0, :, base : base + HD]
+        keys = joined_ref[0, 0, :, base + HD : base + 2 * HD]
+        values = joined_ref[0, 0, :, base + 2 * HD : base + 3 * HD]
+        mixed_grad = mixed_grad_ref[:, head * HD : (head + 1) * HD]
         scores = (dot_nt(keys, query) + dot_nt(spots_ref[...], table_ref[head])) * SCALE
-        exact = jnp.exp(scores - total_ref[0, head : head + 1, :])
+        exact = jnp.exp(scores - total_ref[0, 0, head : head + 1, :])
         value_grad = dot_nn(exact.astype(jnp.bfloat16), mixed_grad)
         prob_grad = dot_nt(values, mixed_grad)
         shared = jnp.sum(exact * prob_grad, 0, keepdims=True)
@@ -194,43 +262,467 @@
         wide = jnp.concatenate([keys, spots_ref[:, : 2 * GRID]], 1)
         query_wide = dot_tn(score_grad, wide)
         shift_ref[head] += query_wide
-        grad_ref[0, :, base : base + HD] = (query_wide[:, :HD] * SCALE).astype(jnp.bfloat16)
-        grad_ref[0, :, base + HD : base + 2 * HD] = key_grad.astype(jnp.bfloat16)
-        grad_ref[0, :, base + 2 * HD : base + 3 * HD] = value_grad.astype(jnp.bfloat16)
-    column_ref[0] = dot_nn(jnp.ones((8, TOKS), jnp.bfloat16), grad_ref[0])
-
-
-def attention_backward(joined_rows, total, mixed_grad, table, spots):
-    images = joined_rows.shape[0]
+        grad_ref[0, 0, :, base : base + HD] = (query_wide[:, :HD] * SCALE).astype(jnp.bfloat16)
+        grad_ref[0, 0, :, base + HD : base + 2 * HD] = key_grad.astype(jnp.bfloat16)
+        grad_ref[0, 0, :, base + 2 * HD : base + 3 * HD] = value_grad.astype(jnp.bfloat16)
+    column_ref[0, 0] = dot_nn(jnp.ones((8, TOKS), jnp.bfloat16), grad_ref[0, 0])
+
+
+def attention_backward(branch_grad, weights, joined_rows, total, table, spots, others):
+    parts, images, _, width = joined_rows.shape
+    heads = width // JOIN
     wide = HD + 2 * GRID
     return pl.pallas_call(
-        attention_backward_kernel,
+        ordered(attention_backward_kernel, 6, len(others)),
+        grid=(parts, images),
+        in_specs=[
+            pl.BlockSpec((1, TOKS, D), lambda m, i: (i, 0, 0)),
+            weight_spec(weights, weights.shape[3], 0),
+            pl.BlockSpec((1, 1, TOKS, width), lambda m, i: (m, i, 0, 0)),
+            pl.BlockSpec((1, 1, heads, TOKS), lambda m, i: (m, i, 0, 0)),
+            pl.BlockSpec((heads, TOKS, 4 * GRID), lambda m, i: (m, 0, 0)),
+            pl.BlockSpec((TOKS, 4 * GRID), lambda m, i: (0, 0)),
+            *unread(others),
+        ],
+        out_specs=[
+            pl.BlockSpec((1, 1, TOKS, width), lambda m, i: (m, i, 0, 0)),
+            pl.BlockSpec((1, 1, 8, width), lambda m, i: (m, i, 0, 0)),
+            pl.BlockSpec((heads, TOKS, wide), lambda m, i: (m, 0, 0)),
+        ],
+        out_shape=[
+            jax.ShapeDtypeStruct((parts, images, TOKS, width), jnp.bfloat16),
+            jax.ShapeDtypeStruct((parts, images, 8, width), jnp.float32),
+            jax.ShapeDtypeStruct((parts * heads, TOKS, wide), jnp.float32),
+        ],
+        scratch_shapes=[pltpu.VMEM((TOKS, heads * HD), jnp.bfloat16)],
+        cost_estimate=cost(images * (2 * TOKS * D * D + H * 10 * TOKS * TOKS * 128), 5e7),
+        compiler_params=params("arbitrary", "arbitrary"),
+        name="attention_backward",
+    )(branch_grad, weights, joined_rows, total, table, spots, *others)
+
+
+def mixback_kernel(mixed_ref, weight_ref, stream_ref, mods_ref, bias_ref, branch_ref, one_ref, second_ref):
+    parts, width = mixed_ref.shape[0], mixed_ref.shape[3]
+    total = bias_ref[...]
+    for part in range(parts):
+        block = weight_ref[:, part]
+        total = total + dot_nt(
+            mixed_ref[part, 0], block.reshape(block.shape[0] * block.shape[1], width)
+        )
+    branch_ref[0] = total.astype(jnp.bfloat16)
+    stream = stream_ref[0] + mods_ref[0, 2:3] * total
+    one_ref[0] = stream
+    normed, _ = norm_of(stream)
+    second_ref[0] = (normed * (1.0 + mods_ref[0, 4:5]) + mods_ref[0, 3:4]).astype(jnp.bfloat16)
+
+
+def mixback_forward(mixed, weights, stream, mods, bias):
+    parts, images, _, width = mixed.shape
+    tile = pl.BlockSpec((1, TOKS, D), lambda i: (i, 0, 0))
+    return pl.pallas_call(
+        mixback_kernel,
         grid=(images,),
         in_specs=[
-            pl.BlockSpec((1, TOKS, H * JOIN), lambda i: (i, 0, 0)),
-            pl.BlockSpec((1, H, TOKS), lambda i: (i, 0, 0)),
-            pl.BlockSpec((1, TOKS, D), lambda i: (i, 0, 0)),
-            pl.BlockSpec(table.shape, lambda i: (0, 0, 0)),
-            pl.BlockSpec(spots.shape, lambda i: (0, 0)),
+            pl.BlockSpec((parts, 1, TOKS, width), lambda i: (0, i, 0, 0)),
+            pl.BlockSpec(weights.shape, lambda i: (0, 0, 0, 0)),
+            tile,
+            pl.BlockSpec((1, 8, D), lambda i: (i, 0, 0)),
+            pl.BlockSpec((1, D), lambda i: (0, 0)),
+        ],
+        out_specs=[tile, tile, tile],
+        out_shape=[
+            jax.ShapeDtypeStruct((images, TOKS, D), jnp.bfloat16),
+            jax.ShapeDtypeStruct((images, TOKS, D), jnp.float32),
+            jax.ShapeDtypeStruct((images, TOKS, D), jnp.bfloat16),
+        ],
+        cost_estimate=cost(images * 2 * TOKS * D * D, images * TOKS * D * 14),
+        compiler_params=params("arbitrary"),
+        name="mixback_forward",
+    )(mixed, weights, stream, mods, bias)
+
+
+def feed_forward_kernel(
+    width,
+    second_ref,
+    expand_ref,
+    narrow_ref,
+    bias_ref,
+    stream_ref,
+    mods_ref,
+    biases_ref,
+    final_ref,
+    final_bias_ref,
+    target_ref,
+    valid_ref,
+    active_ref,
+    slope_ref,
+    two_ref,
+    branch_grad_ref,
+    sums_ref,
+    final_grad_ref,
+    output_ref,
+    total_ref,
+):
+    m, i = pl.program_id(0), pl.program_id(1)
+    last = pl.num_programs(0) - 1
+    chunk = width // 3 if width % 384 == 0 else width
+    second = second_ref[0]
+    total = None
+    for begin in range(0, width, chunk):
+        columns = expand_ref[:, 0, :, begin : begin + chunk]
+        columns = columns.reshape(columns.shape[0] * columns.shape[1], chunk)
+        hidden = dot_nn(second, columns) + bias_ref[0, :, begin : begin + chunk]
+        square = hidden * hidden
+        curve = jnp.tanh(ROOT * hidden * (1.0 + 0.044715 * square))
+        half = 0.5 * (1.0 + curve)
+        active = (hidden * half).astype(jnp.bfloat16)
+        slope = half + 0.5 * hidden * (1.0 - curve * curve) * (
+            ROOT * (1.0 + 3.0 * 0.044715 * square)
+        )
+        active_ref[0, 0, :, begin : begin + chunk] = active
+        slope_ref[0, 0, :, begin : begin + chunk] = slope.astype(jnp.bfloat16)
+        columns = narrow_ref[:, 0, :, begin : begin + chunk]
+        columns = columns.reshape(columns.shape[0] * columns.shape[1], chunk)
+        product = dot_nt(active, columns)
+        total = product if total is None else total + product
+
+    @pl.when(m == 0)
+    def begin_total():
+        total_ref[i] = total
+
+    @pl.when((m > 0) & (m < last))
+    def add_total():
+        total_ref[i] += total
+
+    @pl.when(m == last)
+    def finish():
+        branch = total_ref[i] + total + biases_ref[0:1]
+        gate = mods_ref[0, 5:6]
+        scale = 1.0 + mods_ref[0, 7:8]
+        normed, inverse = norm_of(stream_ref[0] + gate * branch)
+        final_in = (normed * scale + mods_ref[0, 6:7]).astype(jnp.bfloat16)
+        error = dot_nn(final_in, final_ref[...]) + final_bias_ref[...] - target_ref[0]
+        valid = valid_ref[0, :, 0:1]
+        loss = valid * (total_rows(jnp.mean(error * error, -1, keepdims=True)))
+        output_grad = (valid * 2.0 * error / 32.0).astype(jnp.bfloat16)
+        gradient = dot_nt(output_grad, final_ref[...])
+        two = norm_back(normed, inverse, gradient * scale)
+        two_ref[0] = two
+        branch_grad = (gate * two).astype(jnp.bfloat16)
+        branch_grad_ref[0] = branch_grad
+        sums_ref[0, 0:1] = total_rows(gradient)
+        sums_ref[0, 1:2] = total_rows(gradient * normed)
+        sums_ref[0, 2:3] = total_rows(two * branch)
+        sums_ref[0, 3:4] = total_rows(branch_grad.astype(jnp.float32))
+        final_grad_ref[0] = dot_tn(output_grad, final_in)
+        output_ref[0, 0:1] = total_rows(output_grad.astype(jnp.float32))
+        output_ref[0, 1:2] = jnp.broadcast_to(loss, (1, 32))
+
+
+def feed_forward(second_in, weights, lanes, width, bias, stream, mods, biases, final, final_bias, target, valid):
+    images = second_in.shape[0]
+    parts = weights.shape[1]
+    last = parts - 1
+    tile = pl.BlockSpec((1, TOKS, D), lambda m, i: (i, 0, 0))
+    late = pl.BlockSpec((1, TOKS, D), lambda m, i: (hold(m, last, i), 0, 0))
+    wide = pl.BlockSpec((1, 1, TOKS, width), lambda m, i: (m, i, 0, 0))
+    fixed = lambda shape: pl.BlockSpec(shape, lambda m, i: (0,) * len(shape))
+    lately = lambda shape: pl.BlockSpec((1,) + shape, lambda m, i: (hold(m, last, i), 0, 0))
+    return pl.pallas_call(
+        partial(feed_forward_kernel, width),
+        grid=(parts, images),
+        in_specs=[
+            tile,
+            weight_spec(weights, lanes, 0),
+            weight_spec(weights, lanes, 1),
+            pl.BlockSpec((1, 1, width), lambda m, i: (m, 0, 0)),
+            late,
+            pl.BlockSpec((1, 8, D), lambda m, i: (i, 0, 0)),
+            fixed(biases.shape),
+            fixed(final.shape),
+            fixed(final_bias.shape),
+            lately((TOKS, 32)),
+            pl.BlockSpec((1, 1, 128), lambda m, i: (i, 0, 0)),
+        ],
+        out_specs=[wide, wide, late, late, lately((4, D)), lately((32, D)), lately((2, 32))],
+        out_shape=[
+            jax.ShapeDtypeStruct((parts, images, TOKS, width), jnp.bfloat16),
+            jax.ShapeDtypeStruct((parts, images, TOKS, width), jnp.bfloat16),
+            jax.ShapeDtypeStruct((images, TOKS, D), jnp.float32),
+            jax.ShapeDtypeStruct((images, TOKS, D), jnp.bfloat16),
+            jax.ShapeDtypeStruct((images, 4, D), jnp.float32),
+            jax.ShapeDtypeStruct((images, 32, D), jnp.float32),
+            jax.ShapeDtypeStruct((images, 2, 32), jnp.float32),
+        ],
+        scratch_shapes=[pltpu.VMEM((images, TOKS, D), jnp.float32)],
+        cost_estimate=cost(images * 4 * TOKS * D * FF, 6e7, images * TOKS * FF),
+        compiler_params=params("arbitrary", "arbitrary"),
+        name="feed_forward",
+    )(second_in, weights, weights, bias, stream, mods, biases, final, final_bias, target, valid)
+
+
+def feed_backward_kernel(
+    width,
+    branch_grad_ref,
+    expand_ref,
+    narrow_ref,
+    slope_ref,
+    two_ref,
+    stream_ref,
+    branch_ref,
+    mods_ref,
+    hidden_grad_ref,
+    hidden_sum_ref,
+    one_ref,
+    first_grad_ref,
+    sums_ref,
+    total_ref,
+):
+    m, i = pl.program_id(0), pl.program_id(1)
+    last = pl.num_programs(0) - 1
+    chunk = width // 3 if width % 384 == 0 else width
+    branch_grad = branch_grad_ref[0]
+
+    @pl.when(i == 0)
+    def start():
+        hidden_sum_ref[...] = jnp.zeros_like(hidden_sum_ref)
+
+    total = None
+    for begin in range(0, width, chunk):
+        columns = narrow_ref[:, 0, :, begin : begin + chunk]
+        columns = columns.reshape(columns.shape[0] * columns.shape[1], chunk)
+        active_grad = dot_nn(branch_grad, columns)
+        hidden_grad = (
+            active_grad * slope_ref[0, 0, :, begin : begin + chunk].astype(jnp.float32)
+        ).astype(jnp.bfloat16)
+        hidden_grad_ref[0, 0, :, begin : begin + chunk] = hidden_grad
+        hidden_sum_ref[0, :, begin : begin + chunk] += total_rows(hidden_grad.astype(jnp.float32))
+        columns = expand_ref[:, 0, :, begin : begin + chunk]
+        columns = columns.reshape(columns.shape[0] * columns.shape[1], chunk)
+        product = dot_nt(hidden_grad, columns)
+        total = product if total is None else total + product
+
+    @pl.when(m == 0)
+    def begin_total():
+        total_ref[i] = total
+
+    @pl.when((m > 0) & (m < last))
+    def add_total():
+        total_ref[i] += total
+
+    @pl.when(m == last)
+    def finish():
+        gradient = total_ref[i] + total
+        normed, inverse = norm_of(stream_ref[0])
+        one = two_ref[0] + norm_back(normed, inverse, gradient * (1.0 + mods_ref[0, 4:5]))
+        one_ref[0] = one
+        first_grad = (mods_ref[0, 2:3] * one).astype(jnp.bfloat16)
+        first_grad_ref[0] = first_grad
+        sums_ref[0, 0:1] = total_rows(gradient)
+        sums_ref[0, 1:2] = total_rows(gradient * normed)
+        sums_ref[0, 2:3] = total_rows(one * branch_ref[0].astype(jnp.float32))
+        sums_ref[0, 3:4] = total_rows(first_grad.astype(jnp.float32))
+
+
+def feed_backward(branch_grad, weights, lanes, width, slope, two, stream, branch, mods, others):
+    images = branch_grad.shape[0]
+    parts = weights.shape[1]
+    last = parts - 1
+    tile = pl.BlockSpec((1, TOKS, D), lambda m, i: (i, 0, 0))
+    late = pl.BlockSpec((1, TOKS, D), lambda m, i: (hold(m, last, i), 0, 0))
+    wide = pl.BlockSpec((1, 1, TOKS, width), lambda m, i: (m, i, 0, 0))
+    return pl.pallas_call(
+        ordered(partial(feed_backward_kernel, width), 8, len(others)),
+        grid=(parts, images),
+        in_specs=[
+            tile,
+            weight_spec(weights, lanes, 0),
+            weight_spec(weights, lanes, 1),
+            wide,
+            late,
+            late,
+            late,
+            pl.BlockSpec((1, 8, D), lambda m, i: (i, 0, 0)),
+            *unread(others),
         ],
         out_specs=[
-            pl.BlockSpec((1, TOKS, H * JOIN), lambda i: (i, 0, 0)),
-            pl.BlockSpec((1, 8, H * JOIN), lambda i: (i, 0, 0)),
-            pl.BlockSpec((H, TOKS, wide), lambda i: (0, 0, 0)),
+            wide,
+            pl.BlockSpec((1, 1, width), lambda m, i: (m, 0, 0)),
+            late,
+            late,
+            pl.BlockSpec((1, 4, D), lambda m, i: (hold(m, last, i), 0, 0)),
         ],
         out_shape=[
-            jax.ShapeDtypeStruct((images, TOKS, H * JOIN), jnp.bfloat16),
-            jax.ShapeDtypeStruct((images, 8, H * JOIN), jnp.float32),
-            jax.ShapeDtypeStruct((H, TOKS, wide), jnp.float32),
-        ],
-        cost_estimate=pl.CostEstimate(
-            flops=images * H * 10 * TOKS * TOKS * 128,
-            transcendentals=images * H * TOKS * TOKS,
-            bytes_accessed=images * TOKS * D * 16,
+            jax.ShapeDtypeStruct((parts, images, TOKS, width), jnp.bfloat16),
+            jax.ShapeDtypeStruct((parts, 1, width), jnp.float32),
+            jax.ShapeDtypeStruct((images, TOKS, D), jnp.float32),
+            jax.ShapeDtypeStruct((images, TOKS, D), jnp.bfloat16),
+            jax.ShapeDtypeStruct((images, 4, D), jnp.float32),
+        ],
+        scratch_shapes=[pltpu.VMEM((images, TOKS, D), jnp.float32)],
+        cost_estimate=cost(images * 4 * TOKS * D * FF, 6e7),
+        compiler_params=params("arbitrary", "arbitrary"),
+        name="feed_backward",
+    )(branch_grad, weights, weights, slope, two, stream, branch, mods, *others)
+
+
+def joined_backward_kernel(
+    width,
+    grad_ref,
+    weight_ref,
+    one_ref,
+    zero_ref,
+    mods_ref,
+    embed_ref,
+    sums_ref,
+    embed_grad_ref,
+    total_ref,
+):
+    m, i = pl.program_id(0), pl.program_id(1)
+    last = pl.num_programs(0) - 1
+    total = dot_nt(grad_ref[0, 0], block_of(weight_ref, width))
+
+    @pl.when(m == 0)
+    def begin_total():
+        total_ref[i] = total
+
+    @pl.when((m > 0) & (m < last))
+    def add_total():
+        total_ref[i] += total
+
+    @pl.when(m == last)
+    def finish():
+        gradient = total_ref[i] + total
+        normed, inverse = norm_of(zero_ref[0])
+        zero = one_ref[0] + norm_back(normed, inverse, gradient * (1.0 + mods_ref[0, 1:2]))
+        sums_ref[0, 0:1] = total_rows(gradient)
+        sums_ref[0, 1:2] = total_rows(gradient * normed)
+        sums_ref[0, 2:3] = total_rows(zero)
+        sums_ref[0, 3:4] = jnp.zeros((1, D), jnp.float32)
+        upper = zero.astype(jnp.bfloat16)
+        lower = (zero - upper.astype(jnp.float32)).astype(jnp.bfloat16)
+        embed_grad_ref[0] = dot_tn(embed_ref[0], upper) + dot_tn(embed_ref[0], lower)
+
+
+def joined_backward(grad_joined, weights, lanes, one, zero, mods, embed_in, others):
+    parts, images, _, width = grad_joined.shape
+    last = parts - 1
+    late = pl.BlockSpec((1, TOKS, D), lambda m, i: (hold(m, last, i), 0, 0))
+    return pl.pallas_call(
+        ordered(partial(joined_backward_kernel, width), 6, len(others)),
+        grid=(parts, images),
+        in_specs=[
+            pl.BlockSpec((1, 1, TOKS, width), lambda m, i: (m, i, 0, 0)),
+            weight_spec(weights, lanes, 0),
+            late,
+            late,
+            pl.BlockSpec((1, 8, D), lambda m, i: (i, 0, 0)),
+            pl.BlockSpec((1, TOKS, 16), lambda m, i: (i, 0, 0)),
+            *unread(others),
+        ],
+        out_specs=[
+            pl.BlockSpec((1, 4, D), lambda m, i: (hold(m, last, i), 0, 0)),
+            pl.BlockSpec((1, 16, D), lambda m, i: (hold(m, last, i), 0, 0)),
+        ],
+        out_shape=[
+            jax.ShapeDtypeStruct((images, 4, D), jnp.float32),
+            jax.ShapeDtypeStruct((images, 16, D), jnp.float32),
+        ],
+        scratch_shapes=[pltpu.VMEM((images, TOKS, D), jnp.float32)],
+        cost_estimate=cost(images * 2 * TOKS * D * 3 * D, 3e7),
+        compiler_params=params("arbitrary", "arbitrary"),
+        name="joined_backward",
+    )(grad_joined, weights, one, zero, mods, embed_in, *others)
+
+
+def weight_gradient_kernel(widths, *refs):
+    pairs = len(widths)
+    inputs, gradients = refs[:pairs], refs[pairs : 2 * pairs]
+    received_ref = refs[2 * pairs] if len(refs) == 3 * pairs + 2 else None
+    grad_ref, turned = refs[-pairs - 1], refs[-pairs:]
+
+    @pl.when((pl.program_id(0) == 0) & (pl.program_id(1) == 0))
+    def turn():
+        for turned_ref, inputs_ref in zip(turned, inputs):
+            turned_ref[...] = inputs_ref[...].T
+
+    begin = 0
+    for width, turned_ref, gradient_ref in zip(widths, turned, gradients):
+        product = dot_nn(turned_ref[...], gradient_ref[0])
+        if received_ref is not None:
+            product = product + received_ref[0, :, begin : begin + width].astype(jnp.float32)
+        grad_ref[0, :, begin : begin + width] = product.astype(jnp.bfloat16)
+        begin = begin + width
+
+
+def weight_gradient(pairs, chosen, cores, received=None, others=()):
+    rows = pairs[0][0].shape[0]
+    parts = pairs[0][1].shape[0]
+    widths = [gradient.shape[2] for _, gradient in pairs]
+    width = sum(widths)
+    chunks = 3 if len(pairs) == 1 and width % 384 == 0 else 1
+    pieces = [member // chunks for member in widths]
+    count = parts // cores
+    taken = 2 * len(pairs) + (received is not None)
+    kernel = ordered(partial(weight_gradient_kernel, pieces), taken, len(others))
+    out_spec = pl.BlockSpec((1, D, width // chunks), lambda y, k, chosen: (y, 0, k))
+    in_specs = [pl.BlockSpec((rows, D), lambda y, k, chosen: (0, 0)) for _ in pairs] + [
+        pl.BlockSpec((1, rows, piece), lambda y, k, chosen: (y * cores + chosen[0], 0, k))
+        for piece in pieces
+    ]
+    operands = [member for member, _ in pairs] + [member for _, member in pairs]
+    if received is not None:
+        in_specs.append(out_spec)
+        operands.append(received)
+    return pl.pallas_call(
+        lambda chosen_ref, *refs: kernel(*refs),
+        grid_spec=pltpu.PrefetchScalarGridSpec(
+            num_scalar_prefetch=1,
+            grid=(count, chunks),
+            in_specs=in_specs + unread(others),
+            out_specs=out_spec,
+            scratch_shapes=[pltpu.VMEM((D, rows), jnp.bfloat16) for _ in pairs],
         ),
-        compiler_params=pltpu.CompilerParams(vmem_limit_bytes=48 * 1024 * 1024),
-        name="attention_backward",
-    )(joined_rows, total, mixed_grad, table, spots)
+        out_shape=jax.ShapeDtypeStruct((count, D, width), jnp.bfloat16),
+        cost_estimate=cost(2 * rows * D * width * count, rows * (D + width * count) * 2),
+        compiler_params=params("arbitrary", "arbitrary"),
+        name="weight_gradient",
+    )(chosen, *operands, *others)
+
+
+def whole_gradient_kernel(inputs_ref, gradient_ref, grad_ref, turned_ref):
+    @pl.when((pl.program_id(0) == 0) & (pl.program_id(1) == 0))
+    def turn():
+        turned_ref[...] = inputs_ref[...].T
+
+    product = dot_nn(turned_ref[...], gradient_ref[0]).astype(jnp.bfloat16)
+    groups, _, rows, width = grad_ref.shape
+    grad_ref[:, 0] = product.reshape(groups, rows, width)
+
+
+def whole_gradient(inputs, gradient, groups):
+    rows = inputs.shape[0]
+    parts, _, width = gradient.shape
+    chunks = 3 if width % 384 == 0 else 1
+    piece = width // chunks
+    split = groups if (D // groups) % 16 == 0 else 1
+    result = pl.pallas_call(
+        whole_gradient_kernel,
+        grid=(parts, chunks),
+        in_specs=[
+            pl.BlockSpec((rows, D), lambda m, k: (0, 0)),
+            pl.BlockSpec((1, rows, piece), lambda m, k: (m, 0, k)),
+        ],
+        out_specs=pl.BlockSpec((split, 1, D // split, piece), lambda m, k: (0, m, 0, k)),
+        out_shape=jax.ShapeDtypeStruct((split, parts, D // split, width), jnp.bfloat16),
+        scratch_shapes=[pltpu.VMEM((D, rows), jnp.bfloat16)],
+        cost_estimate=cost(2 * rows * D * width * parts, rows * (D + width * parts) * 2),
+        compiler_params=params("arbitrary", "arbitrary"),
+        name="whole_gradient",
+    )(inputs, gradient)
+    if split == 1:
+        result = result.reshape(parts, groups, D // groups, width).transpose(1, 0, 2, 3)
+    return result.reshape(groups * parts, D // groups, width)
 
 
 def relative_tables(rel_table):
@@ -276,34 +768,100 @@
     return lax.dynamic_index_in_dim(values, index, dim, keepdims=False)
 
 
-def reduce_step(values, dim, axis, size, index):
-    if size == 2:
-        received = lax.ppermute(pick(values, 1 - index, dim), axis, [(0, 1), (1, 0)])
-        return pick(values, index, dim).astype(jnp.float32) + received.astype(jnp.float32)
-    moved = jnp.moveaxis(values, dim, 0)
-    received = lax.all_to_all(moved, axis, 0, 0, tiled=True)
-    return jnp.sum(received.astype(jnp.float32), 0)
-
-
-def reduce_weight(gradient, sizes, places):
-    da, db, ny = (sizes[key] for key in ("da", "db", "y"))
-    rows = gradient.shape[0] // (da * db)
-    width = gradient.shape[1] // (ny * 2)
-    blocks = gradient.reshape(da, db, rows, ny, 2, width)
-    kept = reduce_step(blocks, 4, "c", 2, places["c"]).astype(jnp.bfloat16)
-    half = da // 2
-    first = reduce_step(kept[:half], 3, "y", ny, places["y"]).astype(jnp.bfloat16)
-    second = reduce_step(kept[half:], 1, "db", db, places["db"]).astype(jnp.bfloat16)
-    first = reduce_step(first, 1, "db", db, places["db"]).astype(jnp.bfloat16)
-    second = reduce_step(second, 2, "y", ny, places["y"]).astype(jnp.bfloat16)
-    received = lax.all_to_all(jnp.concatenate([first, second], 0), "da", 0, 0, tiled=True)
-    return jnp.sum(received.astype(jnp.float32), 0)
-
-
-def whole_weight(gathered, groups, parts, begin, width):
-    block = gathered.reshape(groups, parts, gathered.shape[1], gathered.shape[2])
-    block = block[:, :, :, begin : begin + width].transpose(0, 2, 1, 3)
-    return block.reshape(groups * gathered.shape[1], parts * width)
+def tie(*values):
+    return lax.optimization_barrier(values)
+
+
+def swap(values, axis):
+    return lax.ppermute(values, axis, [(0, 1), (1, 0)])
+
+
+class Exchange:
+    def __init__(self, sizes, places):
+        self.sizes, self.places = sizes, places
+        self.chosen = places["c"].astype(jnp.int32).reshape(1)
+
+    def gradient(self, pairs, others=()):
+        self.sent = weight_gradient(pairs, 1 - self.chosen, self.sizes["c"], None, others)
+        self.received = swap(self.sent, "c")
+
+    def kept_gradient(self, pairs, others=()):
+        return weight_gradient(pairs, self.chosen, self.sizes["c"], self.received, others)
+
+    def prepare(self, values, dim, axis):
+        size, index = self.sizes[axis], self.places[axis]
+        if size == 2:
+            return pick(values, 1 - index, dim), pick(values, index, dim)
+        return jnp.moveaxis(values, dim, 0), None
+
+    def launch_one(self, sent, axis):
+        if self.sizes[axis] == 2:
+            return swap(sent, axis)
+        return lax.all_to_all(sent, axis, 0, 0, tiled=True)
+
+    def open_first(self, kept):
+        da, db, ny = (self.sizes[key] for key in ("da", "db", "y"))
+        kept = kept.reshape(ny, da, db, D // (da * db), kept.shape[2])
+        half = da // 2
+        sent_a, own_a = self.prepare(kept[:, :half], 0, "y")
+        sent_b, own_b = self.prepare(kept[:, half:], 2, "db")
+        self.own, self.axes = (own_a, own_b), ("y", "db")
+        self.sent = (sent_a, sent_b)
+
+    def launch(self):
+        self.arrived = tuple(map(self.launch_one, self.sent, self.axes))
+
+    def close(self):
+        def add(own, arrived):
+            if own is None:
+                return jnp.sum(arrived.astype(jnp.float32), 0).astype(jnp.bfloat16)
+            return (own.astype(jnp.float32) + arrived.astype(jnp.float32)).astype(jnp.bfloat16)
+
+        return tuple(map(add, self.own, self.arrived))
+
+    def open_second(self):
+        part_a, part_b = self.close()
+        sent_a, own_a = self.prepare(part_a, 1, "db")
+        sent_b, own_b = self.prepare(part_b, 0, "y")
+        self.own, self.axes = (own_a, own_b), ("db", "y")
+        self.sent = (sent_a, sent_b)
+
+    def open_last(self):
+        joint = jnp.concatenate(self.close(), 0)
+        size, index = self.sizes["da"], self.places["da"]
+        if size > 4:
+            self.own, self.sent = None, (joint,)
+            return
+        self.own = pick(joint, index, 0)
+        self.sent = tuple(pick(joint, (index + shift) % size, 0) for shift in range(1, size))
+
+    def launch_last(self):
+        size = self.sizes["da"]
+        if self.own is None:
+            self.arrived = (lax.all_to_all(self.sent[0], "da", 0, 0, tiled=True),)
+            return
+        self.arrived = tuple(
+            lax.ppermute(sent, "da", [(place, (place + shift + 1) % size) for place in range(size)])
+            for shift, sent in enumerate(self.sent)
+        )
+
+    def result(self):
+        if self.own is None:
+            return jnp.sum(self.arrived[0].astype(jnp.float32), 0)
+        return sum((member.astype(jnp.float32) for member in self.arrived), self.own.astype(jnp.float32))
+
+
+def lane_padded(values):
+    width = values.shape[1]
+    return jnp.pad(values, ((0, 0), (0, -width % 128)))
+
+
+def in_parts(gathered, groups, parts):
+    rows, width = gathered.shape[1:]
+    blocks = gathered.reshape(groups, parts, rows, width)
+    if rows % 16 == 0:
+        return blocks
+    return blocks.transpose(1, 0, 2, 3).reshape(1, parts, groups * rows, width)
 
 
 def adamw_update(master, moment, second, gradient):
@@ -375,16 +933,17 @@
     width_mp = timetwo_weight.shape[1]
     mod_width = modulator_weight.shape[1]
 
-    gathered_one = lax.all_gather(
-        jnp.concatenate([joined_weight, mixback_weight], 1).astype(jnp.bfloat16), all_axes
-    )
-    gathered_two = lax.all_gather(
-        jnp.concatenate([expand_weight, narrow_weight], 1).astype(jnp.bfloat16), all_axes
-    )
-    joined = whole_weight(gathered_one, dp, mp, 0, joined_weight.shape[1])
-    mixback = whole_weight(gathered_one, dp, mp, joined_weight.shape[1], mixback_weight.shape[1])
-    expand = whole_weight(gathered_two, dp, mp, 0, expand_weight.shape[1])
-    narrow = whole_weight(gathered_two, dp, mp, expand_weight.shape[1], narrow_weight.shape[1])
+    joined_width, mixback_width = (joined_weight.shape[1], mixback_weight.shape[1])
+    hidden_width = expand_weight.shape[1]
+    shard_one = jnp.concatenate([lane_padded(joined_weight), mixback_weight], 1)
+    shard_two = jnp.concatenate([lane_padded(expand_weight), lane_padded(narrow_weight)], 1)
+    gathered_one = in_parts(
+        lax.all_gather(shard_one.astype(jnp.bfloat16), all_axes), dp, mp
+    )
+    feed = in_parts(lax.all_gather(shard_two.astype(jnp.bfloat16), all_axes), dp, mp)
+    joined_lanes = gathered_one.shape[3] - mixback_width
+    hidden_lanes = feed.shape[3] // 2
+    mixback = gathered_one[:, :, :, joined_lanes:]
 
     facts = small_gather(
         jnp.concatenate([timesteps, labels, dropped, buckets, counts]).astype(jnp.float32),
@@ -398,9 +957,6 @@
     token_count = jnp.sum(facts[:, 3 * group_size + 1]) * TOKS
     time_first = small_gather(timeone_weight.astype(jnp.bfloat16), dp_axes, dp).reshape(
         FREQ, width_mp
-    )
-    time_second_all = small_gather(timetwo_weight.astype(jnp.bfloat16), dp_axes, dp).reshape(
-        D, width_mp
     )
     bucket_width = float(1000 // NB)
     rows_in = frequencies(
@@ -460,6 +1016,7 @@
     spots = spot_table()
     images = own_images
     rows_all = images * TOKS
+    mods = modulation[:, : 8 * D].reshape(images, 8, D)
 
     embed_in = noisy_all.astype(jnp.bfloat16)
     stream_zero = (
@@ -472,12 +1029,10 @@
         + small_piece("embed_bias")
         + position_table()
     )
-    normed_a, inverse_a = layernorm_parts(stream_zero)
+    normed_a, _ = layernorm_parts(stream_zero)
     first_in = (
-        (normed_a * (1.0 + column_of(modulation, 1)) + column_of(modulation, 0))
-        .astype(jnp.bfloat16)
-        .reshape(rows_all, D)
-    )
+        normed_a * (1.0 + column_of(modulation, 1)) + column_of(modulation, 0)
+    ).astype(jnp.bfloat16)
     added = jnp.stack(
         [
             (small_piece("query_bias") + modulation[:, 8 * D : 9 * D]).reshape(images, H, HD),
@@ -485,108 +1040,95 @@
             (small_piece("value_bias") + modulation[:, 9 * D :]).reshape(images, H, HD),
         ],
         2,
-    ).reshape(images, 1, 3 * D)
-    joined_rows = (
-        dot_nn(first_in, joined).reshape(images, TOKS, 3 * D) + added
-    ).astype(jnp.bfloat16)
-    mixed_heads, log_total = attention_forward(joined_rows, table, spots)
-    mixed_heads = mixed_heads.reshape(rows_all, D)
-    branch = (dot_nt(mixed_heads, mixback) + small_piece("out_bias")).reshape(images, TOKS, D)
-    stream_one = stream_zero + column_of(modulation, 2) * branch
-    normed_b, inverse_b = layernorm_parts(stream_one)
-    second_in = (
-        (normed_b * (1.0 + column_of(modulation, 4)) + column_of(modulation, 3))
-        .astype(jnp.bfloat16)
-        .reshape(rows_all, D)
-    )
-    hidden = dot_nn(second_in, expand) + small_piece("fc1_bias")
-    active = jax.nn.gelu(hidden, approximate=True).astype(jnp.bfloat16)
-    branch_two = (dot_nt(active, narrow) + small_piece("fc2_bias")).reshape(images, TOKS, D)
-    stream_two = stream_one + column_of(modulation, 5) * branch_two
-    normed_c, inverse_c = layernorm_parts(stream_two)
-    final_in = (
-        (normed_c * (1.0 + column_of(modulation, 7)) + column_of(modulation, 6))
-        .astype(jnp.bfloat16)
-        .reshape(rows_all, D)
-    )
-    output = dot_nn(final_in, final_weight.astype(jnp.bfloat16)) + small_piece("final_bias")
-
-    residual_error = output - target.reshape(rows_all, 32)
-    valid_rows = jnp.repeat(valid_flags, TOKS)[:, None]
-    loss_part = jnp.sum(valid_rows * jnp.mean(residual_error * residual_error, -1, keepdims=True))
-    grad_out = (valid_rows * 2.0 * residual_error / 32.0).astype(jnp.bfloat16)
-    grad_small = {}
-    grad_small["final_bias"] = jnp.sum(grad_out.astype(jnp.float32), 0)
-    grad_small["final_weight"] = dot_tn(final_in, grad_out).reshape(32 * D)
-    grad_final = dot_nt(grad_out, final_weight.astype(jnp.bfloat16)).reshape(images, TOKS, D)
-
-    def modulate_back(gradient, normed, inverse, scale_col):
-        scaled = gradient * (1.0 + column_of(modulation, scale_col))
-        return (
-            layernorm_back(normed, inverse, scaled),
-            jnp.sum(gradient, 1),
-            jnp.sum(gradient * normed, 1),
-        )
-
-    grad_two, shift_c, scale_c = modulate_back(grad_final, normed_c, inverse_c, 7)
-    grad_branch_two = (
-        (column_of(modulation, 5) * grad_two).astype(jnp.bfloat16).reshape(rows_all, D)
-    )
-    gate_two = jnp.sum(grad_two * branch_two, 1)
-    grad_small["fc2_bias"] = jnp.sum(grad_branch_two.astype(jnp.float32), 0)
-    narrow_grad = reduce_weight(
-        dot_tn(grad_branch_two, active).astype(jnp.bfloat16), sizes, places_now
-    )
-    grad_active = dot_nn(grad_branch_two, narrow)
-    _, pullback = jax.vjp(partial(jax.nn.gelu, approximate=True), hidden)
-    grad_hidden = pullback(grad_active)[0].astype(jnp.bfloat16)
-    grad_small["fc1_bias"] = jnp.sum(grad_hidden.astype(jnp.float32), 0)
-    expand_grad = reduce_weight(
-        dot_tn(second_in, grad_hidden).astype(jnp.bfloat16), sizes, places_now
-    )
-    grad_second = dot_nt(grad_hidden, expand).reshape(images, TOKS, D)
-    grad_one_part, shift_b, scale_b = modulate_back(grad_second, normed_b, inverse_b, 4)
-    grad_one = grad_two + grad_one_part
-    grad_branch = (column_of(modulation, 2) * grad_one).astype(jnp.bfloat16).reshape(rows_all, D)
-    gate_one = jnp.sum(grad_one * branch, 1)
-    grad_small["out_bias"] = jnp.sum(grad_branch.astype(jnp.float32), 0)
-    mixback_grad = reduce_weight(
-        dot_tn(grad_branch, mixed_heads).astype(jnp.bfloat16), sizes, places_now
-    )
-    grad_mixed = dot_nn(grad_branch, mixback).astype(jnp.bfloat16).reshape(images, TOKS, D)
+    )
+    added = added.reshape(images, mp, joined_width).transpose(1, 0, 2)[:, :, None]
+    joined_rows, mixed, log_total = attention_forward(
+        first_in, gathered_one, joined_lanes, joined_width, added, table, spots
+    )
+    branch, stream_one, second_in = mixback_forward(
+        mixed, mixback, stream_zero, mods, small_piece("out_bias")[None]
+    )
+    timetwo_narrow, second_in = tie(timetwo_weight.astype(jnp.bfloat16), second_in)
+    time_second_all = small_gather(timetwo_narrow, dp_axes, dp)
+    active, slope, grad_two, grad_branch_two, sums_c, final_grads, output_sums = feed_forward(
+        second_in,
+        feed,
+        hidden_lanes,
+        hidden_width,
+        small_piece("fc1_bias").reshape(mp, 1, hidden_width),
+        stream_one,
+        mods,
+        small_piece("fc2_bias")[None],
+        final_weight.astype(jnp.bfloat16),
+        small_piece("final_bias")[None],
+        target,
+        jnp.broadcast_to(valid_flags[:, None, None], (images, 1, 128)),
+    )
+    loss_part = jnp.sum(output_sums[:, 1, 0])
+    time_second_all, grad_branch_two = tie(time_second_all, grad_branch_two)
+    time_second_all = time_second_all.reshape(D, width_mp)
+
+    def flat(values):
+        return values.reshape(rows_all, D)
+
+    def in_rows(values):
+        return values.reshape(mp, rows_all, values.shape[3])
+
+    narrow_sum, heads_sum = (Exchange(sizes, places_now) for _ in range(2))
+    narrow_pairs = [(flat(grad_branch_two), in_rows(active))]
+    narrow_sum.gradient(narrow_pairs)
+    grad_hidden, hidden_sums, grad_one, grad_branch, sums_b = feed_backward(
+        grad_branch_two,
+        feed,
+        hidden_lanes,
+        hidden_width,
+        slope,
+        grad_two,
+        stream_one,
+        branch,
+        mods,
+        [narrow_sum.sent],
+    )
+    expand_all = whole_gradient(flat(second_in), in_rows(grad_hidden), dp)
+    expand_shard = lax.psum_scatter(expand_all, all_axes, scatter_dimension=0, tiled=True)[0]
+    narrow_sum.open_first(narrow_sum.kept_gradient(narrow_pairs, [expand_all]))
+    narrow_sum.launch()
     grad_joined, column_sums, shifts = attention_backward(
-        joined_rows, log_total, grad_mixed, table, spots
-    )
-    grad_joined = grad_joined.reshape(rows_all, 3 * D)
-    grad_small["rel_bias"] = relative_gradient(shifts[:, :, HD:])
-    sums = column_sums[:, 0].reshape(images, H, 3, HD)
-    time_query = sums[:, :, 0].reshape(images, D)
-    time_value = sums[:, :, 2].reshape(images, D)
-    grad_small["query_bias"] = jnp.sum(time_query, 0)
-    grad_small["value_bias"] = jnp.sum(time_value, 0)
-    grad_first = dot_nt(grad_joined, joined).reshape(images, TOKS, D)
-    joined_grad = reduce_weight(
-        dot_tn(first_in, grad_joined).astype(jnp.bfloat16), sizes, places_now
-    )
-    grad_zero_part, shift_a, scale_a = modulate_back(grad_first, normed_a, inverse_a, 1)
-    grad_zero = grad_one + grad_zero_part
-    grad_small["embed_bias"] = jnp.sum(grad_zero, (0, 1))
-    grad_small["embed_weight"] = jnp.einsum(
-        "ntc,ntd->cd", embed_in.astype(jnp.float32), grad_zero, precision=highest
-    ).reshape(16 * D)
-
+        grad_branch, mixback, joined_rows, log_total, table, spots, list(narrow_sum.sent)
+    )
+    heads_pairs = [(flat(first_in), in_rows(grad_joined)), (flat(grad_branch), in_rows(mixed))]
+    narrow_sum.arrived, heads_first = tie(narrow_sum.arrived, grad_joined)
+    narrow_sum.open_second()
+    narrow_sum.launch()
+    heads_sum.gradient(heads_pairs, list(narrow_sum.sent))
+    sums_a, embed_grads = joined_backward(
+        heads_first,
+        gathered_one,
+        joined_lanes,
+        grad_one,
+        stream_zero,
+        mods,
+        embed_in,
+        [heads_sum.sent],
+    )
+    sums = (
+        column_sums[:, :, 0]
+        .reshape(mp, images, H // mp, 3, HD)
+        .transpose(3, 1, 0, 2, 4)
+        .reshape(3, images, D)
+    )
     mods_grads = jnp.concatenate(
         [
-            shift_a,
-            scale_a,
-            gate_one,
-            shift_b,
-            scale_b,
-            gate_two,
-            shift_c,
-            scale_c,
-            time_query,
-            time_value,
+            sums_a[:, 0],
+            sums_a[:, 1],
+            sums_b[:, 2],
+            sums_b[:, 0],
+            sums_b[:, 1],
+            sums_c[:, 2],
+            sums_c[:, 0],
+            sums_c[:, 1],
+            sums[0],
+            sums[2],
         ],
         1,
     ).astype(jnp.bfloat16)
@@ -600,6 +1142,27 @@
         0,
         tiled=True,
     ).reshape(images_all, mod_width)
+    heads_kept = heads_sum.kept_gradient(heads_pairs, [to_owners])
+    narrow_sum.open_last()
+    narrow_sum.sent, heads_kept = tie(narrow_sum.sent, heads_kept)
+    narrow_sum.launch_last()
+    returned, heads_kept, expand_shard = tie(returned, heads_kept, expand_shard)
+    heads_sum.open_first(heads_kept)
+    heads_sum.sent, returned = tie(heads_sum.sent, returned)
+    heads_sum.launch()
+    grad_small = {
+        "embed_bias": jnp.sum(sums_a[:, 2], 0),
+        "query_bias": jnp.sum(sums[0], 0),
+        "value_bias": jnp.sum(sums[2], 0),
+        "out_bias": jnp.sum(sums_b[:, 3], 0),
+        "fc1_bias": hidden_sums.reshape(FF),
+        "fc2_bias": jnp.sum(sums_c[:, 3], 0),
+        "final_bias": jnp.sum(output_sums[:, 0], 0),
+        "embed_weight": jnp.sum(embed_grads, 0).reshape(16 * D),
+        "final_weight": jnp.sum(final_grads, 0).T.reshape(32 * D),
+        "rel_bias": relative_gradient(shifts[:, :, HD:]),
+    }
+
     is_image = (global_cols < 8 * D)[None, :]
     returned_wide = returned.astype(jnp.float32)
     cond_bias_grad = jnp.sum(returned_wide, 0)
@@ -622,16 +1185,27 @@
         [cond_part[:images_all], cond_part[images_all : images_all + dp] + cond_part[images_all + dp :]],
         0,
     )
-    grad_act = jnp.sum(small_gather(cond_part, mp_axes, mp), 0)
+    grad_act = small_gather(cond_part, mp_axes, mp)
+    grad_act, narrow_sum.arrived = tie(grad_act, narrow_sum.arrived)
+    grad_act = jnp.sum(grad_act, 0)
     _, pullback = jax.vjp(jax.nn.silu, condition)
     grad_cond_own = pullback(grad_act)[0]
     grad_embed_own = split_rows(grad_cond_own[:images_all], grad_cond_own[images_all:])
     timetwo_grad = dot_tn(grad_embed_own, double_rows(hidden_act))
+    grad_cond = small_gather(grad_cond_own, dp_axes, dp)
+    heads_sum.open_second()
+    heads_sum.sent, grad_cond = tie(heads_sum.sent, grad_cond)
+    heads_sum.launch()
     grad_cond = (
-        small_gather(grad_cond_own, dp_axes, dp)
+        grad_cond
         .transpose(1, 0, 2)
         .reshape(images_all + dp, D)
     )
+    vector = jnp.concatenate([grad_small[key_name] for key_name in TOKEN_SMALLS])
+    slice_length = -(-vector.shape[0] // (dp * mp))
+    padded = jnp.pad(vector, (0, slice_length * dp * mp - vector.shape[0]))
+    padded, grad_cond = tie(padded.reshape(dp * mp, slice_length), grad_cond)
+    slice_sum = jnp.sum(lax.all_to_all(padded, all_axes, 0, 0, tiled=True), 0)
     grad_embed = split_rows(grad_cond[:images_all], grad_cond[images_all:])
     bias_two_grad = jnp.sum(grad_embed.astype(jnp.float32), 0)
     grad_hidden_act = dot_nn(grad_embed, time_second_all)
@@ -657,12 +1231,11 @@
         jnp.concatenate([onehot, onehot], 0), jnp.concatenate([label_upper, label_lower], 0)
     )
 
-    vector = jnp.concatenate([grad_small[key_name] for key_name in TOKEN_SMALLS])
-    slice_length = -(-vector.shape[0] // (dp * mp))
-    padded = jnp.pad(vector, (0, slice_length * dp * mp - vector.shape[0]))
-    slice_sum = jnp.sum(
-        lax.all_to_all(padded.reshape(dp * mp, slice_length), all_axes, 0, 0, tiled=True), 0
-    )
+    heads_sum.open_last()
+    heads_sum.launch_last()
+    heads_grad, narrow_grad = (member.result() for member in (heads_sum, narrow_sum))
+    expand_grad = expand_shard.astype(jnp.float32)
+    joined_grad, mixback_grad = (heads_grad[:, :joined_width], heads_grad[:, joined_width:])
     mod_slice = -(-mod_width // dp)
     one_slice = -(-width_mp // dp)
     own_cond = lax.dynamic_slice_in_dim(

time: 1060 us -> 808 us (0.76)
  Pallas kernels: 69.2 us -> 322 us
  local copies, waits for them, and re-layouts: 344 us -> 95.6 us
  matrix products: 200 us -> 13.7 us
  other arithmetic: 136 us -> 79.3 us
    pallas_call x2 -> x11, Pallas kernels: 69.2 us -> 322 us  [the longest x1 60.4 us: feed_forward(): pl.pallas_call(partial(feed_forward_kernel, width), grid=(parts, images),...]
    reshape x9 -> x10, local copies, waits for them, and re-layouts: 94.6 us -> 6.34 us  [the longest x1 1.9 us: per_device(): padded, grad_cond = tie(padded.reshape(dp * mp, slice_length), grad_cond)]
    dynamic_slice x8 -> x2, local copies, waits for them, and re-layouts: 84.5 us -> 2.55 us  [pick(): return lax.dynamic_index_in_dim(values, index, dim, keepdims=False)]
    dot_general x7 -> x2, matrix products: 66.7 us -> 0.62 us  [dot_nt(): lax.dot_general(left, right, (((1,), (1,)), ((), ())), preferred_element_...]
    dot_general x6 -> x1, matrix products: 65.3 us -> 0.35 us  [dot_nn(): return jnp.dot(left, right, preferred_element_type=jnp.float32)]
    unnamed x340 -> x228, local copies, waits for them, and re-layouts: 74.1 us -> 17 us
    dot_general x9 -> x4, matrix products: 60.9 us -> 9.28 us  [dot_tn(): lax.dot_general(left, right, (((0,), (0,)), ((), ())), preferred_element_...]
    all_gather x2, waiting for transfers between devices: 31.2 us -> 81.1 us  [the longest x1 81.1 us: per_device(): lax.all_gather(shard_two.astype(jnp.bfloat16), all_axes)]
  transfers between devices with their start and end apart: 36 -> 29, of which waited for: 16 -> 12; matrix products, arithmetic and copies ran while one was open for 35% -> 18% of each run, Pallas kernels for 3% -> 39%
where the time goes in v1:
time: 808 us; the launch traced here: 797 us
  Pallas kernels  322 us (40%)
  waiting for transfers between devices  185 us (23%)
  local copies, waits for them, and re-layouts  95.6 us (12%)
  other arithmetic  79.3 us (10%)
  starting transfers between devices  73.6 us (9%)
  between operations  27.4 us (3%)
  matrix products  13.7 us (2%)
    all_gather x1, waiting for transfers between devices, per_device(): lax.all_gather(shard_two.astype(jnp.bfloat16), all_axes)  81.1 us
    pallas_call x1, Pallas kernels, feed_forward(): pl.pallas_call(partial(feed_forward_kernel, width), grid=(parts, images),...  60.4 us
    pallas_call x4, Pallas kernels, weight_gradient(): pl.pallas_call(lambda chosen_ref, *refs: kernel(*refs), grid_spec=pltpu.P...  55.3 us
    pallas_call x1, Pallas kernels, feed_backward(): pl.pallas_call(ordered(partial(feed_backward_kernel, width), 8, len(other...  51.8 us
    pallas_call x1, Pallas kernels, attention_backward(): pl.pallas_call(ordered(attention_backward_kernel, 6, len(others)), grid=(...  49.3 us
    pallas_call x1, Pallas kernels, attention_forward(): pl.pallas_call(partial(attention_forward_kernel, width), grid=(parts, ima...  46.1 us
    all_to_all x7, starting transfers between devices, small_gather(): return lax.all_to_all(spread, axes, 0, 0, tiled=True)  42.2 us
    all_to_all x7, waiting for transfers between devices, small_gather(): return lax.all_to_all(spread, axes, 0, 0, tiled=True)  35.6 us
  transfers between devices with their start and end apart: 29, of which 12 were waited for; matrix products, arithmetic and copies ran while one was open for 18% of the time, Pallas kernels for 39%

profile of v1, /device:TPU:0, one launch (start us, length us, event | category | flops | bytes accessed | tf_op | source)
XLA Modules:
  0.0 796.8 jit_solution(6942236741434913755)
XLA Ops:
  13.4 7.3 all-to-all-start
  25.0 3.8 multiply_cosine_fusion
  32.0 2.3 copy.317
  46.6 6.0 all-to-all-start.1
  54.3 10.1 %all-to-all-done.1 = bf16[8,32,288]{2,1,0:T(8,128)(2,1)S(1)} async-done(((bf16[8,32,288]{2,1,0:T(8,128)(2,1)}), bf16[8,32,288]{2,1,0:T(8,128)(2,1)S(1)}, u32[]{:S(2)}, u32[]{:S(2)}) %all-to-all-start.1) | async-done | bytes 147488 | tf_op jit(solution)/shard_map/all_to_all | solution.py:764
  66.5 3.5 all-to-all-start.2
  70.0 3.8 pad_maximum_fusion.table_ref.refs_4_
  73.9 11.2 %all-to-all-done.2 = f32[4,136,144]{2,1,0:T(8,128)S(1)} async-done(((f32[4,136,144]{2,1,0:T(8,128)}), f32[4,136,144]{2,1,0:T(8,128)S(1)}, u32[]{:S(2)}, u32[]{:S(2)}) %all-to-all-start.2) | async-done | bytes 313376 | tf_op jit(solution)/shard_map/all_to_all | solution.py:764
  88.9 3.0 all-to-all-start.3
  95.6 28.8 %all-to-all-done.3 = bf16[32,4,2880]{2,1,0:T(4,128)(2,1)S(1)} async-done(((bf16[32,4,2880]{2,1,0:T(4,128)(2,1)}), bf16[32,4,2880]{2,1,0:T(4,128)(2,1)S(1)}, u32[]{:S(2)}, u32[]{:S(2)}) %all-to-all-start.3) | async-done | bytes 737312 | tf_op jit(solution)/shard_map/all_to_all | solution.py:998
  127.0 5.8 add_convert_fusion.first_ref
  132.7 4.1 slice.352.weight_ref.refs_1_
  136.9 46.1 %attention_forward.1 = (bf16[4,4,256,864]{3,2,1,0:T(8,128)(2,1)}, bf16[4,4,256,288]{3,2,1,0:T(8,128)(2,1)}, f32[4,4,4,256]{3,2,1,0:T(4,128)}) custom-call(bf16[4,256,1152]{2,1,0:T(8,128)(2,1)} %add_convert_fusion.first_ref, bf16[8,4,144,1184]{3,2,1,0:T(8,128)(2,1)} %bitcast.203, f32[4,4,1,864]{3,2,1,0:T(1,128)} %broadcast_in_dim.98.added_ref, ...), custom_call_target="tpu_custom_call" | custom-call | flops 10301210624 | bytes 30000000 | tf_op jit(solution)/shard_map/attention_forward/pallas_call | solution.py:202
  183.0 11.6 %mixback_forward.1 = (bf16[4,256,1152]{2,1,0:T(8,128)(2,1)}, f32[4,256,1152]{2,1,0:T(8,128)}, bf16[4,256,1152]{2,1,0:T(8,128)(2,1)}) custom-call(bf16[4,4,256,288]{3,2,1,0:T(8,128)(2,1)} %get-tuple-element.79.mixed_ref, bf16[8,4,144,288]{3,2,1,0:T(8,128)(2,1)} %slice.352.weight_ref.refs_1_, f32[4,256,1152]{2,1,0:T(8,128)} %copy-done, ...), custom_call_target="tpu_custom_call" | custom-call | flops 2717908992 | bytes 16515072 | tf_op jit(solution)/shard_map/mixback_forward/pallas_call | solution.py:322
  195.6 4.2 all-to-all-start.4
  200.0 81.1 %all-gather.5.cloned.1.call-done = bf16[32,144,2304]{2,1,0:T(8,128)(2,1)} async-done(((bf16[1,144,2304]{2,1,0:T(8,128)(2,1)}), bf16[32,144,2304]{2,1,0:T(8,128)(2,1)}) %all-gather.5.cloned.1.call-update) | async-done | bytes 21233680 | tf_op jit(solution)/shard_map/all_gather | solution.py:943
  281.8 60.4 %feed_forward.1 = (bf16[4,4,256,1152]{3,2,1,0:T(8,128)(2,1)}, bf16[4,4,256,1152]{3,2,1,0:T(8,128)(2,1)}, f32[4,256,1152]{2,1,0:T(8,128)}, bf16[4,256,1152]{2,1,0...) custom-call(bf16[4,256,1152]{2,1,0:T(8,128)(2,1)} %get-tuple-element.82.second_ref, ...), custom_call_target="tpu_custom_call" | custom-call | flops 21743271936 | bytes 60000000 | tf_op jit(solution)/shard_map/feed_forward/pallas_call | solution.py:431
  342.2 12.5 %weight_gradient.4.refs_8_ = bf16[2,1152,1152]{2,1,0:T(8,128)(2,1)} custom-call(s32[1]{0:T(128)S(6)} %sub.183.chosen_ref, bf16[1024,1152]{1,0:T(8,128)(2,1)} %bitcast.214, bf16[4,1024,1152]{2,1,0:T(8,128)(2,1)} %bitcast.207), custom_call_target="tpu_custom_call" | custom-call | flops 5435817984 | bytes 7077888 | tf_op jit(solution)/shard_map/weight_gradient/pallas_call | solution.py:677
  360.1 51.8 %feed_backward.1 = (bf16[4,4,256,1152]{3,2,1,0:T(8,128)(2,1)}, f32[4,1,1152]{2,1,0:T(1,128)}, f32[4,256,1152]{2,1,0:T(8,128)}, bf16[4,256,1152]{2,1,0:T(8,128)(2,1)}, f32[4,4,1152]{2,1,0:T(4,128)}) custom-call(bf16[4,256,1152]{2,1,0:T(8,128)(2,1)} %get-tuple-element.85.refs_0_, bf16[8,4,144,2304]{3,2,1,0:T(8,128)(2,1)} %bitcast.245, ...), custom_call_target="tpu_custom_call" | custom-call | flops 21743271936 | bytes 60000000 | tf_op jit(solution)/shard_map/feed_backward/pallas_call | solution.py:534
  411.9 20.9 %whole_gradient.1 = bf16[8,4,144,1152]{3,2,1,0:T(8,128)(2,1)} custom-call(bf16[1024,1152]{1,0:T(8,128)(2,1)} %bitcast.247, bf16[4,1024,1152]{2,1,0:T(8,128)(2,1)} %bitcast.248), custom_call_target="tpu_custom_call" | custom-call | flops 10871635968 | bytes 11796480 | tf_op jit(solution)/shard_map/whole_gradient/pallas_call | solution.py:709
  436.7 13.5 %weight_gradient.5 = bf16[2,1152,1152]{2,1,0:T(8,128)(2,1)} custom-call(s32[1]{0:T(128)} %bitcast.chosen_ref, bf16[1024,1152]{1,0:T(8,128)(2,1)} %bitcast.215, bf16[4,1024,1152]{2,1,0:T(8,128)(2,1)} %bitcast.208, bf16[2,1152,1152]{2,1,0:T(8,128)(2,1)} %collective-permute-done.refs_2_, bf16[32,144,1152]{2,1,0:T(8,128)(2,1)} %bitcast.195), custom_call_target="tpu_custom_call" | custom-call | flops 5435817984 | bytes 7077888 | tf_op jit(solution)/shard_map/weight_gradient/pallas_call | solution.py:677
  450.2 3.2 fusion.106
  460.1 49.3 %attention_backward.1 = (bf16[4,4,256,864]{3,2,1,0:T(8,128)(2,1)}, f32[4,4,8,864]{3,2,1,0:T(8,128)}, f32[16,256,104]{2,1,0:T(8,128)}) custom-call(bf16[4,256,1152]{2,1,0:T(8,128)(2,1)} %get-tuple-element.91.refs_0_, bf16[8,4,144,288]{3,2,1,0:T(8,128)(2,1)} %slice.352.weight_ref.refs_1_, bf16[4,4,256,864]{3,2,1,0:T(8,128)(2,1)} %get-tuple-element.92.refs_2_, ...), custom_call_target="tpu_custom_call" | custom-call | flops 8086618112 | bytes 50000000 | tf_op jit(solution)/shard_map/attention_backward/pallas_call | solution.py:275
  511.6 3.5 slice.304
  517.3 2.5 bitcast_reduce_fusion
  526.5 14.4 %weight_gradient.6.refs_6_ = bf16[2,1152,1152]{2,1,0:T(8,128)(2,1)} custom-call(s32[1]{0:T(128)S(6)} %sub.183.chosen_ref, bf16[1024,1152]{1,0:T(8,128)(2,1)} %bitcast.200, bf16[1024,1152]{1,0:T(8,128)(2,1)} %bitcast.205, bf16[4,1024,864]{2,1,0:T(8,128)(2,1)} %bitcast.192, bf16[4,1024,288]{2,1,0:T(8,128)(2,1)} %bitcast.196, ...), custom_call_target="tpu_custom_call" | custom-call | flops 5435817984 | bytes 7077888 | tf_op jit(solution)/shard_map/weight_gradient/pallas_call | solution.py:677
  540.9 26.7 %joined_backward.1 = (f32[4,4,1152]{2,1,0:T(4,128)}, f32[4,16,1152]{2,1,0:T(8,128)}) custom-call(bf16[4,4,256,864]{3,2,1,0:T(8,128)(2,1)} %get-tuple-element.95.refs_0_, bf16[8,4,144,1184]{3,2,1,0:T(8,128)(2,1)} %bitcast.204, f32[4,256,1152]{2,1,0:T(8,128)} %get-tuple-element.96.refs_2_, f32[4,256,1152]{2,1,0:T(8,128)} %copy-done, f32[4,8,1152]{2,1,0:T(8,128)} %bitcast.223, ...), custom_call_target="tpu_custom_call" | custom-call | flops 8153726976 | bytes 30000000 | tf_op jit(solution)/shard_map/joined_backward/pallas_call | solution.py:611
  570.1 3.8 all-to-all-start.5
  579.0 9.6 %concatenate.143 = f32[66688]{0:T(1024)} concatenate(f32[1152]{0:T(1024)S(1)} %slice_reduce_fusion.3, f32[1152]{0:T(1024)S(1)} %reduce_sum.316, f32[1152]{0:T(1024)S(1)} %reduce_sum.318, f32[1152]{0:T(1024)S(1)} %slice_reduce_fusion.2, f32[4608]{0:T(1024)S(1)} %reshape.564, f32[1152]{0:T(1024)S(1)} %copy-done.88, f32[32]{0:T(128)} %slice_reduce_fusion.10, f32[18432]{0:T(1024)S(1)} %reshape.565, ...), dimensions={0} | concatenate | bytes 533504 | tf_op jit(solution)/shard_map/concatenate | solution.py:1204
  597.0 14.9 %weight_gradient.7 = bf16[2,1152,1152]{2,1,0:T(8,128)(2,1)} custom-call(s32[1]{0:T(128)} %bitcast.chosen_ref, bf16[1024,1152]{1,0:T(8,128)(2,1)} %bitcast.201, bf16[1024,1152]{1,0:T(8,128)(2,1)} %bitcast.206, bf16[4,1024,864]{2,1,0:T(8,128)(2,1)} %bitcast.193, bf16[4,1024,288]{2,1,0:T(8,128)(2,1)} %bitcast.197, ...), custom_call_target="tpu_custom_call" | custom-call | flops 5435817984 | bytes 7077888 | tf_op jit(solution)/shard_map/weight_gradient/pallas_call | solution.py:677
  611.9 3.7 collective-permute-start.10
  616.8 3.0 fusion.105
  626.4 4.2 all-to-all-start.6
  636.0 3.4 multiply_reduce_fusion.1
  639.4 5.3 collective-permute-done.9
  647.1 5.2 all-to-all-start.7
  652.3 2.5 multiply_reduce_fusion.6
  654.8 2.9 multiply_reduce_fusion.3
  657.7 12.7 %collective-permute-done.7 = bf16[2,2,144,1152]{3,2,1,0:T(8,128)(2,1)} collective-permute-done((bf16[2,2,144,1152]{3,2,1,0:T(8,128)(2,1)}, bf16[2,2,144,1152]{3,2,1,0:T(8,128)(2,1)}, u32[]{:S(2)}, u32[]{:S(2)}) %collective-permute-start.7) | collective-permute-done | bytes 1327136 | tf_op jit(solution)/shard_map/ppermute | solution.py:776
  685.9 3.7 all-to-all-start.8
  694.0 5.5 collective-permute-done.12
  703.7 2.8 collective-permute-start.13
  711.3 5.1 collective-permute-done.13
  716.4 9.9 %collective-permute-done.14 = bf16[144,1152]{1,0:T(8,128)(2,1)S(1)} collective-permute-done((bf16[144,1152]{1,0:T(8,128)(2,1)S(1)}, bf16[144,1152]{1,0:T(8,128)(2,1)S(1)}, u32[]{:S(2)}, u32[]{:S(2)}) %collective-permute-start.14) | collective-permute-done | bytes 331808 | tf_op jit(solution)/shard_map/ppermute | solution.py:844
  735.7 11.8 %all-to-all-start.9 = ((f32[32,1,2482]{2,1,0:T(1,128)}), f32[32,1,2482]{2,1,0:T(1,128)S(1)}, u32[]{:S(2)}, u32[]{:S(2)}) async-start(f32[32,1,2482]{2,1,0:T(1,128)} %broadcast_in_dim.199), calls=%async_computation.10 | async-start | bytes 655360 | tf_op jit(solution)/shard_map/all_to_all | solution.py:764
  747.5 12.0 %all-to-all-done.9 = f32[32,1,2482]{2,1,0:T(1,128)S(1)} async-done(((f32[32,1,2482]{2,1,0:T(1,128)}), f32[32,1,2482]{2,1,0:T(1,128)S(1)}, u32[]{:S(2)}, u32[]{:S(2)}) %all-to-all-start.9) | async-done | bytes 317728 | tf_op jit(solution)/shard_map/all_to_all | solution.py:764
  777.0 2.4 multiply_subtract_fusion.1
  781.3 3.2 multiply_subtract_fusion
  (500 shorter events, 150.3 us)
Async XLA Ops:
  7.2 125.5 %all-gather.3.cloned.1.call-start = ((), (), s32[]{:S(2)}) async-start(), calls=%async_computation.11 | async-start | bytes 12165120 | tf_op jit(solution)/shard_map/all_gather | solution.py:941
  10.3 270.9 %all-gather.5.cloned.1.call-start = ((), (), s32[]{:S(2)}) async-start(), calls=%async_computation.12 | async-start | bytes 21897216 | tf_op jit(solution)/shard_map/all_gather | solution.py:943
  13.4 32.5 %all-to-all-start = ((f32[8,1,50]{2,1,0:T(1,128)}), f32[8,1,50]{2,1,0:T(1,128)S(1)}, u32[]{:S(2)}, u32[]{:S(2)}) async-start(f32[8,1,50]{2,1,0:T(1,128)} %broadcast_in_dim.83), calls=%async_computation | async-start | bytes 8192 | tf_op jit(solution)/shard_map/all_to_all | solution.py:764
  31.5 33.8 %copy-start.39 = (bf16[144,288]{1,0:T(8,128)(2,1)}, bf16[144,288]{1,0:T(8,128)(2,1)S(1)}, u32[]{:S(2)}) copy-start(bf16[144,288]{1,0:T(8,128)(2,1)S(1)} %convert_element_type.297) | copy-start | bytes 248836
  46.6 17.8 %all-to-all-start.1 = ((bf16[8,32,288]{2,1,0:T(8,128)(2,1)}), bf16[8,32,288]{2,1,0:T(8,128)(2,1)S(1)}, u32[]{:S(2)}, u32[]{:S(2)}) async-start(bf16[8,32,288]{2,1,0:T(8,128)(2,1)} %broadcast_in_dim.88), calls=%async_computation.1 | async-start | bytes 393216 | tf_op jit(solution)/shard_map/all_to_all | solution.py:764
  66.5 18.6 %all-to-all-start.2 = ((f32[4,136,144]{2,1,0:T(8,128)}), f32[4,136,144]{2,1,0:T(8,128)S(1)}, u32[]{:S(2)}, u32[]{:S(2)}) async-start(f32[4,136,144]{2,1,0:T(8,128)} %broadcast_in_dim.94), calls=%async_computation.2 | async-start | bytes 1114112 | tf_op jit(solution)/shard_map/all_to_all | solution.py:764
  70.0 17.6 %copy-start.79 = (pred[2880]{0:T(1024)(128)(4,1)}, pred[2880]{0:T(1024)(128)(4,1)S(1)}, u32[]{:S(2)}) copy-start(pred[2880]{0:T(1024)(128)(4,1)S(1)} %add_compare_fusion) | copy-start | bytes 8644
  70.0 15.8 %copy-start.94 = (f32[144]{0:T(256)S(1)}, f32[144]{0:T(256)}, u32[]{:S(2)}) copy-start(f32[144]{0:T(256)} %dynamic_slice.107) | copy-start | bytes 1732
  70.0 16.8 %copy-start.1 = (f32[144,2880]{1,0:T(8,128)S(1)}, f32[144,2880]{1,0:T(8,128)}, u32[]{:S(2)}) copy-start(f32[144,2880]{1,0:T(8,128)} %param.59) | copy-start | bytes 4976644
  86.8 273.3 %copy-start.58 = (bf16[136,144]{1,0:T(8,128)(2,1)}, bf16[136,144]{1,0:T(8,128)(2,1)S(1)}, u32[]{:S(2)}) copy-start(bf16[136,144]{1,0:T(8,128)(2,1)S(1)} %multiply_convert_fusion.1) | copy-start | bytes 117508
  88.9 35.5 %all-to-all-start.3 = ((bf16[32,4,2880]{2,1,0:T(4,128)(2,1)}), bf16[32,4,2880]{2,1,0:T(4,128)(2,1)S(1)}, u32[]{:S(2)}, u32[]{:S(2)}) async-start(bf16[32,4,2880]{2,1,0:T(4,128)(2,1)} %select_convert_fusion), calls=%async_computation.3 | async-start | bytes 1507328 | tf_op jit(solution)/shard_map/all_to_all | solution.py:998
  95.6 29.5 %copy-start.89 = (f32[1152]{0:T(1024)S(1)}, f32[1152]{0:T(1024)}, u32[]{:S(2)}) copy-start(f32[1152]{0:T(1024)} %get-tuple-element.191) | copy-start | bytes 13828
  95.6 29.5 %copy-start.90 = (f32[1152]{0:T(1024)S(1)}, f32[1152]{0:T(1024)}, u32[]{:S(2)}) copy-start(f32[1152]{0:T(1024)} %get-tuple-element.192) | copy-start | bytes 13828
  95.6 29.7 %copy-start.103 = (f32[3]{0:T(128)S(1)}, f32[3]{0:T(128)}, u32[]{:S(2)}) copy-start(f32[3]{0:T(128)} %pad.51.clone) | copy-start | bytes 40
  195.6 146.6 %all-to-all-start.4 = ((bf16[8,144,288]{2,1,0:T(8,128)(2,1)}), bf16[8,144,288]{2,1,0:T(8,128)(2,1)S(1)}, u32[]{:S(2)}, u32[]{:S(2)}) async-start(bf16[8,144,288]{2,1,0:T(8,128)(2,1)} %broadcast_in_dim.104), calls=%async_computation.4 | async-start | bytes 1769472 | tf_op jit(solution)/shard_map/all_to_all | solution.py:764
  199.8 417.0 %reduce-scatter.2.cloned.1.call-start = ((), (), s32[]{:S(2)}) async-start(), calls=%async_computation.13 | async-start | bytes 10948608 | tf_op jit(solution)/shard_map/reduce_scatter | solution.py:1093
  342.2 13.6 %copy-start.72 = (bf16[136,128]{1,0:T(8,128)(2,1)S(1)}, bf16[136,128]{1,0:T(8,128)(2,1)}, u32[]{:S(2)}) copy-start(bf16[136,128]{1,0:T(8,128)(2,1)} %copy-done.71) | copy-start | bytes 104452
  342.2 13.6 %copy-start.74 = (bf16[136,128]{1,0:T(8,128)(2,1)S(1)}, bf16[136,128]{1,0:T(8,128)(2,1)}, u32[]{:S(2)}) copy-start(bf16[136,128]{1,0:T(8,128)(2,1)} %copy-done.73) | copy-start | bytes 104452
  342.2 15.7 %copy-start.99 = (f32[128]{0:T(128)S(1)}, f32[128]{0:T(128)}, u32[]{:S(2)}) copy-start(f32[128]{0:T(128)} %copy-done.98) | copy-start | bytes 1540
  354.7 82.0 %collective-permute-start = (bf16[2,1152,1152]{2,1,0:T(8,128)(2,1)}, bf16[2,1152,1152]{2,1,0:T(8,128)(2,1)}, u32[]{:S(2)}, u32[]{:S(2)}) collective-permute-start(bf16[2,1152,1152]{2,1,0:T(8,128)(2,1)} %weight_gradient.4.refs_8_), channel_id=1, source_target_pairs={{0,1},{1,0},{2,3},{3,2},{4,5},{5,4},{6,7},{7,6},{8,9},{9,8},{10,11... | collective-permute-start | bytes 15925256 | tf_op jit(solution)/shard_map/ppermute | solution.py:776
  456.0 64.8 %collective-permute-start.1 = (bf16[2,2,144,1152]{3,2,0,1:T(8,128)(2,1)}, bf16[2,2,144,1152]{3,2,0,1:T(8,128)(2,1)}, u32[]{:S(2)}, u32[]{:S(2)}) collective-permute-start(bf16[2,2,144,1152]{3,2,0,1:T(8,128)(2,1)} %bitcast.187), channel_id=1, source_target_pairs={{0,2},{2,0},{1,3},{3,1},{4,6},{6,4},{5,7},{7,5},{8,10},{10,8},{9,1... | collective-permute-start | bytes 3981320 | tf_op jit(solution)/shard_map/ppermute | solution.py:776
  458.8 62.1 %collective-permute-start.2 = (bf16[2,2,144,1152]{3,2,1,0:T(8,128)(2,1)}, bf16[2,2,144,1152]{3,2,1,0:T(8,128)(2,1)}, u32[]{:S(2)}, u32[]{:S(2)}) collective-permute-start(bf16[2,2,144,1152]{3,2,1,0:T(8,128)(2,1)} %dynamic-slice_bitcast_fusion.1.refs_7_), channel_id=1, source_target_pairs={{0,4},{4,0},{1,5},{5,1},{2,6},{6,2},{3,7},{7,3},{8,12},{12,8},{9,1... | collective-permute-start | bytes 3981320 | tf_op jit(solution)/shard_map/ppermute | solution.py:776
  522.7 67.9 %collective-permute-start.4 = (bf16[2,144,1152]{2,1,0:T(8,128)(2,1)S(1)}, bf16[2,144,1152]{2,1,0:T(8,128)(2,1)}, u32[]{:S(2)}, u32[]{:S(2)}) collective-permute-start(bf16[2,144,1152]{2,1,0:T(8,128)(2,1)S(1)} %dynamic-slice_bitcast_fusion.4.refs_5_), channel_id=1, source_target_pairs={{0,2},{2,0},{1,3},{3,1},{4,6},{6,4},{5,7},{7,5},{8,10},{10,8},{9,1... | collective-permute-start | bytes 1990664 | tf_op jit(solution)/shard_map/ppermute | solution.py:776
  525.9 65.9 %collective-permute-start.3 = (bf16[2,144,1152]{2,1,0:T(8,128)(2,1)}, bf16[2,144,1152]{2,1,0:T(8,128)(2,1)}, u32[]{:S(2)}, u32[]{:S(2)}) collective-permute-start(bf16[2,144,1152]{2,1,0:T(8,128)(2,1)} %dynamic-slice_bitcast_fusion.5.refs_4_), channel_id=1, source_target_pairs={{0,4},{4,0},{1,5},{5,1},{2,6},{6,2},{3,7},{7,3},{8,12},{12,8},{9,1... | collective-permute-start | bytes 1990664 | tf_op jit(solution)/shard_map/ppermute | solution.py:776
  540.9 56.1 %collective-permute-start.5 = (bf16[2,1152,1152]{2,1,0:T(8,128)(2,1)}, bf16[2,1152,1152]{2,1,0:T(8,128)(2,1)}, u32[]{:S(2)}, u32[]{:S(2)}) collective-permute-start(bf16[2,1152,1152]{2,1,0:T(8,128)(2,1)} %weight_gradient.6.refs_6_), channel_id=1, source_target_pairs={{0,1},{1,0},{2,3},{3,2},{4,5},{5,4},{6,7},{7,6},{8,9},{9,8},{10,11... | collective-permute-start | bytes 15925256 | tf_op jit(solution)/shard_map/ppermute | solution.py:776
  540.9 27.8 %copy-start.87 = (bf16[4,1152]{1,0:T(4,128)(2,1)S(1)}, bf16[4,1152]{1,0:T(4,128)(2,1)}, u32[]{:S(2)}) copy-start(bf16[4,1152]{1,0:T(4,128)(2,1)} %squeeze.125) | copy-start | bytes 27652
  569.0 19.6 %copy-start.46 = (bf16[4,4,2880]{2,0,1:T(4,128)(2,1)}, bf16[4,4,2880]{2,0,1:T(4,128)(2,1)S(1)}, u32[]{:S(2)}) copy-start(bf16[4,4,2880]{2,0,1:T(4,128)(2,1)S(1)} %copy.395) | copy-start | bytes 276484
  570.1 20.5 %copy-start.9 = (bf16[2,2,144,1152]{3,2,1,0:T(8,128)(2,1)S(1)}, bf16[2,2,144,1152]{3,2,1,0:T(8,128)(2,1)}, u32[]{:S(2)}) copy-start(bf16[2,2,144,1152]{3,2,1,0:T(8,128)(2,1)} %copy-done.8) | copy-start | bytes 3981316
  570.1 25.3 %all-to-all-start.5 = ((bf16[32,4,2880]{2,1,0:T(4,128)(2,1)}), bf16[32,4,2880]{2,1,0:T(4,128)(2,1)}, u32[]{:S(2)}, u32[]{:S(2)}) async-start(bf16[32,4,2880]{2,1,0:T(4,128)(2,1)} %bitcast.46), calls=%async_computation.5 | async-start | bytes 1507328 | tf_op jit(solution)/shard_map/all_to_all | solution.py:1136
  611.9 27.5 %collective-permute-start.10 = (bf16[144,1152]{1,0:T(8,128)(2,1)}, bf16[144,1152]{1,0:T(8,128)(2,1)}, u32[]{:S(2)}, u32[]{:S(2)}) collective-permute-start(bf16[144,1152]{1,0:T(8,128)(2,1)} %get-tuple-element.116), channel_id=1, source_target_pairs={{0,24},{8,0},{16,8},{24,16},{1,25},{9,1},{17,9},{25,17},{2,26},{10... | collective-permute-start | bytes 995336 | tf_op jit(solution)/shard_map/ppermute | solution.py:844
  615.7 23.8 %collective-permute-start.8 = (bf16[144,1152]{1,0:T(8,128)(2,1)}, bf16[144,1152]{1,0:T(8,128)(2,1)}, u32[]{:S(2)}, u32[]{:S(2)}) collective-permute-start(bf16[144,1152]{1,0:T(8,128)(2,1)} %get-tuple-element.114), channel_id=1, source_target_pairs={{0,8},{8,16},{16,24},{24,0},{1,9},{9,17},{17,25},{25,1},{2,10},{10... | collective-permute-start | bytes 995336 | tf_op jit(solution)/shard_map/ppermute | solution.py:844
  615.7 29.1 %collective-permute-start.9 = (bf16[144,1152]{1,0:T(8,128)(2,1)}, bf16[144,1152]{1,0:T(8,128)(2,1)}, u32[]{:S(2)}, u32[]{:S(2)}) collective-permute-start(bf16[144,1152]{1,0:T(8,128)(2,1)} %get-tuple-element.115), channel_id=1, source_target_pairs={{0,16},{8,24},{16,0},{24,8},{1,17},{9,25},{17,1},{25,9},{2,18},{10... | collective-permute-start | bytes 995336 | tf_op jit(solution)/shard_map/ppermute | solution.py:844
  626.4 18.3 %all-to-all-start.6 = ((f32[4,136,144]{2,1,0:T(8,128)}), f32[4,136,144]{2,1,0:T(8,128)}, u32[]{:S(2)}, u32[]{:S(2)}) async-start(f32[4,136,144]{2,1,0:T(8,128)} %broadcast_in_dim.195), calls=%async_computation.7 | async-start | bytes 1114112 | tf_op jit(solution)/shard_map/all_to_all | solution.py:764
  630.6 39.8 %collective-permute-start.7 = (bf16[2,2,144,1152]{3,2,1,0:T(8,128)(2,1)}, bf16[2,2,144,1152]{3,2,1,0:T(8,128)(2,1)}, u32[]{:S(2)}, u32[]{:S(2)}) collective-permute-start(bf16[2,2,144,1152]{3,2,1,0:T(8,128)(2,1)} %dynamic-slice_bitcast_fusion), channel_id=1, source_target_pairs={{0,4},{4,0},{1,5},{5,1},{2,6},{6,2},{3,7},{7,3},{8,12},{12,8},{9,1... | collective-permute-start | bytes 3981320 | tf_op jit(solution)/shard_map/ppermute | solution.py:776
  632.2 40.9 %collective-permute-start.6 = (bf16[2,2,144,1152]{3,2,0,1:T(8,128)(2,1)}, bf16[2,2,144,1152]{3,2,0,1:T(8,128)(2,1)}, u32[]{:S(2)}, u32[]{:S(2)}) collective-permute-start(bf16[2,2,144,1152]{3,2,0,1:T(8,128)(2,1)} %bitcast.224), channel_id=1, source_target_pairs={{0,2},{2,0},{1,3},{3,1},{4,6},{6,4},{5,7},{7,5},{8,10},{10,8},{9,1... | collective-permute-start | bytes 3981320 | tf_op jit(solution)/shard_map/ppermute | solution.py:776
  647.1 31.8 %all-to-all-start.7 = ((f32[8,136,144]{2,1,0:T(8,128)}), f32[8,136,144]{2,1,0:T(8,128)}, u32[]{:S(2)}, u32[]{:S(2)}) async-start(f32[8,136,144]{2,1,0:T(8,128)} %broadcast_in_dim.196), calls=%async_computation.8 | async-start | bytes 2228224 | tf_op jit(solution)/shard_map/all_to_all | solution.py:764
  657.7 15.3 %copy-start.10 = (bf16[1,2,2,144,1152]{4,3,2,1,0:T(8,128)(2,1)S(1)}, bf16[1,2,2,144,1152]{4,3,2,1,0:T(8,128)(2,1)}, u32[]{:S(2)}) copy-start(bf16[1,2,2,144,1152]{4,3,2,1,0:T(8,128)(2,1)} %get-tuple-element.179) | copy-start | bytes 3981316
  682.1 17.4 %collective-permute-start.12 = (bf16[2,144,1152]{2,1,0:T(8,128)(2,1)}, bf16[2,144,1152]{2,1,0:T(8,128)(2,1)}, u32[]{:S(2)}, u32[]{:S(2)}) collective-permute-start(bf16[2,144,1152]{2,1,0:T(8,128)(2,1)} %dynamic-slice_bitcast_fusion.2), channel_id=1, source_target_pairs={{0,2},{2,0},{1,3},{3,1},{4,6},{6,4},{5,7},{7,5},{8,10},{10,8},{9,1... | collective-permute-start | bytes 1990664 | tf_op jit(solution)/shard_map/ppermute | solution.py:776
  683.8 18.0 %collective-permute-start.11 = (bf16[2,144,1152]{2,1,0:T(8,128)(2,1)}, bf16[2,144,1152]{2,1,0:T(8,128)(2,1)}, u32[]{:S(2)}, u32[]{:S(2)}) collective-permute-start(bf16[2,144,1152]{2,1,0:T(8,128)(2,1)} %dynamic-slice_bitcast_fusion.3), channel_id=1, source_target_pairs={{0,4},{4,0},{1,5},{5,1},{2,6},{6,2},{3,7},{7,3},{8,12},{12,8},{9,1... | collective-permute-start | bytes 1990664 | tf_op jit(solution)/shard_map/ppermute | solution.py:776
  685.9 24.5 %all-to-all-start.8 = ((f32[32,1,2084]{2,1,0:T(1,128)}), f32[32,1,2084]{2,1,0:T(1,128)S(1)}, u32[]{:S(2)}, u32[]{:S(2)}) async-start(f32[32,1,2084]{2,1,0:T(1,128)} %all_to_all.48), calls=%async_computation.9 | async-start | bytes 557056 | tf_op jit(solution)/shard_map/all_to_all | solution.py:1208
  703.7 12.7 %collective-permute-start.13 = (bf16[144,1152]{1,0:T(8,128)(2,1)S(1)}, bf16[144,1152]{1,0:T(8,128)(2,1)S(1)}, u32[]{:S(2)}, u32[]{:S(2)}) collective-permute-start(bf16[144,1152]{1,0:T(8,128)(2,1)S(1)} %get-tuple-element.183), channel_id=1, source_target_pairs={{0,8},{8,16},{16,24},{24,0},{1,9},{9,17},{17,25},{25,1},{2,10},{10... | collective-permute-start | bytes 995336 | tf_op jit(solution)/shard_map/ppermute | solution.py:844
  706.5 19.7 %collective-permute-start.14 = (bf16[144,1152]{1,0:T(8,128)(2,1)S(1)}, bf16[144,1152]{1,0:T(8,128)(2,1)S(1)}, u32[]{:S(2)}, u32[]{:S(2)}) collective-permute-start(bf16[144,1152]{1,0:T(8,128)(2,1)S(1)} %get-tuple-element.184), channel_id=1, source_target_pairs={{0,16},{8,24},{16,0},{24,8},{1,17},{9,25},{17,1},{25,9},{2,18},{10... | collective-permute-start | bytes 995336 | tf_op jit(solution)/shard_map/ppermute | solution.py:844
  706.8 19.5 %collective-permute-start.15 = (bf16[144,1152]{1,0:T(8,128)(2,1)S(1)}, bf16[144,1152]{1,0:T(8,128)(2,1)}, u32[]{:S(2)}, u32[]{:S(2)}) collective-permute-start(bf16[144,1152]{1,0:T(8,128)(2,1)S(1)} %get-tuple-element.185), channel_id=1, source_target_pairs={{0,24},{8,0},{16,8},{24,16},{1,25},{9,1},{17,9},{25,17},{2,26},{10... | collective-permute-start | bytes 995336 | tf_op jit(solution)/shard_map/ppermute | solution.py:844
  735.7 34.4 %copy-start.24 = (f32[144,1152]{1,0:T(8,128)S(1)}, f32[144,1152]{1,0:T(8,128)}, u32[]{:S(2)}) copy-start(f32[144,1152]{1,0:T(8,128)} %param.47) | copy-start | bytes 1990660
  735.7 34.4 %copy-start.33 = (bf16[1,144,1152]{2,1,0:T(8,128)(2,1)S(1)}, bf16[1,144,1152]{2,1,0:T(8,128)(2,1)}, u32[]{:S(2)}) copy-start(bf16[1,144,1152]{2,1,0:T(8,128)(2,1)} %reduce-scatter.2.cloned.1.call-done) | copy-start | bytes 995332
  735.7 34.4 %copy-start.50 = (f32[144,1152]{1,0:T(8,128)S(1)}, f32[144,1152]{1,0:T(8,128)}, u32[]{:S(2)}) copy-start(f32[144,1152]{1,0:T(8,128)} %param.49) | copy-start | bytes 1990660
  735.7 34.4 %copy-start.51 = (f32[144,1152]{1,0:T(8,128)S(1)}, f32[144,1152]{1,0:T(8,128)}, u32[]{:S(2)}) copy-start(f32[144,1152]{1,0:T(8,128)} %param.48) | copy-start | bytes 1990660
  735.7 23.8 %all-to-all-start.9 = ((f32[32,1,2482]{2,1,0:T(1,128)}), f32[32,1,2482]{2,1,0:T(1,128)S(1)}, u32[]{:S(2)}, u32[]{:S(2)}) async-start(f32[32,1,2482]{2,1,0:T(1,128)} %broadcast_in_dim.199), calls=%async_computation.10 | async-start | bytes 655360 | tf_op jit(solution)/shard_map/all_to_all | solution.py:764
  (90 other events, 398.8 us)
Sparse Core Ops, SparseCore 0:
  11.5 115.7 all-gather.2
  130.8 150.3 all-gather.4
  433.0 142.9 reduce-scatter.1

commit v2 on v1

--- a/solution.py
+++ b/solution.py
@@ -104,6 +104,8 @@
 SCALE = 1.0 / math.sqrt(HD)
 JOIN = 3 * HD
 ROOT = math.sqrt(2.0 / math.pi)
+CUBE = 0.044715
+SCALE_TWO = SCALE / math.log(2.0)
 
 
 def dot_nn(left, right):
@@ -186,13 +188,15 @@
         query = joined_ref[0, 0, :, base : base + HD]
         keys = joined_ref[0, 0, :, base + HD : base + 2 * HD]
         values = joined_ref[0, 0, :, base + 2 * HD : base + 3 * HD]
-        scores = (dot_nt(keys, query) + dot_nt(spots_ref[...], table_ref[head])) * SCALE
+        scores = SCALE_TWO * dot_nt(
+            jnp.concatenate([keys, spots_ref[...]], 1), jnp.concatenate([query, table_ref[head]], 1)
+        )
         largest = jnp.max(scores, 0, keepdims=True)
-        grown = jnp.exp(scores - largest)
+        grown = jnp.exp2(scores - largest)
         total = jnp.sum(grown, 0, keepdims=True)
         prob = (grown * (1.0 / total)).astype(jnp.bfloat16)
         mixed_ref[0, 0, :, head * HD : (head + 1) * HD] = dot_tn(prob, values).astype(jnp.bfloat16)
-        total_ref[0, 0, head : head + 1, :] = largest + jnp.log(total)
+        total_ref[0, 0, head : head + 1, :] = largest + jnp.log2(total)
 
 
 def attention_forward(first_in, weights, lanes, width, added, table, spots):
@@ -204,7 +208,7 @@
         grid=(parts, images),
         in_specs=[
             pl.BlockSpec((1, TOKS, D), lambda m, i: (i, 0, 0)),
-            weight_spec(weights, lanes, 0),
+            weight_spec(weights, lanes, 1),
             pl.BlockSpec((1, 1, 1, width), lambda m, i: (m, i, 0, 0)),
             pl.BlockSpec((heads, TOKS, 4 * GRID), lambda m, i: (m, 0, 0)),
             pl.BlockSpec((TOKS, 4 * GRID), lambda m, i: (0, 0)),
@@ -252,15 +256,15 @@
         keys = joined_ref[0, 0, :, base + HD : base + 2 * HD]
         values = joined_ref[0, 0, :, base + 2 * HD : base + 3 * HD]
         mixed_grad = mixed_grad_ref[:, head * HD : (head + 1) * HD]
-        scores = (dot_nt(keys, query) + dot_nt(spots_ref[...], table_ref[head])) * SCALE
-        exact = jnp.exp(scores - total_ref[0, 0, head : head + 1, :])
+        wide = jnp.concatenate([keys, spots_ref[...]], 1)
+        scores = SCALE_TWO * dot_nt(wide, jnp.concatenate([query, table_ref[head]], 1))
+        exact = jnp.exp2(scores - total_ref[0, 0, head : head + 1, :])
         value_grad = dot_nn(exact.astype(jnp.bfloat16), mixed_grad)
         prob_grad = dot_nt(values, mixed_grad)
         shared = jnp.sum(exact * prob_grad, 0, keepdims=True)
         score_grad = (exact * (prob_grad - shared)).astype(jnp.bfloat16)
         key_grad = dot_nn(score_grad, query) * SCALE
-        wide = jnp.concatenate([keys, spots_ref[:, : 2 * GRID]], 1)
-        query_wide = dot_tn(score_grad, wide)
+        query_wide = dot_tn(score_grad, wide[:, : HD + 2 * GRID])
         shift_ref[head] += query_wide
         grad_ref[0, 0, :, base : base + HD] = (query_wide[:, :HD] * SCALE).astype(jnp.bfloat16)
         grad_ref[0, 0, :, base + HD : base + 2 * HD] = key_grad.astype(jnp.bfloat16)
@@ -341,21 +345,48 @@
     )(mixed, weights, stream, mods, bias)
 
 
-def feed_forward_kernel(
+def expand_kernel(width, second_ref, expand_ref, bias_ref, active_ref, slope_ref):
+    hidden = dot_nn(second_ref[0], block_of(expand_ref, width)) + bias_ref[0]
+    square = hidden * hidden
+    curve = jnp.tanh(hidden * (ROOT + ROOT * CUBE * square))
+    half = 0.5 + 0.5 * curve
+    active = hidden * half
+    slope = half + active * (0.5 - 0.5 * curve) * (2.0 * ROOT + 6.0 * ROOT * CUBE * square)
+    active_ref[0, 0] = active.astype(jnp.bfloat16)
+    slope_ref[0, 0] = slope.astype(jnp.bfloat16)
+
+
+def expand_forward(second_in, weights, lanes, width, bias):
+    images = second_in.shape[0]
+    parts = weights.shape[1]
+    wide = pl.BlockSpec((1, 1, TOKS, width), lambda m, i: (m, i, 0, 0))
+    return pl.pallas_call(
+        partial(expand_kernel, width),
+        grid=(parts, images),
+        in_specs=[
+            pl.BlockSpec((1, TOKS, D), lambda m, i: (i, 0, 0)),
+            weight_spec(weights, lanes, 0),
+            pl.BlockSpec((1, 1, width), lambda m, i: (m, 0, 0)),
+        ],
+        out_specs=[wide, wide],
+        out_shape=[jax.ShapeDtypeStruct((parts, images, TOKS, width), jnp.bfloat16)] * 2,
+        cost_estimate=cost(images * 2 * TOKS * D * FF, 3e7, images * TOKS * FF),
+        compiler_params=params("arbitrary", "arbitrary"),
+        name="expand_forward",
+    )(second_in, weights, bias)
+
+
+def narrow_kernel(
     width,
-    second_ref,
-    expand_ref,
+    active_ref,
     narrow_ref,
-    bias_ref,
     stream_ref,
     mods_ref,
-    biases_ref,
+    bias_ref,
     final_ref,
     final_bias_ref,
     target_ref,
     valid_ref,
-    active_ref,
-    slope_ref,
     two_ref,
     branch_grad_ref,
     sums_ref,
@@ -365,26 +396,7 @@
 ):
     m, i = pl.program_id(0), pl.program_id(1)
     last = pl.num_programs(0) - 1
-    chunk = width // 3 if width % 384 == 0 else width
-    second = second_ref[0]
-    total = None
-    for begin in range(0, width, chunk):
-        columns = expand_ref[:, 0, :, begin : begin + chunk]
-        columns = columns.reshape(columns.shape[0] * columns.shape[1], chunk)
-        hidden = dot_nn(second, columns) + bias_ref[0, :, begin : begin + chunk]
-        square = hidden * hidden
-        curve = jnp.tanh(ROOT * hidden * (1.0 + 0.044715 * square))
-        half = 0.5 * (1.0 + curve)
-        active = (hidden * half).astype(jnp.bfloat16)
-        slope = half + 0.5 * hidden * (1.0 - curve * curve) * (
-            ROOT * (1.0 + 3.0 * 0.044715 * square)
-        )
-        active_ref[0, 0, :, begin : begin + chunk] = active
-        slope_ref[0, 0, :, begin : begin + chunk] = slope.astype(jnp.bfloat16)
-        columns = narrow_ref[:, 0, :, begin : begin + chunk]
-        columns = columns.reshape(columns.shape[0] * columns.shape[1], chunk)
-        product = dot_nt(active, columns)
-        total = product if total is None else total + product
+    total = dot_nt(active_ref[0, 0], block_of(narrow_ref, width))
 
     @pl.when(m == 0)
     def begin_total():
@@ -396,7 +408,7 @@
 
     @pl.when(m == last)
     def finish():
-        branch = total_ref[i] + total + biases_ref[0:1]
+        branch = total_ref[i] + total + bias_ref[...]
         gate = mods_ref[0, 5:6]
         scale = 1.0 + mods_ref[0, 7:8]
         normed, inverse = norm_of(stream_ref[0] + gate * branch)
@@ -419,35 +431,28 @@
         output_ref[0, 1:2] = jnp.broadcast_to(loss, (1, 32))
 
 
-def feed_forward(second_in, weights, lanes, width, bias, stream, mods, biases, final, final_bias, target, valid):
-    images = second_in.shape[0]
-    parts = weights.shape[1]
+def narrow_forward(active, weights, lanes, width, stream, mods, bias, final, final_bias, target, valid):
+    parts, images = active.shape[:2]
     last = parts - 1
-    tile = pl.BlockSpec((1, TOKS, D), lambda m, i: (i, 0, 0))
     late = pl.BlockSpec((1, TOKS, D), lambda m, i: (hold(m, last, i), 0, 0))
-    wide = pl.BlockSpec((1, 1, TOKS, width), lambda m, i: (m, i, 0, 0))
     fixed = lambda shape: pl.BlockSpec(shape, lambda m, i: (0,) * len(shape))
     lately = lambda shape: pl.BlockSpec((1,) + shape, lambda m, i: (hold(m, last, i), 0, 0))
     return pl.pallas_call(
-        partial(feed_forward_kernel, width),
+        partial(narrow_kernel, width),
         grid=(parts, images),
         in_specs=[
-            tile,
+            pl.BlockSpec((1, 1, TOKS, width), lambda m, i: (m, i, 0, 0)),
             weight_spec(weights, lanes, 0),
-            weight_spec(weights, lanes, 1),
-            pl.BlockSpec((1, 1, width), lambda m, i: (m, 0, 0)),
             late,
             pl.BlockSpec((1, 8, D), lambda m, i: (i, 0, 0)),
-            fixed(biases.shape),
+            fixed(bias.shape),
             fixed(final.shape),
             fixed(final_bias.shape),
             lately((TOKS, 32)),
             pl.BlockSpec((1, 1, 128), lambda m, i: (i, 0, 0)),
         ],
-        out_specs=[wide, wide, late, late, lately((4, D)), lately((32, D)), lately((2, 32))],
+        out_specs=[late, late, lately((4, D)), lately((32, D)), lately((2, 32))],
         out_shape=[
-            jax.ShapeDtypeStruct((parts, images, TOKS, width), jnp.bfloat16),
-            jax.ShapeDtypeStruct((parts, images, TOKS, width), jnp.bfloat16),
             jax.ShapeDtypeStruct((images, TOKS, D), jnp.float32),
             jax.ShapeDtypeStruct((images, TOKS, D), jnp.bfloat16),
             jax.ShapeDtypeStruct((images, 4, D), jnp.float32),
@@ -455,10 +460,10 @@
             jax.ShapeDtypeStruct((images, 2, 32), jnp.float32),
         ],
         scratch_shapes=[pltpu.VMEM((images, TOKS, D), jnp.float32)],
-        cost_estimate=cost(images * 4 * TOKS * D * FF, 6e7, images * TOKS * FF),
+        cost_estimate=cost(images * 2 * TOKS * D * FF, 4e7),
         compiler_params=params("arbitrary", "arbitrary"),
-        name="feed_forward",
-    )(second_in, weights, weights, bias, stream, mods, biases, final, final_bias, target, valid)
+        name="narrow_forward",
+    )(active, weights, stream, mods, bias, final, final_bias, target, valid)
 
 
 def feed_backward_kernel(
@@ -480,7 +485,7 @@
 ):
     m, i = pl.program_id(0), pl.program_id(1)
     last = pl.num_programs(0) - 1
-    chunk = width // 3 if width % 384 == 0 else width
+    chunk = width
     branch_grad = branch_grad_ref[0]
 
     @pl.when(i == 0)
@@ -524,9 +529,11 @@
         sums_ref[0, 3:4] = total_rows(first_grad.astype(jnp.float32))
 
 
-def feed_backward(branch_grad, weights, lanes, width, slope, two, stream, branch, mods, others):
+def feed_backward(
+    branch_grad, expand, narrow, lanes, width, slope, two, stream, branch, mods, others
+):
     images = branch_grad.shape[0]
-    parts = weights.shape[1]
+    parts = expand.shape[1]
     last = parts - 1
     tile = pl.BlockSpec((1, TOKS, D), lambda m, i: (i, 0, 0))
     late = pl.BlockSpec((1, TOKS, D), lambda m, i: (hold(m, last, i), 0, 0))
@@ -536,8 +543,8 @@
         grid=(parts, images),
         in_specs=[
             tile,
-            weight_spec(weights, lanes, 0),
-            weight_spec(weights, lanes, 1),
+            weight_spec(expand, lanes, 0),
+            weight_spec(narrow, lanes, 0),
             wide,
             late,
             late,
@@ -563,7 +570,7 @@
         cost_estimate=cost(images * 4 * TOKS * D * FF, 6e7),
         compiler_params=params("arbitrary", "arbitrary"),
         name="feed_backward",
-    )(branch_grad, weights, weights, slope, two, stream, branch, mods, *others)
+    )(branch_grad, expand, narrow, slope, two, stream, branch, mods, *others)
 
 
 def joined_backward_kernel(
@@ -613,7 +620,7 @@
         grid=(parts, images),
         in_specs=[
             pl.BlockSpec((1, 1, TOKS, width), lambda m, i: (m, i, 0, 0)),
-            weight_spec(weights, lanes, 0),
+            weight_spec(weights, lanes, 1),
             late,
             late,
             pl.BlockSpec((1, 8, D), lambda m, i: (i, 0, 0)),
@@ -660,7 +667,7 @@
     parts = pairs[0][1].shape[0]
     widths = [gradient.shape[2] for _, gradient in pairs]
     width = sum(widths)
-    chunks = 3 if len(pairs) == 1 and width % 384 == 0 else 1
+    chunks = 1
     pieces = [member // chunks for member in widths]
     count = parts // cores
     taken = 2 * len(pairs) + (received is not None)
@@ -725,6 +732,11 @@
     return result.reshape(groups * parts, D // groups, width)
 
 
+def two_terms(values):
+    upper = lax.reduce_precision(values, 8, 7)
+    return upper.astype(jnp.bfloat16), (values - upper).astype(jnp.bfloat16)
+
+
 def relative_tables(rel_table):
     rows = offset_table()
     span = 2 * GRID - 1
@@ -734,9 +746,7 @@
     table = jnp.concatenate(
         [jnp.broadcast_to(along_rows, full), jnp.broadcast_to(along_cols, full)], 3
     ).reshape(H, TOKS, 2 * GRID) * math.sqrt(HD)
-    upper = table.astype(jnp.bfloat16)
-    lower = (table - upper.astype(jnp.float32)).astype(jnp.bfloat16)
-    return jnp.concatenate([upper, lower], 2)
+    return jnp.concatenate(two_terms(table), 2)
 
 
 def spot_table():
@@ -935,29 +945,41 @@
 
     joined_width, mixback_width = (joined_weight.shape[1], mixback_weight.shape[1])
     hidden_width = expand_weight.shape[1]
-    shard_one = jnp.concatenate([lane_padded(joined_weight), mixback_weight], 1)
-    shard_two = jnp.concatenate([lane_padded(expand_weight), lane_padded(narrow_weight)], 1)
-    gathered_one = in_parts(
-        lax.all_gather(shard_one.astype(jnp.bfloat16), all_axes), dp, mp
-    )
-    feed = in_parts(lax.all_gather(shard_two.astype(jnp.bfloat16), all_axes), dp, mp)
-    joined_lanes = gathered_one.shape[3] - mixback_width
-    hidden_lanes = feed.shape[3] // 2
-    mixback = gathered_one[:, :, :, joined_lanes:]
-
-    facts = small_gather(
-        jnp.concatenate([timesteps, labels, dropped, buckets, counts]).astype(jnp.float32),
+    shard_one = jnp.concatenate(
+        [
+            lane_padded(expand_weight),
+            lane_padded(jnp.concatenate([joined_weight, mixback_weight], 1)),
+        ],
+        1,
+    )
+    first = in_parts(lax.all_gather(shard_one.astype(jnp.bfloat16), all_axes), dp, mp)
+    narrow = in_parts(
+        lax.all_gather(lane_padded(narrow_weight).astype(jnp.bfloat16), all_axes), dp, mp
+    )
+    lanes = narrow.shape[3]
+    mixback = first[:, :, :, lanes + joined_width : lanes + joined_width + mixback_width]
+
+    facts_own = jnp.concatenate([timesteps, labels, dropped, buckets, counts])
+    first_words = timeone_weight.size
+    packed = small_gather(
+        jnp.concatenate(
+            [
+                timeone_weight.astype(jnp.bfloat16).reshape(first_words),
+                (facts_own // 8).astype(jnp.bfloat16),
+                (facts_own % 8).astype(jnp.bfloat16),
+            ]
+        ),
         dp_axes,
         dp,
     )
+    facts = packed[:, first_words:].astype(jnp.float32).reshape(dp, 2, facts_own.shape[0])
+    facts = 8.0 * facts[:, 0] + facts[:, 1]
     times_all = facts[:, :group_size].reshape(images_all)
     labels_all = facts[:, group_size : 2 * group_size].reshape(images_all)
     dropped_all = facts[:, 2 * group_size : 3 * group_size].reshape(images_all)
     buckets_all = facts[:, 3 * group_size]
     token_count = jnp.sum(facts[:, 3 * group_size + 1]) * TOKS
-    time_first = small_gather(timeone_weight.astype(jnp.bfloat16), dp_axes, dp).reshape(
-        FREQ, width_mp
-    )
+    time_first = packed[:, :first_words].reshape(FREQ, width_mp)
     bucket_width = float(1000 // NB)
     rows_in = frequencies(
         jnp.concatenate([times_all, buckets_all * bucket_width + 0.5 * bucket_width])
@@ -1043,19 +1065,21 @@
     )
     added = added.reshape(images, mp, joined_width).transpose(1, 0, 2)[:, :, None]
     joined_rows, mixed, log_total = attention_forward(
-        first_in, gathered_one, joined_lanes, joined_width, added, table, spots
+        first_in, first, lanes, joined_width, added, table, spots
     )
     branch, stream_one, second_in = mixback_forward(
         mixed, mixback, stream_zero, mods, small_piece("out_bias")[None]
     )
     timetwo_narrow, second_in = tie(timetwo_weight.astype(jnp.bfloat16), second_in)
     time_second_all = small_gather(timetwo_narrow, dp_axes, dp)
-    active, slope, grad_two, grad_branch_two, sums_c, final_grads, output_sums = feed_forward(
-        second_in,
-        feed,
-        hidden_lanes,
+    active, slope = expand_forward(
+        second_in, first, lanes, hidden_width, small_piece("fc1_bias").reshape(mp, 1, hidden_width)
+    )
+    grad_two, grad_branch_two, sums_c, final_grads, output_sums = narrow_forward(
+        active,
+        narrow,
+        lanes,
         hidden_width,
-        small_piece("fc1_bias").reshape(mp, 1, hidden_width),
         stream_one,
         mods,
         small_piece("fc2_bias")[None],
@@ -1079,8 +1103,9 @@
     narrow_sum.gradient(narrow_pairs)
     grad_hidden, hidden_sums, grad_one, grad_branch, sums_b = feed_backward(
         grad_branch_two,
-        feed,
-        hidden_lanes,
+        first,
+        narrow,
+        lanes,
         hidden_width,
         slope,
         grad_two,
@@ -1103,8 +1128,8 @@
     heads_sum.gradient(heads_pairs, list(narrow_sum.sent))
     sums_a, embed_grads = joined_backward(
         heads_first,
-        gathered_one,
-        joined_lanes,
+        first,
+        lanes,
         grad_one,
         stream_zero,
         mods,
@@ -1171,8 +1196,7 @@
     )
 
     def split_rows(image_rows, bucket_rows):
-        upper = bucket_rows.astype(jnp.bfloat16)
-        lower = (bucket_rows - upper.astype(jnp.float32)).astype(jnp.bfloat16)
+        upper, lower = two_terms(bucket_rows)
         return jnp.concatenate([image_rows.astype(jnp.bfloat16), upper, lower], 0)
 
     def double_rows(rows):
@@ -1225,8 +1249,7 @@
     )
     timeone_grad = dot_tn(double_rows(rows_own), grad_hidden_time)
     label_rows = lax.dynamic_slice_in_dim(grad_cond[:images_all], mp_index * width_mp, width_mp, 1)
-    label_upper = label_rows.astype(jnp.bfloat16)
-    label_lower = (label_rows - label_upper.astype(jnp.float32)).astype(jnp.bfloat16)
+    label_upper, label_lower = two_terms(label_rows)
     class_raw = dot_tn(
         jnp.concatenate([onehot, onehot], 0), jnp.concatenate([label_upper, label_lower], 0)
     )

time: 808 us -> 753 us (0.932)
  Pallas kernels: 322 us -> 291 us
  waiting for transfers between devices: 185 us -> 170 us
  starting transfers between devices: 73.6 us -> 62 us
    all_gather x1, waiting for transfers between devices: 81.1 us -> 22.8 us  [per_device(): lax.all_gather(lane_padded(narrow_weight).astype(jnp.bfloat16), all_axes)]
    all_gather x1, waiting for transfers between devices: 0.01 us -> 45.3 us  [per_device(): lax.all_gather(shard_one.astype(jnp.bfloat16), all_axes)]
    pallas_call x1, Pallas kernels: 46.1 us -> 32.7 us  [attention_forward(): pl.pallas_call(partial(attention_forward_kernel, width), grid=(parts, ima...]
    all_to_all x7 -> x6, waiting for transfers between devices: 35.6 us -> 23.4 us  [small_gather(): return lax.all_to_all(spread, axes, 0, 0, tiled=True)]
    pallas_call x1, Pallas kernels: 49.3 us -> 39.3 us  [attention_backward(): pl.pallas_call(ordered(attention_backward_kernel, 6, len(others)), grid=(...]
    all_to_all x7 -> x6, starting transfers between devices: 42.2 us -> 33.6 us  [small_gather(): return lax.all_to_all(spread, axes, 0, 0, tiled=True)]
    unnamed x228 -> x231, local copies, waits for them, and re-layouts: 17 us -> 18.5 us
    pallas_call x1 -> x2, Pallas kernels: 60.4 us -> 60.1 us  [the longest x1 31.9 us: narrow_forward(): pl.pallas_call(partial(narrow_kernel, width), grid=(parts, images), in_sp...]
  transfers between devices with their start and end apart: 29 -> 28, of which waited for: 12 -> 13; matrix products, arithmetic and copies ran while one was open for 18% -> 20% of each run, Pallas kernels for 39% -> 38%
where the time goes in v2:
time: 753 us; the launch traced here: 742 us
  Pallas kernels  291 us (39%)
  waiting for transfers between devices  170 us (23%)
  local copies, waits for them, and re-layouts  97.9 us (13%)
  other arithmetic  78 us (10%)
  starting transfers between devices  62 us (8%)
  between operations  27.7 us (4%)
  matrix products  15 us (2%)
    pallas_call x4, Pallas kernels, weight_gradient(): pl.pallas_call(lambda chosen_ref, *refs: kernel(*refs), grid_spec=pltpu.P...  53 us
    pallas_call x1, Pallas kernels, feed_backward(): pl.pallas_call(ordered(partial(feed_backward_kernel, width), 8, len(other...  46.2 us
    all_gather x1, waiting for transfers between devices, per_device(): lax.all_gather(shard_one.astype(jnp.bfloat16), all_axes)  45.3 us
    pallas_call x1, Pallas kernels, attention_backward(): pl.pallas_call(ordered(attention_backward_kernel, 6, len(others)), grid=(...  39.3 us
    all_to_all x6, starting transfers between devices, small_gather(): return lax.all_to_all(spread, axes, 0, 0, tiled=True)  33.6 us
    pallas_call x1, Pallas kernels, attention_forward(): pl.pallas_call(partial(attention_forward_kernel, width), grid=(parts, ima...  32.7 us
    pallas_call x1, Pallas kernels, narrow_forward(): pl.pallas_call(partial(narrow_kernel, width), grid=(parts, images), in_sp...  31.9 us
    pallas_call x1, Pallas kernels, expand_forward(): pl.pallas_call(partial(expand_kernel, width), grid=(parts, images), in_sp...  28.2 us
  transfers between devices with their start and end apart: 28, of which 13 were waited for; matrix products, arithmetic and copies ran while one was open for 20% of the time, Pallas kernels for 38%

profile of v2, /device:TPU:0, one launch (start us, length us, event | category | flops | bytes accessed | tf_op | source)
XLA Modules:
  0.0 741.8 jit_solution(11420992986647978571)
XLA Ops:
  16.3 7.3 all-to-all-start
  40.0 2.8 multiply_cosine_fusion
  51.9 3.6 all-to-all-start.1
  55.6 3.2 pad_maximum_fusion.table_ref.refs_4_
  58.8 8.0 %all-to-all-done.1 = f32[4,136,144]{2,1,0:T(8,128)S(1)} async-done(((f32[4,136,144]{2,1,0:T(8,128)}), f32[4,136,144]{2,1,0:T(8,128)S(1)}, u32[]{:S(2)}, u32[]{:S(2)}) %all-to-all-start.1) | async-done | bytes 313376 | tf_op jit(solution)/shard_map/all_to_all | solution.py:774
  70.7 4.5 all-to-all-start.2
  78.9 27.7 %all-to-all-done.2 = bf16[32,4,2880]{2,1,0:T(4,128)(2,1)S(1)} async-done(((bf16[32,4,2880]{2,1,0:T(4,128)(2,1)}), bf16[32,4,2880]{2,1,0:T(4,128)(2,1)S(1)}, u32[]{:S(2)}, u32[]{:S(2)}) %all-to-all-start.2) | async-done | bytes 737312 | tf_op jit(solution)/shard_map/all_to_all | solution.py:1020
  109.2 5.7 add_convert_fusion.first_ref
  114.9 45.3 %all-gather.4.cloned.1.call-done = bf16[32,144,2304]{2,1,0:T(8,128)(2,1)} async-done(((bf16[1,144,2304]{2,1,0:T(8,128)(2,1)}), bf16[32,144,2304]{2,1,0:T(8,128)(2,1)}) %all-gather.4.cloned.1.call-update) | async-done | bytes 21233680 | tf_op jit(solution)/shard_map/all_gather | solution.py:955
  160.2 5.7 slice.372.weight_ref.refs_1_
  165.9 32.7 %attention_forward.1 = (bf16[4,4,256,864]{3,2,1,0:T(8,128)(2,1)}, bf16[4,4,256,288]{3,2,1,0:T(8,128)(2,1)}, f32[4,4,4,256]{3,2,1,0:T(4,128)}) custom-call(bf16[4,256,1152]{2,1,0:T(8,128)(2,1)} %add_convert_fusion.first_ref, bf16[8,4,144,2304]{3,2,1,0:T(8,128)(2,1)} %bitcast.194, f32[4,4,1,864]{3,2,1,0:T(1,128)} %broadcast_in_dim.95.added_ref, ...), custom_call_target="tpu_custom_call" | custom-call | flops 10301210624 | bytes 30000000 | tf_op jit(solution)/shard_map/attention_forward/pallas_call | solution.py:206
  198.6 11.5 %mixback_forward.1 = (bf16[4,256,1152]{2,1,0:T(8,128)(2,1)}, f32[4,256,1152]{2,1,0:T(8,128)}, bf16[4,256,1152]{2,1,0:T(8,128)(2,1)}) custom-call(bf16[4,4,256,288]{3,2,1,0:T(8,128)(2,1)} %get-tuple-element.79.mixed_ref, bf16[8,4,144,288]{3,2,1,0:T(8,128)(2,1)} %slice.372.weight_ref.refs_1_, f32[4,256,1152]{2,1,0:T(8,128)} %copy-done, ...), custom_call_target="tpu_custom_call" | custom-call | flops 2717908992 | bytes 16515072 | tf_op jit(solution)/shard_map/mixback_forward/pallas_call | solution.py:326
  211.1 3.9 all-to-all-start.3
  215.3 28.2 %expand_forward.1 = (bf16[4,4,256,1152]{3,2,1,0:T(8,128)(2,1)}, bf16[4,4,256,1152]{3,2,1,0:T(8,128)(2,1)}) custom-call(bf16[4,256,1152]{2,1,0:T(8,128)(2,1)} %get-tuple-element.82.second_ref, bf16[8,4,144,2304]{3,2,1,0:T(8,128)(2,1)} %bitcast.195, f32[4,1,1152]{2,1,0:T(1,128)} %reshape.511.bias_ref), custom_call_target="tpu_custom_call" | custom-call | flops 10871635968 | bytes 30000000 | tf_op jit(solution)/shard_map/expand_forward/pallas_call | solution.py:363
  243.5 22.8 %all-gather.6.cloned.1.call-done = bf16[4608,1152]{1,0:T(8,128)(2,1)} async-done(((bf16[144,1152]{1,0:T(8,128)(2,1)}), bf16[4608,1152]{1,0:T(8,128)(2,1)}) %all-gather.6.cloned.1.call-update) | async-done | bytes 10616848 | tf_op jit(solution)/shard_map/all_gather | solution.py:957
  266.9 31.9 %narrow_forward.1 = (f32[4,256,1152]{2,1,0:T(8,128)}, bf16[4,256,1152]{2,1,0:T(8,128)(2,1)}, f32[4,4,1152]{2,1,0:T(4,128)}, f32[4,32,1152]{2,1,0:T(8,128)}, f32[4,2,32]{2,1,0:T(2,128)}) custom-call(bf16[4,4,256,1152]{3,2,1,0:T(8,128)(2,1)} %get-tuple-element.83.active_ref, bf16[8,4,144,1152]{3,2,1,0:T(8,128)(2,1)} %bitcast.243, ...), custom_call_target="tpu_custom_call" | custom-call | flops 10871635968 | bytes 40000000 | tf_op jit(solution)/shard_map/narrow_forward/pallas_call | solution.py:440
  298.9 11.4 %weight_gradient.4.refs_8_ = bf16[2,1152,1152]{2,1,0:T(8,128)(2,1)} custom-call(s32[1]{0:T(128)S(6)} %sub.190.chosen_ref, bf16[1024,1152]{1,0:T(8,128)(2,1)} %bitcast.213, bf16[4,1024,1152]{2,1,0:T(8,128)(2,1)} %bitcast.206), custom_call_target="tpu_custom_call" | custom-call | flops 5435817984 | bytes 7077888 | tf_op jit(solution)/shard_map/weight_gradient/pallas_call | solution.py:684
  316.4 46.2 %feed_backward.1 = (bf16[4,4,256,1152]{3,2,1,0:T(8,128)(2,1)}, f32[4,1,1152]{2,1,0:T(1,128)}, f32[4,256,1152]{2,1,0:T(8,128)}, bf16[4,256,1152]{2,1,0:T(8,128)(2,1)}, f32[4,4,1152]{2,1,0:T(4,128)}) custom-call(bf16[4,256,1152]{2,1,0:T(8,128)(2,1)} %get-tuple-element.86.refs_0_, bf16[8,4,144,2304]{3,2,1,0:T(8,128)(2,1)} %bitcast.196, ...), custom_call_target="tpu_custom_call" | custom-call | flops 21743271936 | bytes 60000000 | tf_op jit(solution)/shard_map/feed_backward/pallas_call | solution.py:541
  362.6 21.2 %whole_gradient.1 = bf16[8,4,144,1152]{3,2,1,0:T(8,128)(2,1)} custom-call(bf16[1024,1152]{1,0:T(8,128)(2,1)} %bitcast.245, bf16[4,1024,1152]{2,1,0:T(8,128)(2,1)} %bitcast.246), custom_call_target="tpu_custom_call" | custom-call | flops 10871635968 | bytes 11796480 | tf_op jit(solution)/shard_map/whole_gradient/pallas_call | solution.py:716
  386.8 12.2 %weight_gradient.5 = bf16[2,1152,1152]{2,1,0:T(8,128)(2,1)} custom-call(s32[1]{0:T(128)} %bitcast.chosen_ref, bf16[1024,1152]{1,0:T(8,128)(2,1)} %bitcast.214, bf16[4,1024,1152]{2,1,0:T(8,128)(2,1)} %bitcast.207, bf16[2,1152,1152]{2,1,0:T(8,128)(2,1)} %collective-permute-done.refs_2_, bf16[32,144,1152]{2,1,0:T(8,128)(2,1)} %bitcast.192), custom_call_target="tpu_custom_call" | custom-call | flops 5435817984 | bytes 7077888 | tf_op jit(solution)/shard_map/weight_gradient/pallas_call | solution.py:684
  399.1 3.2 fusion.113
  408.9 39.3 %attention_backward.1 = (bf16[4,4,256,864]{3,2,1,0:T(8,128)(2,1)}, f32[4,4,8,864]{3,2,1,0:T(8,128)}, f32[16,256,104]{2,1,0:T(8,128)}) custom-call(bf16[4,256,1152]{2,1,0:T(8,128)(2,1)} %get-tuple-element.91.refs_0_, bf16[8,4,144,288]{3,2,1,0:T(8,128)(2,1)} %slice.372.weight_ref.refs_1_, bf16[4,4,256,864]{3,2,1,0:T(8,128)(2,1)} %get-tuple-element.92.refs_2_, ...), custom_call_target="tpu_custom_call" | custom-call | flops 8086618112 | bytes 50000000 | tf_op jit(solution)/shard_map/attention_backward/pallas_call | solution.py:279
  449.9 3.6 slice.320
  456.2 2.4 bitcast_reduce_fusion
  465.9 14.3 %weight_gradient.6.refs_6_ = bf16[2,1152,1152]{2,1,0:T(8,128)(2,1)} custom-call(s32[1]{0:T(128)S(6)} %sub.190.chosen_ref, bf16[1024,1152]{1,0:T(8,128)(2,1)} %bitcast.202, bf16[1024,1152]{1,0:T(8,128)(2,1)} %bitcast.204, bf16[4,1024,864]{2,1,0:T(8,128)(2,1)} %bitcast.189, bf16[4,1024,288]{2,1,0:T(8,128)(2,1)} %bitcast.198, ...), custom_call_target="tpu_custom_call" | custom-call | flops 5435817984 | bytes 7077888 | tf_op jit(solution)/shard_map/weight_gradient/pallas_call | solution.py:684
  480.2 27.3 %joined_backward.1 = (f32[4,4,1152]{2,1,0:T(4,128)}, f32[4,16,1152]{2,1,0:T(8,128)}) custom-call(bf16[4,4,256,864]{3,2,1,0:T(8,128)(2,1)} %get-tuple-element.95.refs_0_, bf16[8,4,144,2304]{3,2,1,0:T(8,128)(2,1)} %bitcast.197, f32[4,256,1152]{2,1,0:T(8,128)} %get-tuple-element.96.refs_2_, f32[4,256,1152]{2,1,0:T(8,128)} %copy-done, f32[4,8,1152]{2,1,0:T(8,128)} %bitcast.222, ...), custom_call_target="tpu_custom_call" | custom-call | flops 8153726976 | bytes 30000000 | tf_op jit(solution)/shard_map/joined_backward/pallas_call | solution.py:618
  510.0 3.7 all-to-all-start.4
  519.6 8.3 %concatenate.130 = f32[66688]{0:T(1024)} concatenate(f32[1152]{0:T(1024)S(1)} %slice_reduce_fusion.3, f32[1152]{0:T(1024)S(1)} %reduce_sum.316, f32[1152]{0:T(1024)S(1)} %reduce_sum.318, f32[1152]{0:T(1024)S(1)} %copy-done.88, f32[4608]{0:T(1024)S(1)} %reshape.525, f32[1152]{0:T(1024)S(1)} %slice_reduce_fusion.1, f32[32]{0:T(128)S(1)} %slice_reduce_fusion.10, ...), dimensions={0} | concatenate | bytes 533504 | tf_op jit(solution)/shard_map/concatenate | solution.py:1228
  534.7 6.2 all-to-all-done.4
  542.4 15.0 %weight_gradient.7 = bf16[2,1152,1152]{2,1,0:T(8,128)(2,1)} custom-call(s32[1]{0:T(128)} %bitcast.chosen_ref, bf16[1024,1152]{1,0:T(8,128)(2,1)} %bitcast.203, bf16[1024,1152]{1,0:T(8,128)(2,1)} %bitcast.205, bf16[4,1024,864]{2,1,0:T(8,128)(2,1)} %bitcast.190, bf16[4,1024,288]{2,1,0:T(8,128)(2,1)} %bitcast.199, ...), custom_call_target="tpu_custom_call" | custom-call | flops 5435817984 | bytes 7077888 | tf_op jit(solution)/shard_map/weight_gradient/pallas_call | solution.py:684
  560.3 3.0 fusion.112
  570.0 4.2 all-to-all-start.5
  579.1 3.4 multiply_reduce_fusion.1
  582.5 7.0 collective-permute-done.9
  591.8 4.7 all-to-all-start.6
  596.5 2.5 multiply_reduce_fusion.6
  599.0 2.9 multiply_reduce_fusion.3
  601.9 11.8 %collective-permute-done.7 = bf16[2,2,144,1152]{3,2,1,0:T(8,128)(2,1)} collective-permute-done((bf16[2,2,144,1152]{3,2,1,0:T(8,128)(2,1)}, bf16[2,2,144,1152]{3,2,1,0:T(8,128)(2,1)}, u32[]{:S(2)}, u32[]{:S(2)}) %collective-permute-start.7) | collective-permute-done | bytes 1327136 | tf_op jit(solution)/shard_map/ppermute | solution.py:786
  620.0 3.4 all-to-all-done.6
  630.9 2.6 all-to-all-start.7
  637.9 7.5 %collective-permute-done.12 = bf16[2,144,1152]{2,1,0:T(8,128)(2,1)} collective-permute-done((bf16[2,144,1152]{2,1,0:T(8,128)(2,1)}, bf16[2,144,1152]{2,1,0:T(8,128)(2,1)}, u32[]{:S(2)}, u32[]{:S(2)}) %collective-permute-start.12) | collective-permute-done | bytes 663584 | tf_op jit(solution)/shard_map/ppermute | solution.py:786
  649.5 2.8 collective-permute-start.14
  655.1 6.5 collective-permute-done.13
  661.7 11.2 %collective-permute-done.14 = bf16[144,1152]{1,0:T(8,128)(2,1)S(1)} collective-permute-done((bf16[144,1152]{1,0:T(8,128)(2,1)S(1)}, bf16[144,1152]{1,0:T(8,128)(2,1)S(1)}, u32[]{:S(2)}, u32[]{:S(2)}) %collective-permute-start.14) | collective-permute-done | bytes 331808 | tf_op jit(solution)/shard_map/ppermute | solution.py:854
  682.3 9.9 %all-to-all-start.8 = ((f32[32,1,2482]{2,1,0:T(1,128)}), f32[32,1,2482]{2,1,0:T(1,128)S(1)}, u32[]{:S(2)}, u32[]{:S(2)}) async-start(f32[32,1,2482]{2,1,0:T(1,128)} %broadcast_in_dim.192), calls=%async_computation.9 | async-start | bytes 655360 | tf_op jit(solution)/shard_map/all_to_all | solution.py:774
  692.3 12.0 %all-to-all-done.8 = f32[32,1,2482]{2,1,0:T(1,128)S(1)} async-done(((f32[32,1,2482]{2,1,0:T(1,128)}), f32[32,1,2482]{2,1,0:T(1,128)S(1)}, u32[]{:S(2)}, u32[]{:S(2)}) %all-to-all-start.8) | async-done | bytes 317728 | tf_op jit(solution)/shard_map/all_to_all | solution.py:774
  721.7 2.4 multiply_subtract_fusion.1
  726.0 3.2 multiply_subtract_fusion
  (508 shorter events, 153.8 us)
Async XLA Ops:
  7.2 153.0 %all-gather.4.cloned.1.call-start = ((), (), s32[]{:S(2)}) async-start(), calls=%async_computation.10 | async-start | bytes 21897216 | tf_op jit(solution)/shard_map/all_gather | solution.py:955
  10.7 13.8 %copy-start.43 = (f32[144,288]{1,0:T(8,128)S(1)}, f32[144,288]{1,0:T(8,128)}, u32[]{:S(2)}) copy-start(f32[144,288]{1,0:T(8,128)} %param.56) | copy-start | bytes 497668
  10.7 255.5 %all-gather.6.cloned.1.call-start = ((), (), s32[]{:S(2)}) async-start(), calls=%async_computation.12 | async-start | bytes 10948608 | tf_op jit(solution)/shard_map/all_gather | solution.py:957
  16.3 31.1 %all-to-all-start = ((bf16[8,2,4658]{2,1,0:T(2,128)(2,1)}), bf16[8,2,4658]{2,1,0:T(2,128)(2,1)S(1)}, u32[]{:S(2)}, u32[]{:S(2)}) async-start(bf16[8,2,4658]{2,1,0:T(2,128)(2,1)} %reshape.565), calls=%async_computation | async-start | bytes 303104 | tf_op jit(solution)/shard_map/all_to_all | solution.py:774
  24.5 25.8 %copy-start.37 = (bf16[144,288]{1,0:T(8,128)(2,1)}, bf16[144,288]{1,0:T(8,128)(2,1)S(1)}, u32[]{:S(2)}) copy-start(bf16[144,288]{1,0:T(8,128)(2,1)S(1)} %convert_element_type.272) | copy-start | bytes 248836
  39.4 28.1 %copy-start.93 = (f32[144]{0:T(256)}, f32[144]{0:T(256)S(1)}, u32[]{:S(2)}) copy-start(f32[144]{0:T(256)S(1)} %dynamic_slice.107) | copy-start | bytes 1732
  51.9 14.9 %all-to-all-start.1 = ((f32[4,136,144]{2,1,0:T(8,128)}), f32[4,136,144]{2,1,0:T(8,128)S(1)}, u32[]{:S(2)}, u32[]{:S(2)}) async-start(f32[4,136,144]{2,1,0:T(8,128)} %broadcast_in_dim.91), calls=%async_computation.1 | async-start | bytes 1114112 | tf_op jit(solution)/shard_map/all_to_all | solution.py:774
  55.6 13.7 %copy-start.84 = (pred[2880]{0:T(1024)(128)(4,1)}, pred[2880]{0:T(1024)(128)(4,1)S(1)}, u32[]{:S(2)}) copy-start(pred[2880]{0:T(1024)(128)(4,1)S(1)} %add_compare_fusion) | copy-start | bytes 8644
  68.5 247.2 %copy-start.59 = (bf16[136,144]{1,0:T(8,128)(2,1)}, bf16[136,144]{1,0:T(8,128)(2,1)S(1)}, u32[]{:S(2)}) copy-start(bf16[136,144]{1,0:T(8,128)(2,1)S(1)} %multiply_convert_fusion.1) | copy-start | bytes 117508
  70.7 35.9 %all-to-all-start.2 = ((bf16[32,4,2880]{2,1,0:T(4,128)(2,1)}), bf16[32,4,2880]{2,1,0:T(4,128)(2,1)S(1)}, u32[]{:S(2)}, u32[]{:S(2)}) async-start(bf16[32,4,2880]{2,1,0:T(4,128)(2,1)} %select_convert_fusion), calls=%async_computation.2 | async-start | bytes 1507328 | tf_op jit(solution)/shard_map/all_to_all | solution.py:1020
  78.9 28.4 %copy-start.89 = (f32[1152]{0:T(1024)S(1)}, f32[1152]{0:T(1024)}, u32[]{:S(2)}) copy-start(f32[1152]{0:T(1024)} %get-tuple-element.187) | copy-start | bytes 13828
  78.9 28.4 %copy-start.90 = (f32[1152]{0:T(1024)S(1)}, f32[1152]{0:T(1024)}, u32[]{:S(2)}) copy-start(f32[1152]{0:T(1024)} %get-tuple-element.188) | copy-start | bytes 13828
  78.9 28.7 %copy-start.103 = (f32[3]{0:T(128)S(1)}, f32[3]{0:T(128)}, u32[]{:S(2)}) copy-start(f32[3]{0:T(128)} %pad.43.clone) | copy-start | bytes 40
  211.1 87.7 %all-to-all-start.3 = ((bf16[8,144,288]{2,1,0:T(8,128)(2,1)}), bf16[8,144,288]{2,1,0:T(8,128)(2,1)S(1)}, u32[]{:S(2)}, u32[]{:S(2)}) async-start(bf16[8,144,288]{2,1,0:T(8,128)(2,1)} %broadcast_in_dim.101), calls=%async_computation.3 | async-start | bytes 1769472 | tf_op jit(solution)/shard_map/all_to_all | solution.py:774
  215.0 345.3 %reduce-scatter.2.cloned.1.call-start = ((), (), s32[]{:S(2)}) async-start(), calls=%async_computation.11 | async-start | bytes 10948608 | tf_op jit(solution)/shard_map/reduce_scatter | solution.py:1118
  298.9 13.9 %copy-start.73 = (bf16[136,128]{1,0:T(8,128)(2,1)S(1)}, bf16[136,128]{1,0:T(8,128)(2,1)}, u32[]{:S(2)}) copy-start(bf16[136,128]{1,0:T(8,128)(2,1)} %copy-done.72) | copy-start | bytes 104452
  298.9 13.9 %copy-start.75 = (bf16[136,128]{1,0:T(8,128)(2,1)S(1)}, bf16[136,128]{1,0:T(8,128)(2,1)}, u32[]{:S(2)}) copy-start(bf16[136,128]{1,0:T(8,128)(2,1)} %copy-done.74) | copy-start | bytes 104452
  298.9 16.0 %copy-start.98 = (f32[128]{0:T(128)S(1)}, f32[128]{0:T(128)}, u32[]{:S(2)}) copy-start(f32[128]{0:T(128)} %copy-done.97) | copy-start | bytes 1540
  298.9 16.8 %copy-start.101 = (f32[4,2,32]{2,1,0:T(2,128)S(1)}, f32[4,2,32]{2,1,0:T(2,128)}, u32[]{:S(2)}) copy-start(f32[4,2,32]{2,1,0:T(2,128)} %get-tuple-element.104) | copy-start | bytes 3076
  298.9 17.4 %copy-start.78 = (f32[4,4,1152]{2,1,0:T(4,128)S(1)}, f32[4,4,1152]{2,1,0:T(4,128)}, u32[]{:S(2)}) copy-start(f32[4,4,1152]{2,1,0:T(4,128)} %get-tuple-element.103) | copy-start | bytes 221188
  310.4 76.5 %collective-permute-start = (bf16[2,1152,1152]{2,1,0:T(8,128)(2,1)}, bf16[2,1152,1152]{2,1,0:T(8,128)(2,1)}, u32[]{:S(2)}, u32[]{:S(2)}) collective-permute-start(bf16[2,1152,1152]{2,1,0:T(8,128)(2,1)} %weight_gradient.4.refs_8_), channel_id=1, source_target_pairs={{0,1},{1,0},{2,3},{3,2},{4,5},{5,4},{6,7},{7,6},{8,9},{9,8},{10,11... | collective-permute-start | bytes 15925256 | tf_op jit(solution)/shard_map/ppermute | solution.py:786
  404.9 55.4 %collective-permute-start.1 = (bf16[2,2,144,1152]{3,2,0,1:T(8,128)(2,1)}, bf16[2,2,144,1152]{3,2,0,1:T(8,128)(2,1)}, u32[]{:S(2)}, u32[]{:S(2)}) collective-permute-start(bf16[2,2,144,1152]{3,2,0,1:T(8,128)(2,1)} %bitcast.183), channel_id=1, source_target_pairs={{0,2},{2,0},{1,3},{3,1},{4,6},{6,4},{5,7},{7,5},{8,10},{10,8},{9,1... | collective-permute-start | bytes 3981320 | tf_op jit(solution)/shard_map/ppermute | solution.py:786
  407.5 52.8 %collective-permute-start.2 = (bf16[2,2,144,1152]{3,2,1,0:T(8,128)(2,1)}, bf16[2,2,144,1152]{3,2,1,0:T(8,128)(2,1)}, u32[]{:S(2)}, u32[]{:S(2)}) collective-permute-start(bf16[2,2,144,1152]{3,2,1,0:T(8,128)(2,1)} %dynamic-slice_bitcast_fusion.1.refs_7_), channel_id=1, source_target_pairs={{0,4},{4,0},{1,5},{5,1},{2,6},{6,2},{3,7},{7,3},{8,12},{12,8},{9,1... | collective-permute-start | bytes 3981320 | tf_op jit(solution)/shard_map/ppermute | solution.py:786
  462.1 67.7 %collective-permute-start.4 = (bf16[2,144,1152]{2,1,0:T(8,128)(2,1)S(1)}, bf16[2,144,1152]{2,1,0:T(8,128)(2,1)}, u32[]{:S(2)}, u32[]{:S(2)}) collective-permute-start(bf16[2,144,1152]{2,1,0:T(8,128)(2,1)S(1)} %dynamic-slice_bitcast_fusion.4.refs_5_), channel_id=1, source_target_pairs={{0,2},{2,0},{1,3},{3,1},{4,6},{6,4},{5,7},{7,5},{8,10},{10,8},{9,1... | collective-permute-start | bytes 1990664 | tf_op jit(solution)/shard_map/ppermute | solution.py:786
  465.3 65.8 %collective-permute-start.3 = (bf16[2,144,1152]{2,1,0:T(8,128)(2,1)}, bf16[2,144,1152]{2,1,0:T(8,128)(2,1)}, u32[]{:S(2)}, u32[]{:S(2)}) collective-permute-start(bf16[2,144,1152]{2,1,0:T(8,128)(2,1)} %dynamic-slice_bitcast_fusion.5.refs_4_), channel_id=1, source_target_pairs={{0,4},{4,0},{1,5},{5,1},{2,6},{6,2},{3,7},{7,3},{8,12},{12,8},{9,1... | collective-permute-start | bytes 1990664 | tf_op jit(solution)/shard_map/ppermute | solution.py:786
  480.2 62.2 %collective-permute-start.5 = (bf16[2,1152,1152]{2,1,0:T(8,128)(2,1)}, bf16[2,1152,1152]{2,1,0:T(8,128)(2,1)}, u32[]{:S(2)}, u32[]{:S(2)}) collective-permute-start(bf16[2,1152,1152]{2,1,0:T(8,128)(2,1)} %weight_gradient.6.refs_6_), channel_id=1, source_target_pairs={{0,1},{1,0},{2,3},{3,2},{4,5},{5,4},{6,7},{7,6},{8,9},{9,8},{10,11... | collective-permute-start | bytes 15925256 | tf_op jit(solution)/shard_map/ppermute | solution.py:786
  508.9 19.0 %copy-start.45 = (bf16[4,4,2880]{2,0,1:T(4,128)(2,1)}, bf16[4,4,2880]{2,0,1:T(4,128)(2,1)S(1)}, u32[]{:S(2)}) copy-start(bf16[4,4,2880]{2,0,1:T(4,128)(2,1)S(1)} %copy.398) | copy-start | bytes 276484
  510.0 19.8 %copy-start.10 = (bf16[2,2,144,1152]{3,2,1,0:T(8,128)(2,1)S(1)}, bf16[2,2,144,1152]{3,2,1,0:T(8,128)(2,1)}, u32[]{:S(2)}) copy-start(bf16[2,2,144,1152]{3,2,1,0:T(8,128)(2,1)} %copy-done.9) | copy-start | bytes 3981316
  510.0 30.9 %all-to-all-start.4 = ((bf16[32,4,2880]{2,1,0:T(4,128)(2,1)}), bf16[32,4,2880]{2,1,0:T(4,128)(2,1)}, u32[]{:S(2)}, u32[]{:S(2)}) async-start(bf16[32,4,2880]{2,1,0:T(4,128)(2,1)} %bitcast.44), calls=%async_computation.4 | async-start | bytes 1507328 | tf_op jit(solution)/shard_map/all_to_all | solution.py:1161
  557.4 25.1 %collective-permute-start.10 = (bf16[144,1152]{1,0:T(8,128)(2,1)}, bf16[144,1152]{1,0:T(8,128)(2,1)}, u32[]{:S(2)}, u32[]{:S(2)}) collective-permute-start(bf16[144,1152]{1,0:T(8,128)(2,1)} %get-tuple-element.116), channel_id=1, source_target_pairs={{0,24},{8,0},{16,8},{24,16},{1,25},{9,1},{17,9},{25,17},{2,26},{10... | collective-permute-start | bytes 995336 | tf_op jit(solution)/shard_map/ppermute | solution.py:854
  558.7 23.8 %collective-permute-start.8 = (bf16[144,1152]{1,0:T(8,128)(2,1)}, bf16[144,1152]{1,0:T(8,128)(2,1)}, u32[]{:S(2)}, u32[]{:S(2)}) collective-permute-start(bf16[144,1152]{1,0:T(8,128)(2,1)} %get-tuple-element.114), channel_id=1, source_target_pairs={{0,8},{8,16},{16,24},{24,0},{1,9},{9,17},{17,25},{25,1},{2,10},{10... | collective-permute-start | bytes 995336 | tf_op jit(solution)/shard_map/ppermute | solution.py:854
  559.4 30.1 %collective-permute-start.9 = (bf16[144,1152]{1,0:T(8,128)(2,1)}, bf16[144,1152]{1,0:T(8,128)(2,1)}, u32[]{:S(2)}, u32[]{:S(2)}) collective-permute-start(bf16[144,1152]{1,0:T(8,128)(2,1)} %get-tuple-element.115), channel_id=1, source_target_pairs={{0,16},{8,24},{16,0},{24,8},{1,17},{9,25},{17,1},{25,9},{2,18},{10... | collective-permute-start | bytes 995336 | tf_op jit(solution)/shard_map/ppermute | solution.py:854
  570.0 19.6 %all-to-all-start.5 = ((f32[4,136,144]{2,1,0:T(8,128)}), f32[4,136,144]{2,1,0:T(8,128)}, u32[]{:S(2)}, u32[]{:S(2)}) async-start(f32[4,136,144]{2,1,0:T(8,128)} %broadcast_in_dim.188), calls=%async_computation.6 | async-start | bytes 1114112 | tf_op jit(solution)/shard_map/all_to_all | solution.py:774
  574.2 39.6 %collective-permute-start.7 = (bf16[2,2,144,1152]{3,2,1,0:T(8,128)(2,1)}, bf16[2,2,144,1152]{3,2,1,0:T(8,128)(2,1)}, u32[]{:S(2)}, u32[]{:S(2)}) collective-permute-start(bf16[2,2,144,1152]{3,2,1,0:T(8,128)(2,1)} %dynamic-slice_bitcast_fusion), channel_id=1, source_target_pairs={{0,4},{4,0},{1,5},{5,1},{2,6},{6,2},{3,7},{7,3},{8,12},{12,8},{9,1... | collective-permute-start | bytes 3981320 | tf_op jit(solution)/shard_map/ppermute | solution.py:786
  575.2 41.1 %collective-permute-start.6 = (bf16[2,2,144,1152]{3,2,0,1:T(8,128)(2,1)}, bf16[2,2,144,1152]{3,2,0,1:T(8,128)(2,1)}, u32[]{:S(2)}, u32[]{:S(2)}) collective-permute-start(bf16[2,2,144,1152]{3,2,0,1:T(8,128)(2,1)} %bitcast.223), channel_id=1, source_target_pairs={{0,2},{2,0},{1,3},{3,1},{4,6},{6,4},{5,7},{7,5},{8,10},{10,8},{9,1... | collective-permute-start | bytes 3981320 | tf_op jit(solution)/shard_map/ppermute | solution.py:786
  591.8 31.5 %all-to-all-start.6 = ((f32[8,136,144]{2,1,0:T(8,128)}), f32[8,136,144]{2,1,0:T(8,128)}, u32[]{:S(2)}, u32[]{:S(2)}) async-start(f32[8,136,144]{2,1,0:T(8,128)} %broadcast_in_dim.189), calls=%async_computation.7 | async-start | bytes 2228224 | tf_op jit(solution)/shard_map/all_to_all | solution.py:774
  601.9 14.4 %copy-start.8 = (bf16[1,2,2,144,1152]{4,3,2,1,0:T(8,128)(2,1)S(1)}, bf16[1,2,2,144,1152]{4,3,2,1,0:T(8,128)(2,1)}, u32[]{:S(2)}) copy-start(bf16[1,2,2,144,1152]{4,3,2,1,0:T(8,128)(2,1)} %get-tuple-element.169) | copy-start | bytes 3981316
  626.6 18.8 %collective-permute-start.12 = (bf16[2,144,1152]{2,1,0:T(8,128)(2,1)}, bf16[2,144,1152]{2,1,0:T(8,128)(2,1)}, u32[]{:S(2)}, u32[]{:S(2)}) collective-permute-start(bf16[2,144,1152]{2,1,0:T(8,128)(2,1)} %dynamic-slice_bitcast_fusion.2), channel_id=1, source_target_pairs={{0,2},{2,0},{1,3},{3,1},{4,6},{6,4},{5,7},{7,5},{8,10},{10,8},{9,1... | collective-permute-start | bytes 1990664 | tf_op jit(solution)/shard_map/ppermute | solution.py:786
  628.5 18.5 %collective-permute-start.11 = (bf16[2,144,1152]{2,1,0:T(8,128)(2,1)}, bf16[2,144,1152]{2,1,0:T(8,128)(2,1)}, u32[]{:S(2)}, u32[]{:S(2)}) collective-permute-start(bf16[2,144,1152]{2,1,0:T(8,128)(2,1)} %dynamic-slice_bitcast_fusion.3), channel_id=1, source_target_pairs={{0,4},{4,0},{1,5},{5,1},{2,6},{6,2},{3,7},{7,3},{8,12},{12,8},{9,1... | collective-permute-start | bytes 1990664 | tf_op jit(solution)/shard_map/ppermute | solution.py:786
  630.9 23.3 %all-to-all-start.7 = ((f32[32,1,2084]{2,1,0:T(1,128)}), f32[32,1,2084]{2,1,0:T(1,128)S(1)}, u32[]{:S(2)}, u32[]{:S(2)}) async-start(f32[32,1,2084]{2,1,0:T(1,128)} %all_to_all.44), calls=%async_computation.8 | async-start | bytes 557056 | tf_op jit(solution)/shard_map/all_to_all | solution.py:1232
  649.0 12.7 %collective-permute-start.13 = (bf16[144,1152]{1,0:T(8,128)(2,1)S(1)}, bf16[144,1152]{1,0:T(8,128)(2,1)S(1)}, u32[]{:S(2)}, u32[]{:S(2)}) collective-permute-start(bf16[144,1152]{1,0:T(8,128)(2,1)S(1)} %get-tuple-element.175), channel_id=1, source_target_pairs={{0,8},{8,16},{16,24},{24,0},{1,9},{9,17},{17,25},{25,1},{2,10},{10... | collective-permute-start | bytes 995336 | tf_op jit(solution)/shard_map/ppermute | solution.py:854
  649.5 23.3 %collective-permute-start.14 = (bf16[144,1152]{1,0:T(8,128)(2,1)S(1)}, bf16[144,1152]{1,0:T(8,128)(2,1)S(1)}, u32[]{:S(2)}, u32[]{:S(2)}) collective-permute-start(bf16[144,1152]{1,0:T(8,128)(2,1)S(1)} %get-tuple-element.176), channel_id=1, source_target_pairs={{0,16},{8,24},{16,0},{24,8},{1,17},{9,25},{17,1},{25,9},{2,18},{10... | collective-permute-start | bytes 995336 | tf_op jit(solution)/shard_map/ppermute | solution.py:854
  652.3 20.5 %collective-permute-start.15 = (bf16[144,1152]{1,0:T(8,128)(2,1)S(1)}, bf16[144,1152]{1,0:T(8,128)(2,1)}, u32[]{:S(2)}, u32[]{:S(2)}) collective-permute-start(bf16[144,1152]{1,0:T(8,128)(2,1)S(1)} %get-tuple-element.177), channel_id=1, source_target_pairs={{0,24},{8,0},{16,8},{24,16},{1,25},{9,1},{17,9},{25,17},{2,26},{10... | collective-permute-start | bytes 995336 | tf_op jit(solution)/shard_map/ppermute | solution.py:854
  682.3 32.5 %copy-start.23 = (f32[144,1152]{1,0:T(8,128)S(1)}, f32[144,1152]{1,0:T(8,128)}, u32[]{:S(2)}) copy-start(f32[144,1152]{1,0:T(8,128)} %param.47) | copy-start | bytes 1990660
  682.3 32.5 %copy-start.31 = (bf16[1,144,1152]{2,1,0:T(8,128)(2,1)S(1)}, bf16[1,144,1152]{2,1,0:T(8,128)(2,1)}, u32[]{:S(2)}) copy-start(bf16[1,144,1152]{2,1,0:T(8,128)(2,1)} %reduce-scatter.2.cloned.1.call-done) | copy-start | bytes 995332
  682.3 32.5 %copy-start.49 = (f32[144,1152]{1,0:T(8,128)S(1)}, f32[144,1152]{1,0:T(8,128)}, u32[]{:S(2)}) copy-start(f32[144,1152]{1,0:T(8,128)} %param.49) | copy-start | bytes 1990660
  682.3 32.5 %copy-start.50 = (f32[144,1152]{1,0:T(8,128)S(1)}, f32[144,1152]{1,0:T(8,128)}, u32[]{:S(2)}) copy-start(f32[144,1152]{1,0:T(8,128)} %param.48) | copy-start | bytes 1990660
  682.3 21.9 %all-to-all-start.8 = ((f32[32,1,2482]{2,1,0:T(1,128)}), f32[32,1,2482]{2,1,0:T(1,128)S(1)}, u32[]{:S(2)}, u32[]{:S(2)}) async-start(f32[32,1,2482]{2,1,0:T(1,128)} %broadcast_in_dim.192), calls=%async_computation.9 | async-start | bytes 655360 | tf_op jit(solution)/shard_map/all_to_all | solution.py:774
  (89 other events, 375.5 us)
Sparse Core Ops, SparseCore 0:
  11.5 148.5 all-gather.3
  163.7 102.5 all-gather.5
  383.9 156.2 reduce-scatter.1

commit v3 on v2

--- a/solution.py
+++ b/solution.py
@@ -392,66 +392,61 @@
     sums_ref,
     final_grad_ref,
     output_ref,
-    total_ref,
 ):
-    m, i = pl.program_id(0), pl.program_id(1)
-    last = pl.num_programs(0) - 1
-    total = dot_nt(active_ref[0, 0], block_of(narrow_ref, width))
-
-    @pl.when(m == 0)
-    def begin_total():
-        total_ref[i] = total
-
-    @pl.when((m > 0) & (m < last))
-    def add_total():
-        total_ref[i] += total
-
-    @pl.when(m == last)
-    def finish():
-        branch = total_ref[i] + total + bias_ref[...]
-        gate = mods_ref[0, 5:6]
-        scale = 1.0 + mods_ref[0, 7:8]
-        normed, inverse = norm_of(stream_ref[0] + gate * branch)
-        final_in = (normed * scale + mods_ref[0, 6:7]).astype(jnp.bfloat16)
-        error = dot_nn(final_in, final_ref[...]) + final_bias_ref[...] - target_ref[0]
-        valid = valid_ref[0, :, 0:1]
-        loss = valid * (total_rows(jnp.mean(error * error, -1, keepdims=True)))
-        output_grad = (valid * 2.0 * error / 32.0).astype(jnp.bfloat16)
-        gradient = dot_nt(output_grad, final_ref[...])
-        two = norm_back(normed, inverse, gradient * scale)
-        two_ref[0] = two
-        branch_grad = (gate * two).astype(jnp.bfloat16)
-        branch_grad_ref[0] = branch_grad
-        sums_ref[0, 0:1] = total_rows(gradient)
-        sums_ref[0, 1:2] = total_rows(gradient * normed)
-        sums_ref[0, 2:3] = total_rows(two * branch)
-        sums_ref[0, 3:4] = total_rows(branch_grad.astype(jnp.float32))
-        final_grad_ref[0] = dot_tn(output_grad, final_in)
-        output_ref[0, 0:1] = total_rows(output_grad.astype(jnp.float32))
-        output_ref[0, 1:2] = jnp.broadcast_to(loss, (1, 32))
+    total = None
+    for part in range(active_ref.shape[0]):
+        block = narrow_ref[:, part, :, :width]
+        block = block.reshape(block.shape[0] * block.shape[1], width)
+        product = dot_nt(active_ref[part, 0], block)
+        total = product if total is None else total + product
+    branch = total + bias_ref[...]
+    gate = mods_ref[0, 5:6]
+    scale = 1.0 + mods_ref[0, 7:8]
+    normed, inverse = norm_of(stream_ref[0] + gate * branch)
+    final_in = (normed * scale + mods_ref[0, 6:7]).astype(jnp.bfloat16)
+    error = dot_nn(final_in, final_ref[...]) + final_bias_ref[...] - target_ref[0]
+    valid = valid_ref[0, :, 0:1]
+    loss = valid * (total_rows(jnp.mean(error * error, -1, keepdims=True)))
+    output_grad = (valid * 2.0 * error / 32.0).astype(jnp.bfloat16)
+    gradient = dot_nt(output_grad, final_ref[...])
+    two = norm_back(normed, inverse, gradient * scale)
+    two_ref[0] = two
+    branch_grad = (gate * two).astype(jnp.bfloat16)
+    branch_grad_ref[0] = branch_grad
+    sums_ref[0, 0:1] = total_rows(gradient)
+    sums_ref[0, 1:2] = total_rows(gradient * normed)
+    sums_ref[0, 2:3] = total_rows(two * branch)
+    sums_ref[0, 3:4] = total_rows(branch_grad.astype(jnp.float32))
+    final_grad_ref[0] = dot_tn(output_grad, final_in)
+    output_ref[0, 0:1] = total_rows(output_grad.astype(jnp.float32))
+    output_ref[0, 1:2] = jnp.broadcast_to(loss, (1, 32))
 
 
 def narrow_forward(active, weights, lanes, width, stream, mods, bias, final, final_bias, target, valid):
     parts, images = active.shape[:2]
-    last = parts - 1
-    late = pl.BlockSpec((1, TOKS, D), lambda m, i: (hold(m, last, i), 0, 0))
-    fixed = lambda shape: pl.BlockSpec(shape, lambda m, i: (0,) * len(shape))
-    lately = lambda shape: pl.BlockSpec((1,) + shape, lambda m, i: (hold(m, last, i), 0, 0))
+    groups, _, rows, _ = weights.shape
+    tile = pl.BlockSpec((1, TOKS, D), lambda i: (i, 0, 0))
+    fixed = lambda shape: pl.BlockSpec(shape, lambda i: (0,) * len(shape))
+    each = lambda shape: pl.BlockSpec((1,) + shape, lambda i: (i, 0, 0))
     return pl.pallas_call(
         partial(narrow_kernel, width),
-        grid=(parts, images),
+        grid=(images,),
         in_specs=[
-            pl.BlockSpec((1, 1, TOKS, width), lambda m, i: (m, i, 0, 0)),
-            weight_spec(weights, lanes, 0),
-            late,
-            pl.BlockSpec((1, 8, D), lambda m, i: (i, 0, 0)),
+            pl.BlockSpec((parts, 1, TOKS, width), lambda i: (0, i, 0, 0)),
+            pl.BlockSpec(
+                (groups, parts, rows, lanes),
+                lambda i: (0, 0, 0, 0),
+                pipeline_mode=pl.Buffered(1),
+            ),
+            tile,
+            each((8, D)),
             fixed(bias.shape),
             fixed(final.shape),
             fixed(final_bias.shape),
-            lately((TOKS, 32)),
-            pl.BlockSpec((1, 1, 128), lambda m, i: (i, 0, 0)),
-        ],
-        out_specs=[late, late, lately((4, D)), lately((32, D)), lately((2, 32))],
+            each((TOKS, 32)),
+            each((1, 128)),
+        ],
+        out_specs=[tile, tile, each((4, D)), each((32, D)), each((2, 32))],
         out_shape=[
             jax.ShapeDtypeStruct((images, TOKS, D), jnp.float32),
             jax.ShapeDtypeStruct((images, TOKS, D), jnp.bfloat16),
@@ -459,9 +454,8 @@
             jax.ShapeDtypeStruct((images, 32, D), jnp.float32),
             jax.ShapeDtypeStruct((images, 2, 32), jnp.float32),
         ],
-        scratch_shapes=[pltpu.VMEM((images, TOKS, D), jnp.float32)],
         cost_estimate=cost(images * 2 * TOKS * D * FF, 4e7),
-        compiler_params=params("arbitrary", "arbitrary"),
+        compiler_params=params("arbitrary"),
         name="narrow_forward",
     )(active, weights, stream, mods, bias, final, final_bias, target, valid)
 
@@ -574,70 +568,55 @@
 
 
 def joined_backward_kernel(
-    width,
-    grad_ref,
-    weight_ref,
-    one_ref,
-    zero_ref,
-    mods_ref,
-    embed_ref,
-    sums_ref,
-    embed_grad_ref,
-    total_ref,
+    width, grad_ref, weight_ref, one_ref, zero_ref, mods_ref, embed_ref, sums_ref, embed_grad_ref
 ):
-    m, i = pl.program_id(0), pl.program_id(1)
-    last = pl.num_programs(0) - 1
-    total = dot_nt(grad_ref[0, 0], block_of(weight_ref, width))
-
-    @pl.when(m == 0)
-    def begin_total():
-        total_ref[i] = total
-
-    @pl.when((m > 0) & (m < last))
-    def add_total():
-        total_ref[i] += total
-
-    @pl.when(m == last)
-    def finish():
-        gradient = total_ref[i] + total
-        normed, inverse = norm_of(zero_ref[0])
-        zero = one_ref[0] + norm_back(normed, inverse, gradient * (1.0 + mods_ref[0, 1:2]))
-        sums_ref[0, 0:1] = total_rows(gradient)
-        sums_ref[0, 1:2] = total_rows(gradient * normed)
-        sums_ref[0, 2:3] = total_rows(zero)
-        sums_ref[0, 3:4] = jnp.zeros((1, D), jnp.float32)
-        upper = zero.astype(jnp.bfloat16)
-        lower = (zero - upper.astype(jnp.float32)).astype(jnp.bfloat16)
-        embed_grad_ref[0] = dot_tn(embed_ref[0], upper) + dot_tn(embed_ref[0], lower)
+    gradient = None
+    for part in range(grad_ref.shape[0]):
+        block = weight_ref[:, part, :, :width]
+        block = block.reshape(block.shape[0] * block.shape[1], width)
+        product = dot_nt(grad_ref[part, 0], block)
+        gradient = product if gradient is None else gradient + product
+    normed, inverse = norm_of(zero_ref[0])
+    zero = one_ref[0] + norm_back(normed, inverse, gradient * (1.0 + mods_ref[0, 1:2]))
+    sums_ref[0, 0:1] = total_rows(gradient)
+    sums_ref[0, 1:2] = total_rows(gradient * normed)
+    sums_ref[0, 2:3] = total_rows(zero)
+    sums_ref[0, 3:4] = jnp.zeros((1, D), jnp.float32)
+    upper = zero.astype(jnp.bfloat16)
+    lower = (zero - upper.astype(jnp.float32)).astype(jnp.bfloat16)
+    embed_grad_ref[0] = dot_tn(embed_ref[0], upper) + dot_tn(embed_ref[0], lower)
 
 
 def joined_backward(grad_joined, weights, lanes, one, zero, mods, embed_in, others):
     parts, images, _, width = grad_joined.shape
-    last = parts - 1
-    late = pl.BlockSpec((1, TOKS, D), lambda m, i: (hold(m, last, i), 0, 0))
+    groups, _, rows, _ = weights.shape
+    tile = pl.BlockSpec((1, TOKS, D), lambda i: (i, 0, 0))
     return pl.pallas_call(
         ordered(partial(joined_backward_kernel, width), 6, len(others)),
-        grid=(parts, images),
+        grid=(images,),
         in_specs=[
-            pl.BlockSpec((1, 1, TOKS, width), lambda m, i: (m, i, 0, 0)),
-            weight_spec(weights, lanes, 1),
-            late,
-            late,
-            pl.BlockSpec((1, 8, D), lambda m, i: (i, 0, 0)),
-            pl.BlockSpec((1, TOKS, 16), lambda m, i: (i, 0, 0)),
+            pl.BlockSpec((parts, 1, TOKS, width), lambda i: (0, i, 0, 0)),
+            pl.BlockSpec(
+                (groups, parts, rows, lanes),
+                lambda i: (0, 0, 0, 1),
+                pipeline_mode=pl.Buffered(1),
+            ),
+            tile,
+            tile,
+            pl.BlockSpec((1, 8, D), lambda i: (i, 0, 0)),
+            pl.BlockSpec((1, TOKS, 16), lambda i: (i, 0, 0)),
             *unread(others),
         ],
         out_specs=[
-            pl.BlockSpec((1, 4, D), lambda m, i: (hold(m, last, i), 0, 0)),
-            pl.BlockSpec((1, 16, D), lambda m, i: (hold(m, last, i), 0, 0)),
+            pl.BlockSpec((1, 4, D), lambda i: (i, 0, 0)),
+            pl.BlockSpec((1, 16, D), lambda i: (i, 0, 0)),
         ],
         out_shape=[
             jax.ShapeDtypeStruct((images, 4, D), jnp.float32),
             jax.ShapeDtypeStruct((images, 16, D), jnp.float32),
         ],
-        scratch_shapes=[pltpu.VMEM((images, TOKS, D), jnp.float32)],
         cost_estimate=cost(images * 2 * TOKS * D * 3 * D, 3e7),
-        compiler_params=params("arbitrary", "arbitrary"),
+        compiler_params=params("arbitrary"),
         name="joined_backward",
     )(grad_joined, weights, one, zero, mods, embed_in, *others)
 
@@ -710,7 +689,7 @@
 def whole_gradient(inputs, gradient, groups):
     rows = inputs.shape[0]
     parts, _, width = gradient.shape
-    chunks = 3 if width % 384 == 0 else 1
+    chunks = 1
     piece = width // chunks
     split = groups if (D // groups) % 16 == 0 else 1
     result = pl.pallas_call(
@@ -1166,15 +1145,19 @@
         0,
         0,
         tiled=True,
-    ).reshape(images_all, mod_width)
+    )
     heads_kept = heads_sum.kept_gradient(heads_pairs, [to_owners])
     narrow_sum.open_last()
     narrow_sum.sent, heads_kept = tie(narrow_sum.sent, heads_kept)
     narrow_sum.launch_last()
-    returned, heads_kept, expand_shard = tie(returned, heads_kept, expand_shard)
+    heads_kept, shifts, embed_grads, final_grads = tie(
+        heads_kept, shifts, embed_grads, final_grads
+    )
+    returned, heads_kept = tie(returned, heads_kept)
     heads_sum.open_first(heads_kept)
     heads_sum.sent, returned = tie(heads_sum.sent, returned)
     heads_sum.launch()
+    returned = returned.reshape(images_all, mod_width)
     grad_small = {
         "embed_bias": jnp.sum(sums_a[:, 2], 0),
         "query_bias": jnp.sum(sums[0], 0),
@@ -1210,7 +1193,9 @@
         0,
     )
     grad_act = small_gather(cond_part, mp_axes, mp)
-    grad_act, narrow_sum.arrived = tie(grad_act, narrow_sum.arrived)
+    grad_act, narrow_sum.arrived, expand_shard, grad_small = tie(
+        grad_act, narrow_sum.arrived, expand_shard, grad_small
+    )
     grad_act = jnp.sum(grad_act, 0)
     _, pullback = jax.vjp(jax.nn.silu, condition)
     grad_cond_own = pullback(grad_act)[0]
@@ -1218,8 +1203,8 @@
     timetwo_grad = dot_tn(grad_embed_own, double_rows(hidden_act))
     grad_cond = small_gather(grad_cond_own, dp_axes, dp)
     heads_sum.open_second()
-    heads_sum.sent, grad_cond = tie(heads_sum.sent, grad_cond)
     heads_sum.launch()
+    grad_cond, heads_sum.arrived = tie(grad_cond, heads_sum.arrived)
     grad_cond = (
         grad_cond
         .transpose(1, 0, 2)
@@ -1295,27 +1280,29 @@
     loss_sum = jnp.sum(final[:, ends + 1])
     factor = jnp.minimum(1.0, clip_level / grad_norm)
     token_smalls = final[:, :slice_length].reshape(dp * mp * slice_length)
-    pieces = {"time_bias_two": bias_two_grad / token_count}
-    pieces["cond_bias"] = (
+    cond_bias = (
         final[:, slice_length : slice_length + mod_slice]
         .reshape(dp, mp, mod_slice)
         .transpose(1, 0, 2)
         .reshape(mp, dp * mod_slice)[:, :mod_width]
         .reshape(10 * D)
     )
-    pieces["time_bias_one"] = (
+    time_bias_one = (
         final[:, slice_length + mod_slice : ends]
         .reshape(dp, mp, one_slice)
         .transpose(1, 0, 2)
         .reshape(mp, dp * one_slice)[:, :width_mp]
         .reshape(D)
     )
-    offset = 0
-    for key_name in TOKEN_SMALLS:
-        length = places[key_name][1]
-        pieces[key_name] = token_smalls[offset : offset + length]
-        offset = offset + length
-    small_grad = jnp.concatenate([pieces[key_name] for key_name in places])
+    small_grad = jnp.concatenate(
+        [
+            token_smalls[:D],
+            time_bias_one,
+            bias_two_grad / token_count,
+            cond_bias,
+            token_smalls[D : smalls_weight.shape[0] - 12 * D],
+        ]
+    )
     gradients = owned + [class_grad, small_grad]
     results = [loss_sum, token_count, grad_norm]
     for master, moment, second, gradient in zip(masters, moments, seconds, gradients):

time: 753 us -> 731 us (0.971)
  Pallas kernels: 291 us -> 276 us
  local copies, waits for them, and re-layouts: 97.9 us -> 88.9 us
  waiting for transfers between devices: 170 us -> 162 us
    unnamed x231 -> x249, local copies, waits for them, and re-layouts: 18.5 us -> 15.7 us
  transfers between devices with their start and end apart: 28 -> 28, of which waited for: 13 -> 10; matrix products, arithmetic and copies ran while one was open for 20% -> 20% of each run, Pallas kernels for 38% -> 37%
where the time goes in v3:
time: 731 us; the launch traced here: 720 us
  Pallas kernels  276 us (38%)
  waiting for transfers between devices  162 us (22%)
  local copies, waits for them, and re-layouts  88.9 us (12%)
  other arithmetic  83 us (11%)
  starting transfers between devices  68.7 us (9%)
  between operations  27.3 us (4%)
  matrix products  14.1 us (2%)
    pallas_call x4, Pallas kernels, weight_gradient(): pl.pallas_call(lambda chosen_ref, *refs: kernel(*refs), grid_spec=pltpu.P...  52.6 us
    pallas_call x1, Pallas kernels, feed_backward(): pl.pallas_call(ordered(partial(feed_backward_kernel, width), 8, len(other...  46.1 us
    all_gather x1, waiting for transfers between devices, per_device(): lax.all_gather(shard_one.astype(jnp.bfloat16), all_axes)  44.7 us
    pallas_call x1, Pallas kernels, attention_backward(): pl.pallas_call(ordered(attention_backward_kernel, 6, len(others)), grid=(...  39.3 us
    all_to_all x6, starting transfers between devices, small_gather(): return lax.all_to_all(spread, axes, 0, 0, tiled=True)  37.3 us
    pallas_call x1, Pallas kernels, attention_forward(): pl.pallas_call(partial(attention_forward_kernel, width), grid=(parts, ima...  32.7 us
    pallas_call x1, Pallas kernels, expand_forward(): pl.pallas_call(partial(expand_kernel, width), grid=(parts, images), in_sp...  28.2 us
    all_to_all x1, waiting for transfers between devices, per_device(): lax.all_to_all(outgoing.reshape(dp * mp, own_images, mod_width), all_axes...  28.1 us
  transfers between devices with their start and end apart: 28, of which 10 were waited for; matrix products, arithmetic and copies ran while one was open for 20% of the time, Pallas kernels for 37%

profile of v3, /device:TPU:0, one launch (start us, length us, event | category | flops | bytes accessed | tf_op | source)
XLA Modules:
  0.0 720.0 jit_solution(17361038248307982749)
XLA Ops:
  16.3 7.3 %all-to-all-start = ((bf16[8,2,4658]{2,1,0:T(2,128)(2,1)}), bf16[8,2,4658]{2,1,0:T(2,128)(2,1)S(1)}, u32[]{:S(2)}, u32[]{:S(2)}) async-start(bf16[8,2,4658]{2,1,0:T(2,128)(2,1)} %reshape.564), calls=%async_computation | async-start | bytes 303104 | tf_op jit(solution)/shard_map/all_to_all | solution.py:753
  25.3 2.3 copy.327
  40.8 2.8 multiply_cosine_fusion
  52.6 3.7 all-to-all-start.1
  56.4 3.2 pad_maximum_fusion.table_ref.refs_4_
  59.6 7.3 %all-to-all-done.1 = f32[4,136,144]{2,1,0:T(8,128)S(1)} async-done(((f32[4,136,144]{2,1,0:T(8,128)}), f32[4,136,144]{2,1,0:T(8,128)S(1)}, u32[]{:S(2)}, u32[]{:S(2)}) %all-to-all-start.1) | async-done | bytes 313376 | tf_op jit(solution)/shard_map/all_to_all | solution.py:753
  70.7 4.5 all-to-all-start.2
  78.9 28.1 %all-to-all-done.2 = bf16[32,4,2880]{2,1,0:T(4,128)(2,1)S(1)} async-done(((bf16[32,4,2880]{2,1,0:T(4,128)(2,1)}), bf16[32,4,2880]{2,1,0:T(4,128)(2,1)S(1)}, u32[]{:S(2)}, u32[]{:S(2)}) %all-to-all-start.2) | async-done | bytes 737312 | tf_op jit(solution)/shard_map/all_to_all | solution.py:999
  109.5 5.7 add_convert_fusion.first_ref
  115.3 44.7 %all-gather.4.cloned.1.call-done = bf16[32,144,2304]{2,1,0:T(8,128)(2,1)} async-done(((bf16[1,144,2304]{2,1,0:T(8,128)(2,1)}), bf16[32,144,2304]{2,1,0:T(8,128)(2,1)}) %all-gather.4.cloned.1.call-update) | async-done | bytes 21233680 | tf_op jit(solution)/shard_map/all_gather | solution.py:934
  160.0 5.7 slice.363.weight_ref.refs_1_
  165.7 32.7 %attention_forward.1 = (bf16[4,4,256,864]{3,2,1,0:T(8,128)(2,1)}, bf16[4,4,256,288]{3,2,1,0:T(8,128)(2,1)}, f32[4,4,4,256]{3,2,1,0:T(4,128)}) custom-call(bf16[4,256,1152]{2,1,0:T(8,128)(2,1)} %add_convert_fusion.first_ref, bf16[8,4,144,2304]{3,2,1,0:T(8,128)(2,1)} %bitcast.192, f32[4,4,1,864]{3,2,1,0:T(1,128)} %broadcast_in_dim.96.added_ref, ...), custom_call_target="tpu_custom_call" | custom-call | flops 10301210624 | bytes 30000000 | tf_op jit(solution)/shard_map/attention_forward/pallas_call | solution.py:206
  198.5 11.5 %mixback_forward.1 = (bf16[4,256,1152]{2,1,0:T(8,128)(2,1)}, f32[4,256,1152]{2,1,0:T(8,128)}, bf16[4,256,1152]{2,1,0:T(8,128)(2,1)}) custom-call(bf16[4,4,256,288]{3,2,1,0:T(8,128)(2,1)} %get-tuple-element.93.mixed_ref, bf16[8,4,144,288]{3,2,1,0:T(8,128)(2,1)} %slice.363.weight_ref.refs_1_, f32[4,256,1152]{2,1,0:T(8,128)} %copy-done, ...), custom_call_target="tpu_custom_call" | custom-call | flops 2717908992 | bytes 16515072 | tf_op jit(solution)/shard_map/mixback_forward/pallas_call | solution.py:326
  211.0 3.7 all-to-all-start.3
  215.1 28.2 %expand_forward.1 = (bf16[4,4,256,1152]{3,2,1,0:T(8,128)(2,1)}, bf16[4,4,256,1152]{3,2,1,0:T(8,128)(2,1)}) custom-call(bf16[4,256,1152]{2,1,0:T(8,128)(2,1)} %get-tuple-element.96.second_ref, bf16[8,4,144,2304]{3,2,1,0:T(8,128)(2,1)} %bitcast.193, f32[4,1,1152]{2,1,0:T(1,128)} %reshape.511.bias_ref), custom_call_target="tpu_custom_call" | custom-call | flops 10871635968 | bytes 30000000 | tf_op jit(solution)/shard_map/expand_forward/pallas_call | solution.py:363
  243.3 22.6 %all-gather.6.cloned.1.call-done = bf16[4608,1152]{1,0:T(8,128)(2,1)} async-done(((bf16[144,1152]{1,0:T(8,128)(2,1)}), bf16[4608,1152]{1,0:T(8,128)(2,1)}) %all-gather.6.cloned.1.call-update) | async-done | bytes 10616848 | tf_op jit(solution)/shard_map/all_gather | solution.py:936
  266.6 27.1 %narrow_forward.1 = (f32[4,256,1152]{2,1,0:T(8,128)}, bf16[4,256,1152]{2,1,0:T(8,128)(2,1)}, f32[4,4,1152]{2,1,0:T(4,128)}, f32[4,32,1152]{2,1,0:T(8,128)}, f32[4,2,32]{2,1,0:T(2,128)}) custom-call(bf16[4,4,256,1152]{3,2,1,0:T(8,128)(2,1)} %get-tuple-element.97.active_ref, bf16[8,4,144,1152]{3,2,1,0:T(8,128)(2,1)} %bitcast.241, ...), custom_call_target="tpu_custom_call" | custom-call | flops 10871635968 | bytes 40000000 | tf_op jit(solution)/shard_map/narrow_forward/pallas_call | solution.py:431
  293.9 11.4 %weight_gradient.4.refs_8_ = bf16[2,1152,1152]{2,1,0:T(8,128)(2,1)} custom-call(s32[1]{0:T(128)S(6)} %sub.190.chosen_ref, bf16[1024,1152]{1,0:T(8,128)(2,1)} %bitcast.212, bf16[4,1024,1152]{2,1,0:T(8,128)(2,1)} %bitcast.204), custom_call_target="tpu_custom_call" | custom-call | flops 5435817984 | bytes 7077888 | tf_op jit(solution)/shard_map/weight_gradient/pallas_call | solution.py:663
  311.9 46.1 %feed_backward.1 = (bf16[4,4,256,1152]{3,2,1,0:T(8,128)(2,1)}, f32[4,1,1152]{2,1,0:T(1,128)}, f32[4,256,1152]{2,1,0:T(8,128)}, bf16[4,256,1152]{2,1,0:T(8,128)(2,1)}, f32[4,4,1152]{2,1,0:T(4,128)}) custom-call(bf16[4,256,1152]{2,1,0:T(8,128)(2,1)} %get-tuple-element.100.refs_0_, bf16[8,4,144,2304]{3,2,1,0:T(8,128)(2,1)} %bitcast.194, ...), custom_call_target="tpu_custom_call" | custom-call | flops 21743271936 | bytes 60000000 | tf_op jit(solution)/shard_map/feed_backward/pallas_call | solution.py:535
  358.8 17.7 %whole_gradient.1 = bf16[8,4,144,1152]{3,2,1,0:T(8,128)(2,1)} custom-call(bf16[1024,1152]{1,0:T(8,128)(2,1)} %bitcast.243, bf16[4,1024,1152]{2,1,0:T(8,128)(2,1)} %bitcast.244), custom_call_target="tpu_custom_call" | custom-call | flops 10871635968 | bytes 11796480 | tf_op jit(solution)/shard_map/whole_gradient/pallas_call | solution.py:695
  378.0 12.0 %weight_gradient.5 = bf16[2,1152,1152]{2,1,0:T(8,128)(2,1)} custom-call(s32[1]{0:T(128)} %bitcast.chosen_ref, bf16[1024,1152]{1,0:T(8,128)(2,1)} %bitcast.213, bf16[4,1024,1152]{2,1,0:T(8,128)(2,1)} %bitcast.205, bf16[2,1152,1152]{2,1,0:T(8,128)(2,1)} %collective-permute-done.refs_2_, bf16[32,144,1152]{2,1,0:T(8,128)(2,1)} %bitcast.190), custom_call_target="tpu_custom_call" | custom-call | flops 5435817984 | bytes 7077888 | tf_op jit(solution)/shard_map/weight_gradient/pallas_call | solution.py:663
  390.0 3.2 fusion.113
  401.4 39.3 %attention_backward.1 = (bf16[4,4,256,864]{3,2,1,0:T(8,128)(2,1)}, f32[4,4,8,864]{3,2,1,0:T(8,128)}, f32[16,256,104]{2,1,0:T(8,128)}) custom-call(bf16[4,256,1152]{2,1,0:T(8,128)(2,1)} %get-tuple-element.105.refs_0_, bf16[8,4,144,288]{3,2,1,0:T(8,128)(2,1)} %slice.363.weight_ref.refs_1_, bf16[4,4,256,864]{3,2,1,0:T(8,128)(2,1)} %get-tuple-element.106.refs_2_, ...), custom_call_target="tpu_custom_call" | custom-call | flops 8086618112 | bytes 50000000 | tf_op jit(solution)/shard_map/attention_backward/pallas_call | solution.py:279
  450.4 14.2 %weight_gradient.6.refs_6_ = bf16[2,1152,1152]{2,1,0:T(8,128)(2,1)} custom-call(s32[1]{0:T(128)S(6)} %sub.190.chosen_ref, bf16[1024,1152]{1,0:T(8,128)(2,1)} %bitcast.200, bf16[1024,1152]{1,0:T(8,128)(2,1)} %bitcast.202, bf16[4,1024,864]{2,1,0:T(8,128)(2,1)} %bitcast.187, bf16[4,1024,288]{2,1,0:T(8,128)(2,1)} %bitcast.196, ...), custom_call_target="tpu_custom_call" | custom-call | flops 5435817984 | bytes 7077888 | tf_op jit(solution)/shard_map/weight_gradient/pallas_call | solution.py:663
  464.6 20.9 %joined_backward.1 = (f32[4,4,1152]{2,1,0:T(4,128)}, f32[4,16,1152]{2,1,0:T(8,128)}) custom-call(bf16[4,4,256,864]{3,2,1,0:T(8,128)(2,1)} %get-tuple-element.109.refs_0_, bf16[8,4,144,2304]{3,2,1,0:T(8,128)(2,1)} %bitcast.195, f32[4,256,1152]{2,1,0:T(8,128)} %get-tuple-element.110.refs_2_, f32[4,256,1152]{2,1,0:T(8,128)} %copy-done, ...), custom_call_target="tpu_custom_call" | custom-call | flops 8153726976 | bytes 30000000 | tf_op jit(solution)/shard_map/joined_backward/pallas_call | solution.py:594
  487.9 4.0 all-to-all-start.4
  498.4 15.0 %weight_gradient.7 = bf16[2,1152,1152]{2,1,0:T(8,128)(2,1)} custom-call(s32[1]{0:T(128)} %bitcast.chosen_ref, bf16[1024,1152]{1,0:T(8,128)(2,1)} %bitcast.201, bf16[1024,1152]{1,0:T(8,128)(2,1)} %bitcast.203, bf16[4,1024,864]{2,1,0:T(8,128)(2,1)} %bitcast.188, bf16[4,1024,288]{2,1,0:T(8,128)(2,1)} %bitcast.197, ...), custom_call_target="tpu_custom_call" | custom-call | flops 5435817984 | bytes 7077888 | tf_op jit(solution)/shard_map/weight_gradient/pallas_call | solution.py:663
  513.4 7.1 all-to-all-done.4
  520.5 3.2 fusion.112
  545.7 4.3 all-to-all-start.5
  552.2 2.3 collective-permute-start.8
  557.5 3.4 multiply_reduce_fusion.1
  566.5 10.2 %collective-permute-done.7 = bf16[144,1152]{1,0:T(8,128)(2,1)S(1)} collective-permute-done((bf16[144,1152]{1,0:T(8,128)(2,1)}, bf16[144,1152]{1,0:T(8,128)(2,1)S(1)}, u32[]{:S(2)}, u32[]{:S(2)}) %collective-permute-start.7) | collective-permute-done | bytes 331808 | tf_op jit(solution)/shard_map/ppermute | solution.py:833
  579.1 9.1 %all-to-all-start.6 = ((f32[8,136,144]{2,1,0:T(8,128)}), f32[8,136,144]{2,1,0:T(8,128)}, u32[]{:S(2)}, u32[]{:S(2)}) async-start(f32[8,136,144]{2,1,0:T(8,128)} %broadcast_in_dim.189), calls=%async_computation.7 | async-start | bytes 2228224 | tf_op jit(solution)/shard_map/all_to_all | solution.py:753
  591.0 2.0 collective-permute-start.10
  594.3 2.3 concatenate.133
  597.5 2.5 multiply_reduce_fusion.6
  600.8 2.7 multiply_reduce_fusion.3
  603.6 13.5 %collective-permute-done.10 = bf16[2,144,1152]{2,1,0:T(8,128)(2,1)} collective-permute-done((bf16[2,144,1152]{2,1,0:T(8,128)(2,1)}, bf16[2,144,1152]{2,1,0:T(8,128)(2,1)}, u32[]{:S(2)}, u32[]{:S(2)}) %collective-permute-start.10) | collective-permute-done | bytes 663584 | tf_op jit(solution)/shard_map/ppermute | solution.py:765
  632.9 2.6 all-to-all-start.7
  636.2 2.9 multiply_reduce_fusion.2
  641.4 11.5 %collective-permute-done.14 = bf16[144,1152]{1,0:T(8,128)(2,1)S(1)} collective-permute-done((bf16[144,1152]{1,0:T(8,128)(2,1)S(1)}, bf16[144,1152]{1,0:T(8,128)(2,1)S(1)}, u32[]{:S(2)}, u32[]{:S(2)}) %collective-permute-start.14) | collective-permute-done | bytes 331808 | tf_op jit(solution)/shard_map/ppermute | solution.py:833
  660.9 4.6 all-to-all-done.7
  668.7 9.3 %all-to-all-start.8 = ((f32[32,1,2482]{2,1,0:T(1,128)}), f32[32,1,2482]{2,1,0:T(1,128)S(1)}, u32[]{:S(2)}, u32[]{:S(2)}) async-start(f32[32,1,2482]{2,1,0:T(1,128)} %broadcast_in_dim.192), calls=%async_computation.9 | async-start | bytes 655360 | tf_op jit(solution)/shard_map/all_to_all | solution.py:753
  678.0 12.0 %all-to-all-done.8 = f32[32,1,2482]{2,1,0:T(1,128)S(1)} async-done(((f32[32,1,2482]{2,1,0:T(1,128)}), f32[32,1,2482]{2,1,0:T(1,128)S(1)}, u32[]{:S(2)}, u32[]{:S(2)}) %all-to-all-start.8) | async-done | bytes 317728 | tf_op jit(solution)/shard_map/all_to_all | solution.py:753
  692.3 2.8 multiply_subtract_fusion.3
  700.2 2.4 multiply_subtract_fusion.1
  704.5 3.2 multiply_subtract_fusion
  (526 shorter events, 153.6 us)
Async XLA Ops:
  7.2 152.8 %all-gather.4.cloned.1.call-start = ((), (), s32[]{:S(2)}) async-start(), calls=%async_computation.10 | async-start | bytes 21897216 | tf_op jit(solution)/shard_map/all_gather | solution.py:934
  10.7 12.8 %copy-start.25 = (f32[80512]{0:T(1024)S(1)}, f32[80512]{0:T(1024)}, u32[]{:S(2)}) copy-start(f32[80512]{0:T(1024)} %param.65) | copy-start | bytes 966148
  10.7 13.8 %copy-start.43 = (f32[144,288]{1,0:T(8,128)S(1)}, f32[144,288]{1,0:T(8,128)}, u32[]{:S(2)}) copy-start(f32[144,288]{1,0:T(8,128)} %param.56) | copy-start | bytes 497668
  10.7 255.2 %all-gather.6.cloned.1.call-start = ((), (), s32[]{:S(2)}) async-start(), calls=%async_computation.12 | async-start | bytes 10948608 | tf_op jit(solution)/shard_map/all_gather | solution.py:936
  11.6 13.1 %copy-start.66 = (f32[4,4,1024]{2,1,0:T(4,128)S(1)}, f32[4,4,1024]{2,1,0:T(4,128)}, u32[]{:S(2)}) copy-start(f32[4,4,1024]{2,1,0:T(4,128)} %param.35) | copy-start | bytes 196612
  11.6 13.1 %copy-start.86 = (f32[4,4,1024]{2,1,0:T(4,128)S(1)}, f32[4,4,1024]{2,1,0:T(4,128)}, u32[]{:S(2)}) copy-start(f32[4,4,1024]{2,1,0:T(4,128)} %param.34) | copy-start | bytes 196612
  16.3 31.8 %all-to-all-start = ((bf16[8,2,4658]{2,1,0:T(2,128)(2,1)}), bf16[8,2,4658]{2,1,0:T(2,128)(2,1)S(1)}, u32[]{:S(2)}, u32[]{:S(2)}) async-start(bf16[8,2,4658]{2,1,0:T(2,128)(2,1)} %reshape.564), calls=%async_computation | async-start | bytes 303104 | tf_op jit(solution)/shard_map/all_to_all | solution.py:753
  24.5 26.5 %copy-start.37 = (bf16[144,288]{1,0:T(8,128)(2,1)}, bf16[144,288]{1,0:T(8,128)(2,1)S(1)}, u32[]{:S(2)}) copy-start(bf16[144,288]{1,0:T(8,128)(2,1)S(1)} %convert_element_type.275) | copy-start | bytes 248836
  40.1 27.4 %copy-start.101 = (f32[144]{0:T(256)}, f32[144]{0:T(256)S(1)}, u32[]{:S(2)}) copy-start(f32[144]{0:T(256)S(1)} %dynamic_slice.107) | copy-start | bytes 1732
  52.6 14.3 %all-to-all-start.1 = ((f32[4,136,144]{2,1,0:T(8,128)}), f32[4,136,144]{2,1,0:T(8,128)S(1)}, u32[]{:S(2)}, u32[]{:S(2)}) async-start(f32[4,136,144]{2,1,0:T(8,128)} %broadcast_in_dim.92), calls=%async_computation.1 | async-start | bytes 1114112 | tf_op jit(solution)/shard_map/all_to_all | solution.py:753
  56.3 13.0 %copy-start.89 = (pred[2880]{0:T(1024)(128)(4,1)}, pred[2880]{0:T(1024)(128)(4,1)S(1)}, u32[]{:S(2)}) copy-start(pred[2880]{0:T(1024)(128)(4,1)S(1)} %add_compare_fusion) | copy-start | bytes 8644
  68.6 242.0 %copy-start.63 = (bf16[136,144]{1,0:T(8,128)(2,1)}, bf16[136,144]{1,0:T(8,128)(2,1)S(1)}, u32[]{:S(2)}) copy-start(bf16[136,144]{1,0:T(8,128)(2,1)S(1)} %multiply_convert_fusion.1) | copy-start | bytes 117508
  70.7 36.2 %all-to-all-start.2 = ((bf16[32,4,2880]{2,1,0:T(4,128)(2,1)}), bf16[32,4,2880]{2,1,0:T(4,128)(2,1)S(1)}, u32[]{:S(2)}, u32[]{:S(2)}) async-start(bf16[32,4,2880]{2,1,0:T(4,128)(2,1)} %select_convert_fusion), calls=%async_computation.2 | async-start | bytes 1507328 | tf_op jit(solution)/shard_map/all_to_all | solution.py:999
  78.9 28.8 %copy-start.97 = (f32[1152]{0:T(1024)S(1)}, f32[1152]{0:T(1024)}, u32[]{:S(2)}) copy-start(f32[1152]{0:T(1024)} %get-tuple-element.218) | copy-start | bytes 13828
  78.9 29.0 %copy-start.112 = (f32[3]{0:T(128)S(1)}, f32[3]{0:T(128)}, u32[]{:S(2)}) copy-start(f32[3]{0:T(128)} %pad.43.clone) | copy-start | bytes 40
  211.0 82.8 %all-to-all-start.3 = ((bf16[8,144,288]{2,1,0:T(8,128)(2,1)}), bf16[8,144,288]{2,1,0:T(8,128)(2,1)S(1)}, u32[]{:S(2)}, u32[]{:S(2)}) async-start(bf16[8,144,288]{2,1,0:T(8,128)(2,1)} %broadcast_in_dim.102), calls=%async_computation.3 | async-start | bytes 1769472 | tf_op jit(solution)/shard_map/all_to_all | solution.py:753
  214.7 362.0 %reduce-scatter.2.cloned.1.call-start = ((), (), s32[]{:S(2)}) async-start(), calls=%async_computation.11 | async-start | bytes 10948608 | tf_op jit(solution)/shard_map/reduce_scatter | solution.py:1097
  293.8 13.9 %copy-start.77 = (bf16[136,128]{1,0:T(8,128)(2,1)S(1)}, bf16[136,128]{1,0:T(8,128)(2,1)}, u32[]{:S(2)}) copy-start(bf16[136,128]{1,0:T(8,128)(2,1)} %copy-done.76) | copy-start | bytes 104452
  293.8 13.9 %copy-start.79 = (bf16[136,128]{1,0:T(8,128)(2,1)S(1)}, bf16[136,128]{1,0:T(8,128)(2,1)}, u32[]{:S(2)}) copy-start(bf16[136,128]{1,0:T(8,128)(2,1)} %copy-done.78) | copy-start | bytes 104452
  293.8 16.0 %copy-start.107 = (f32[128]{0:T(128)S(1)}, f32[128]{0:T(128)}, u32[]{:S(2)}) copy-start(f32[128]{0:T(128)} %copy-done.106) | copy-start | bytes 1540
  293.8 16.8 %copy-start.84 = (f32[4,4,1152]{2,1,0:T(4,128)S(1)}, f32[4,4,1152]{2,1,0:T(4,128)}, u32[]{:S(2)}) copy-start(f32[4,4,1152]{2,1,0:T(4,128)} %get-tuple-element.115) | copy-start | bytes 221188
  293.8 16.8 %copy-start.110 = (f32[4,2,32]{2,1,0:T(2,128)S(1)}, f32[4,2,32]{2,1,0:T(2,128)}, u32[]{:S(2)}) copy-start(f32[4,2,32]{2,1,0:T(2,128)} %get-tuple-element.130) | copy-start | bytes 3076
  305.3 72.7 %collective-permute-start = (bf16[2,1152,1152]{2,1,0:T(8,128)(2,1)}, bf16[2,1152,1152]{2,1,0:T(8,128)(2,1)}, u32[]{:S(2)}, u32[]{:S(2)}) collective-permute-start(bf16[2,1152,1152]{2,1,0:T(8,128)(2,1)} %weight_gradient.4.refs_8_), channel_id=1, source_target_pairs={{0,1},{1,0},{2,3},{3,2},{4,5},{5,4},{6,7},{7,6},{8,9},{9,8},{10,11... | collective-permute-start | bytes 15925256 | tf_op jit(solution)/shard_map/ppermute | solution.py:765
  395.8 48.1 %collective-permute-start.1 = (bf16[2,2,144,1152]{3,2,0,1:T(8,128)(2,1)}, bf16[2,2,144,1152]{3,2,0,1:T(8,128)(2,1)}, u32[]{:S(2)}, u32[]{:S(2)}) collective-permute-start(bf16[2,2,144,1152]{3,2,0,1:T(8,128)(2,1)} %bitcast.181), channel_id=1, source_target_pairs={{0,2},{2,0},{1,3},{3,1},{4,6},{6,4},{5,7},{7,5},{8,10},{10,8},{9,1... | collective-permute-start | bytes 3981320 | tf_op jit(solution)/shard_map/ppermute | solution.py:765
  398.4 45.5 %collective-permute-start.2 = (bf16[2,2,144,1152]{3,2,1,0:T(8,128)(2,1)}, bf16[2,2,144,1152]{3,2,1,0:T(8,128)(2,1)}, u32[]{:S(2)}, u32[]{:S(2)}) collective-permute-start(bf16[2,2,144,1152]{3,2,1,0:T(8,128)(2,1)} %dynamic-slice_bitcast_fusion.1.refs_7_), channel_id=1, source_target_pairs={{0,4},{4,0},{1,5},{5,1},{2,6},{6,2},{3,7},{7,3},{8,12},{12,8},{9,1... | collective-permute-start | bytes 3981320 | tf_op jit(solution)/shard_map/ppermute | solution.py:765
  446.7 46.8 %collective-permute-start.4 = (bf16[2,144,1152]{2,1,0:T(8,128)(2,1)}, bf16[2,144,1152]{2,1,0:T(8,128)(2,1)}, u32[]{:S(2)}, u32[]{:S(2)}) collective-permute-start(bf16[2,144,1152]{2,1,0:T(8,128)(2,1)} %dynamic-slice_bitcast_fusion.4.refs_5_), channel_id=1, source_target_pairs={{0,2},{2,0},{1,3},{3,1},{4,6},{6,4},{5,7},{7,5},{8,10},{10,8},{9,1... | collective-permute-start | bytes 1990664 | tf_op jit(solution)/shard_map/ppermute | solution.py:765
  449.8 45.1 %collective-permute-start.3 = (bf16[2,144,1152]{2,1,0:T(8,128)(2,1)}, bf16[2,144,1152]{2,1,0:T(8,128)(2,1)}, u32[]{:S(2)}, u32[]{:S(2)}) collective-permute-start(bf16[2,144,1152]{2,1,0:T(8,128)(2,1)} %dynamic-slice_bitcast_fusion.5.refs_4_), channel_id=1, source_target_pairs={{0,4},{4,0},{1,5},{5,1},{2,6},{6,2},{3,7},{7,3},{8,12},{12,8},{9,1... | collective-permute-start | bytes 1990664 | tf_op jit(solution)/shard_map/ppermute | solution.py:765
  464.6 33.8 %collective-permute-start.5 = (bf16[2,1152,1152]{2,1,0:T(8,128)(2,1)}, bf16[2,1152,1152]{2,1,0:T(8,128)(2,1)}, u32[]{:S(2)}, u32[]{:S(2)}) collective-permute-start(bf16[2,1152,1152]{2,1,0:T(8,128)(2,1)} %weight_gradient.6.refs_6_), channel_id=1, source_target_pairs={{0,1},{1,0},{2,3},{3,2},{4,5},{5,4},{6,7},{7,6},{8,9},{9,8},{10,11... | collective-permute-start | bytes 15925256 | tf_op jit(solution)/shard_map/ppermute | solution.py:765
  487.9 32.5 %all-to-all-start.4 = ((bf16[32,4,2880]{2,1,0:T(4,128)(2,1)}), bf16[32,4,2880]{2,1,0:T(4,128)(2,1)S(1)}, u32[]{:S(2)}, u32[]{:S(2)}) async-start(bf16[32,4,2880]{2,1,0:T(4,128)(2,1)} %bitcast.210), calls=%async_computation.4 | async-start | bytes 1507328 | tf_op jit(solution)/shard_map/all_to_all | solution.py:1140
  527.3 33.6 %collective-permute-start.11 = (bf16[2,2,144,1152]{3,2,1,0:T(8,128)(2,1)}, bf16[2,2,144,1152]{3,2,1,0:T(8,128)(2,1)}, u32[]{:S(2)}, u32[]{:S(2)}) collective-permute-start(bf16[2,2,144,1152]{3,2,1,0:T(8,128)(2,1)} %dynamic-slice_bitcast_fusion), channel_id=1, source_target_pairs={{0,4},{4,0},{1,5},{5,1},{2,6},{6,2},{3,7},{7,3},{8,12},{12,8},{9,1... | collective-permute-start | bytes 3981320 | tf_op jit(solution)/shard_map/ppermute | solution.py:765
  528.7 59.6 %collective-permute-start.9 = (bf16[2,2,144,1152]{3,2,0,1:T(8,128)(2,1)}, bf16[2,2,144,1152]{3,2,0,1:T(8,128)(2,1)}, u32[]{:S(2)}, u32[]{:S(2)}) collective-permute-start(bf16[2,2,144,1152]{3,2,0,1:T(8,128)(2,1)} %bitcast.180), channel_id=1, source_target_pairs={{0,2},{2,0},{1,3},{3,1},{4,6},{6,4},{5,7},{7,5},{8,10},{10,8},{9,1... | collective-permute-start | bytes 3981320 | tf_op jit(solution)/shard_map/ppermute | solution.py:765
  545.7 20.8 %all-to-all-start.5 = ((f32[4,136,144]{2,1,0:T(8,128)}), f32[4,136,144]{2,1,0:T(8,128)}, u32[]{:S(2)}, u32[]{:S(2)}) async-start(f32[4,136,144]{2,1,0:T(8,128)} %broadcast_in_dim.188), calls=%async_computation.5 | async-start | bytes 1114112 | tf_op jit(solution)/shard_map/all_to_all | solution.py:753
  550.5 16.0 %collective-permute-start.6 = (bf16[144,1152]{1,0:T(8,128)(2,1)}, bf16[144,1152]{1,0:T(8,128)(2,1)S(1)}, u32[]{:S(2)}, u32[]{:S(2)}) collective-permute-start(bf16[144,1152]{1,0:T(8,128)(2,1)} %get-tuple-element.125), channel_id=1, source_target_pairs={{0,8},{8,16},{16,24},{24,0},{1,9},{9,17},{17,25},{25,1},{2,10},{10... | collective-permute-start | bytes 995336 | tf_op jit(solution)/shard_map/ppermute | solution.py:833
  550.7 26.0 %collective-permute-start.7 = (bf16[144,1152]{1,0:T(8,128)(2,1)}, bf16[144,1152]{1,0:T(8,128)(2,1)S(1)}, u32[]{:S(2)}, u32[]{:S(2)}) collective-permute-start(bf16[144,1152]{1,0:T(8,128)(2,1)} %get-tuple-element.126), channel_id=1, source_target_pairs={{0,16},{8,24},{16,0},{24,8},{1,17},{9,25},{17,1},{25,9},{2,18},{10... | collective-permute-start | bytes 995336 | tf_op jit(solution)/shard_map/ppermute | solution.py:833
  552.2 24.5 %collective-permute-start.8 = (bf16[144,1152]{1,0:T(8,128)(2,1)}, bf16[144,1152]{1,0:T(8,128)(2,1)}, u32[]{:S(2)}, u32[]{:S(2)}) collective-permute-start(bf16[144,1152]{1,0:T(8,128)(2,1)} %get-tuple-element.127), channel_id=1, source_target_pairs={{0,24},{8,0},{16,8},{24,16},{1,25},{9,1},{17,9},{25,17},{2,26},{10... | collective-permute-start | bytes 995336 | tf_op jit(solution)/shard_map/ppermute | solution.py:833
  563.6 14.3 %copy-start.32 = (f32[136,144]{1,0:T(8,128)S(1)}, f32[136,144]{1,0:T(8,128)}, u32[]{:S(2)}) copy-start(f32[136,144]{1,0:T(8,128)} %reduce_sum.319) | copy-start | bytes 235012
  563.6 14.3 %copy-start.102 = (f32[144]{0:T(256)S(1)}, f32[144]{0:T(256)}, u32[]{:S(2)}) copy-start(f32[144]{0:T(256)} %copy-done.101) | copy-start | bytes 1732
  564.5 39.0 %collective-permute-start.12 = (bf16[2,144,1152]{2,1,0:T(8,128)(2,1)}, bf16[2,144,1152]{2,1,0:T(8,128)(2,1)}, u32[]{:S(2)}, u32[]{:S(2)}) collective-permute-start(bf16[2,144,1152]{2,1,0:T(8,128)(2,1)} %dynamic-slice_bitcast_fusion.2), channel_id=1, source_target_pairs={{0,2},{2,0},{1,3},{3,1},{4,6},{6,4},{5,7},{7,5},{8,10},{10,8},{9,1... | collective-permute-start | bytes 1990664 | tf_op jit(solution)/shard_map/ppermute | solution.py:765
  579.1 38.0 %all-to-all-start.6 = ((f32[8,136,144]{2,1,0:T(8,128)}), f32[8,136,144]{2,1,0:T(8,128)}, u32[]{:S(2)}, u32[]{:S(2)}) async-start(f32[8,136,144]{2,1,0:T(8,128)} %broadcast_in_dim.189), calls=%async_computation.7 | async-start | bytes 2228224 | tf_op jit(solution)/shard_map/all_to_all | solution.py:753
  591.0 26.1 %collective-permute-start.10 = (bf16[2,144,1152]{2,1,0:T(8,128)(2,1)}, bf16[2,144,1152]{2,1,0:T(8,128)(2,1)}, u32[]{:S(2)}, u32[]{:S(2)}) collective-permute-start(bf16[2,144,1152]{2,1,0:T(8,128)(2,1)} %dynamic-slice_bitcast_fusion.3), channel_id=1, source_target_pairs={{0,4},{4,0},{1,5},{5,1},{2,6},{6,2},{3,7},{7,3},{8,12},{12,8},{9,1... | collective-permute-start | bytes 1990664 | tf_op jit(solution)/shard_map/ppermute | solution.py:765
  626.8 14.7 %collective-permute-start.13 = (bf16[144,1152]{1,0:T(8,128)(2,1)}, bf16[144,1152]{1,0:T(8,128)(2,1)S(1)}, u32[]{:S(2)}, u32[]{:S(2)}) collective-permute-start(bf16[144,1152]{1,0:T(8,128)(2,1)} %get-tuple-element.205), channel_id=1, source_target_pairs={{0,8},{8,16},{16,24},{24,0},{1,9},{9,17},{17,25},{25,1},{2,10},{10... | collective-permute-start | bytes 995336 | tf_op jit(solution)/shard_map/ppermute | solution.py:833
  628.7 24.3 %collective-permute-start.14 = (bf16[144,1152]{1,0:T(8,128)(2,1)S(1)}, bf16[144,1152]{1,0:T(8,128)(2,1)S(1)}, u32[]{:S(2)}, u32[]{:S(2)}) collective-permute-start(bf16[144,1152]{1,0:T(8,128)(2,1)S(1)} %get-tuple-element.206), channel_id=1, source_target_pairs={{0,16},{8,24},{16,0},{24,8},{1,17},{9,25},{17,1},{25,9},{2,18},{10... | collective-permute-start | bytes 995336 | tf_op jit(solution)/shard_map/ppermute | solution.py:833
  630.6 23.1 %collective-permute-start.15 = (bf16[144,1152]{1,0:T(8,128)(2,1)S(1)}, bf16[144,1152]{1,0:T(8,128)(2,1)}, u32[]{:S(2)}, u32[]{:S(2)}) collective-permute-start(bf16[144,1152]{1,0:T(8,128)(2,1)S(1)} %get-tuple-element.207), channel_id=1, source_target_pairs={{0,24},{8,0},{16,8},{24,16},{1,25},{9,1},{17,9},{25,17},{2,26},{10... | collective-permute-start | bytes 995336 | tf_op jit(solution)/shard_map/ppermute | solution.py:833
  632.9 32.6 %all-to-all-start.7 = ((f32[32,1,2084]{2,1,0:T(1,128)}), f32[32,1,2084]{2,1,0:T(1,128)S(1)}, u32[]{:S(2)}, u32[]{:S(2)}) async-start(f32[32,1,2084]{2,1,0:T(1,128)} %all_to_all.44), calls=%async_computation.8 | async-start | bytes 557056 | tf_op jit(solution)/shard_map/all_to_all | solution.py:1217
  641.4 24.3 %copy-start.104 = (f32[360]{0:T(512)S(1)}, f32[360]{0:T(512)}, u32[]{:S(2)}) copy-start(f32[360]{0:T(512)} %dynamic_slice.125) | copy-start | bytes 4324
  668.7 23.5 %copy-start.23 = (f32[144,1152]{1,0:T(8,128)S(1)}, f32[144,1152]{1,0:T(8,128)}, u32[]{:S(2)}) copy-start(f32[144,1152]{1,0:T(8,128)} %param.47) | copy-start | bytes 1990660
  668.7 23.5 %copy-start.49 = (f32[144,1152]{1,0:T(8,128)S(1)}, f32[144,1152]{1,0:T(8,128)}, u32[]{:S(2)}) copy-start(f32[144,1152]{1,0:T(8,128)} %param.49) | copy-start | bytes 1990660
  668.7 21.3 %all-to-all-start.8 = ((f32[32,1,2482]{2,1,0:T(1,128)}), f32[32,1,2482]{2,1,0:T(1,128)S(1)}, u32[]{:S(2)}, u32[]{:S(2)}) async-start(f32[32,1,2482]{2,1,0:T(1,128)} %broadcast_in_dim.192), calls=%async_computation.9 | async-start | bytes 655360 | tf_op jit(solution)/shard_map/all_to_all | solution.py:753
  (97 other events, 406.3 us)
Sparse Core Ops, SparseCore 0:
  11.5 148.4 all-gather.3
  163.5 102.4 all-gather.5
  376.7 159.9 reduce-scatter.1
